TPU v7x, 32 devices: a whole 2x2x4 slice. The times are simulated.
32 devices in a mesh: dp: 8 (over z, core), expert: 4 (over y, x).
Axes of the slice: x: 2, y: 2, z: 4, core: 2. Of those that a mesh axis runs over, the one named last changes fastest.
Arguments:
- tokens: bfloat16 [32768, 768], P(('dp', 'expert')), may hold values from -6 to 6
- segment_ids: int32 [32, 1024], P(('dp', 'expert')), may hold values from 0 to 3, never falling along the last dimension, each value on 1 to 512 neighbouring positions
- expert_order: int32 [32768], P(('dp', 'expert')), may hold values from 0 to 1023, as said below
- expert_counts: int32 [32, 8], P(('dp', 'expert')), may hold values from 0 to 256, as said below
- norm1_gain: float32 [768], replicated, may hold values from 0.5 to 1.5
- norm1_bias: float32 [768], replicated, may hold values from -0.5 to 0.5
- query_w: bfloat16 [768, 768], replicated, may hold values from -0.3125 to 0.3125
- key_w: bfloat16 [768, 768], replicated, may hold values from -0.3125 to 0.3125
- value_w: bfloat16 [768, 768], replicated, may hold values from -0.21875 to 0.21875
- out_w: bfloat16 [768, 768], replicated, may hold values from -0.625 to 0.625
- norm2_gain: float32 [768], replicated, may hold values from 0.5 to 1.5
- norm2_bias: float32 [768], replicated, may hold values from -0.5 to 0.5
- router_w: bfloat16 [768, 8], replicated, may hold values from -0.15625 to 0.15625
- expert_in: bfloat16 [8, 768, 3072], P('expert'), may hold values from -0.21875 to 0.21875
- expert_out: bfloat16 [8, 3072, 768], P('expert'), may hold values from -0.3125 to 0.3125
- cotangent: bfloat16 [32768, 768], P(('dp', 'expert')), may hold values from -8 to 8
Outputs:
- block_out: bfloat16 [32768, 768], P(('dp', 'expert'))
- tokens_grad: bfloat16 [32768, 768], P(('dp', 'expert'))
- norm1_gain_grad: float32 [768], replicated
- norm1_bias_grad: float32 [768], replicated
- query_grad: float32 [768, 768], replicated
- key_grad: float32 [768, 768], replicated
- value_grad: float32 [768, 768], replicated
- out_grad: float32 [768, 768], replicated
- norm2_gain_grad: float32 [768], replicated
- norm2_bias_grad: float32 [768], replicated
- expert_in_grad: float32 [8, 768, 3072], P('expert', 'dp')
- expert_out_grad: float32 [8, 3072, 768], P('expert', 'dp')
Inputs may be any that keep to these rules, and one draw needn't show every extreme that they name: `segment_ids`: each row holds 4 documents in order, each of 1 to 512 positions. `expert_order`: each block of 1024 entries (one device's tokens) holds every number 0 to 1023 once; its p-th entry is the token that stands p-th when that device's tokens are ordered by expert. `expert_counts`: row d counts device d's tokens for each expert and sums to 1024; no count exceeds 256, and one expert, the same in every row, has exactly 256 in every row.
All inputs are finite; a program needn't handle non-finite values.
Results may differ from a plain program's by a relative error of at most 0.015.
Values may be sent and summed in bfloat16 or wider, within the bound.
No kernel may reach another device: no remote copies, remote signals or barrier semaphores. Data moves between devices by JAX's collectives and lax.ppermute only.
A program may use at most 320 MiB of HBM per device.

v0:
```python
import jax
import jax.numpy as jnp
from jax import lax
from jax.sharding import PartitionSpec as P

HEADS = 12
HEAD_DIM = 64


EPSILON = 1e-05
NEG_LARGE = -1e30
ROOT_HALF = 0.7071067811865476
NORMAL_PEAK = 0.3989422804014327


def norm_parts(values):
    centered = values - jnp.mean(values, axis=-1, keepdims=True)
    inverse_std = lax.rsqrt(jnp.mean(centered * centered, axis=-1, keepdims=True) + EPSILON)
    return (centered * inverse_std, inverse_std)


def norm_back(grad_normed, normed, inverse_std, gain_vec):
    scaled = grad_normed * gain_vec
    return inverse_std * (
        scaled
        - jnp.mean(scaled, axis=-1, keepdims=True)
        - normed * jnp.mean(scaled * normed, axis=-1, keepdims=True)
    )


def gelu_slope(pre_act):
    return 0.5 * (1.0 + lax.erf(pre_act * ROOT_HALF)) + pre_act * NORMAL_PEAK * jnp.exp(
        -0.5 * pre_act * pre_act
    )


def route_maps(expert_order, counts_row, capacity):
    tok_count = expert_order.shape[0]
    experts = counts_row.shape[0]
    upper_end = jnp.cumsum(counts_row)
    lower_end = upper_end - counts_row
    slot_rank = lax.broadcasted_iota(jnp.int32, (experts, capacity), 1)
    positions = jnp.minimum(lower_end[:, None] + slot_rank, tok_count - 1).reshape(-1)
    source_rows = expert_order[positions]
    filled = (slot_rank < counts_row[:, None]).reshape(-1)
    inverse = (
        jnp.zeros((tok_count,), jnp.int32).at[expert_order].set(lax.iota(jnp.int32, tok_count))
    )
    expert_of = jnp.sum((upper_end[None, :] <= inverse[:, None]).astype(jnp.int32), axis=1)
    chosen = expert_of[:, None] == lax.iota(jnp.int32, experts)[None, :]
    first_slot = jnp.sum(jnp.where(chosen, lower_end[None, :], 0), axis=1)
    buffer_row = expert_of * capacity + inverse - first_slot
    return (source_rows, filled, buffer_row, chosen)


def pick_sequence(array, sequence):
    return lax.dynamic_index_in_dim(array, sequence, 0, keepdims=False)


def block_mask(segment_row, first_row, block_rows):
    length = segment_row.shape[0]
    query_segs = lax.dynamic_slice_in_dim(segment_row, first_row, block_rows, 0)
    query_place = first_row + lax.iota(jnp.int32, block_rows)
    key_place = lax.iota(jnp.int32, length)
    return (query_segs[:, None] == segment_row[None, :]) & (
        key_place[None, :] <= query_place[:, None]
    )


def attention_forward(queries, key_rows, value_rows, segment_ids):
    sequences, length = segment_ids.shape
    block_rows = min(512, length)
    block_count = length // block_rows
    score_scale = HEAD_DIM ** (-0.5)
    query_heads = queries.reshape(sequences, length, HEADS, HEAD_DIM)
    key_heads = key_rows.reshape(sequences, length, HEADS, HEAD_DIM)
    value_heads = value_rows.reshape(sequences, length, HEADS, HEAD_DIM)

    def one_block(position):
        sequence = position // block_count
        first_row = position % block_count * block_rows
        query_block = lax.dynamic_slice_in_dim(
            pick_sequence(query_heads, sequence), first_row, block_rows, 0
        )
        key_seq = pick_sequence(key_heads, sequence)
        value_seq = pick_sequence(value_heads, sequence)
        allowed = block_mask(pick_sequence(segment_ids, sequence), first_row, block_rows)
        scores = (
            jnp.einsum("qhd,khd->hqk", query_block, key_seq, preferred_element_type=jnp.float32)
            * score_scale
        )
        scores = jnp.where(allowed[None], scores, NEG_LARGE)
        row_max = jnp.max(scores, axis=-1, keepdims=True)
        weights = jnp.exp(scores - row_max)
        row_total = jnp.sum(weights, axis=-1, keepdims=True)
        attn_prob = (weights / row_total).astype(jnp.bfloat16)
        mixture = jnp.einsum(
            "hqk,khd->qhd", attn_prob, value_seq, preferred_element_type=jnp.float32
        )
        return (mixture.astype(jnp.bfloat16), (row_max + jnp.log(row_total))[..., 0])

    mixtures, log_totals = lax.map(one_block, lax.iota(jnp.int32, sequences * block_count))
    return (mixtures.reshape(sequences * length, HEADS * HEAD_DIM), log_totals)


def attention_backward(queries, key_rows, value_rows, segment_ids, log_totals, grad_mixture):
    sequences, length = segment_ids.shape
    block_rows = min(512, length)
    block_count = length // block_rows
    score_scale = HEAD_DIM ** (-0.5)
    query_heads = queries.reshape(sequences, length, HEADS, HEAD_DIM)
    key_heads = key_rows.reshape(sequences, length, HEADS, HEAD_DIM)
    value_heads = value_rows.reshape(sequences, length, HEADS, HEAD_DIM)
    grad_heads = grad_mixture.reshape(sequences, length, HEADS, HEAD_DIM)
    total_blocks = log_totals.reshape(sequences, block_count, HEADS, block_rows)

    def one_sequence(sequence):
        query_seq = pick_sequence(query_heads, sequence)
        key_seq = pick_sequence(key_heads, sequence)
        value_seq = pick_sequence(value_heads, sequence)
        grad_seq = pick_sequence(grad_heads, sequence)
        segment_row = pick_sequence(segment_ids, sequence)
        totals_seq = pick_sequence(total_blocks, sequence)

        def step(running, position):
            grad_keys, grad_values = running
            first_row = position * block_rows
            query_block = lax.dynamic_slice_in_dim(query_seq, first_row, block_rows, 0)
            grad_block = lax.dynamic_slice_in_dim(grad_seq, first_row, block_rows, 0)
            totals_block = pick_sequence(totals_seq, position)
            allowed = block_mask(segment_row, first_row, block_rows)
            scores = (
                jnp.einsum("qhd,khd->hqk", query_block, key_seq, preferred_element_type=jnp.float32)
                * score_scale
            )
            attn_prob = jnp.where(allowed[None], jnp.exp(scores - totals_block[..., None]), 0.0)
            grad_values = grad_values + jnp.einsum(
                "hqk,qhd->khd",
                attn_prob.astype(jnp.bfloat16),
                grad_block,
                preferred_element_type=jnp.float32,
            )
            grad_prob = jnp.einsum(
                "qhd,khd->hqk", grad_block, value_seq, preferred_element_type=jnp.float32
            )
            grad_scores = (
                attn_prob * (grad_prob - jnp.sum(attn_prob * grad_prob, axis=-1, keepdims=True))
            ).astype(jnp.bfloat16)
            grad_query = (
                jnp.einsum("hqk,khd->qhd", grad_scores, key_seq, preferred_element_type=jnp.float32)
                * score_scale
            ).astype(jnp.bfloat16)
            grad_keys = (
                grad_keys
                + jnp.einsum(
                    "hqk,qhd->khd", grad_scores, query_block, preferred_element_type=jnp.float32
                )
                * score_scale
            )
            return ((grad_keys, grad_values), grad_query)

        zeros_seq = jnp.zeros((length, HEADS, HEAD_DIM), jnp.float32)
        (grad_keys, grad_values), grad_query = lax.scan(
            step, (zeros_seq, zeros_seq), lax.iota(jnp.int32, block_count)
        )
        return (
            grad_query.reshape(length, HEADS, HEAD_DIM),
            grad_keys.astype(jnp.bfloat16),
            grad_values.astype(jnp.bfloat16),
        )

    grad_query, grad_keys, grad_values = lax.map(one_sequence, lax.iota(jnp.int32, sequences))
    model_width = HEADS * HEAD_DIM
    return (
        grad_query.reshape(-1, model_width),
        grad_keys.reshape(-1, model_width),
        grad_values.reshape(-1, model_width),
    )


def shards(
    tokens,
    segment_ids,
    expert_order,
    expert_counts,
    norm1_gain,
    norm1_bias,
    query_w,
    key_w,
    value_w,
    out_w,
    norm2_gain,
    norm2_bias,
    router_w,
    expert_in,
    expert_out,
    cotangent,
):
    groups = lax.axis_size("expert")
    local_experts = expert_in.shape[0]
    experts = expert_counts.shape[1]
    model_width = tokens.shape[1]
    capacity = 2 * tokens.shape[0] // experts
    slab_rows = groups * capacity
    no_value = jnp.zeros((), jnp.bfloat16)
    source_rows, filled, buffer_row, chosen = route_maps(expert_order, expert_counts[0], capacity)
    inputs = tokens.astype(jnp.float32)
    normed1, inverse1 = norm_parts(inputs)
    attn_in = (normed1 * norm1_gain + norm1_bias).astype(jnp.bfloat16)
    queries = jnp.dot(attn_in, query_w, preferred_element_type=jnp.float32).astype(jnp.bfloat16)
    key_rows = jnp.dot(attn_in, key_w, preferred_element_type=jnp.float32).astype(jnp.bfloat16)
    value_rows = jnp.dot(attn_in, value_w, preferred_element_type=jnp.float32).astype(jnp.bfloat16)
    mixture, log_totals = attention_forward(queries, key_rows, value_rows, segment_ids)
    resid = inputs + jnp.dot(mixture, out_w, preferred_element_type=jnp.float32)
    normed2, inverse2 = norm_parts(resid)
    hidden = (normed2 * norm2_gain + norm2_bias).astype(jnp.bfloat16)
    logits = jnp.dot(hidden, router_w, preferred_element_type=jnp.float32)
    gate_value = jax.nn.sigmoid(jnp.sum(jnp.where(chosen, logits, 0.0), axis=1))
    outgoing = jnp.where(filled[:, None], hidden[source_rows], no_value).reshape(
        groups, local_experts, capacity, model_width
    )
    arrived = lax.all_to_all(outgoing, "expert", split_axis=0, concat_axis=2, tiled=True).reshape(
        local_experts, slab_rows, model_width
    )
    pre_act = jnp.einsum("erd,edf->erf", arrived, expert_in, preferred_element_type=jnp.float32)
    activated = jax.nn.gelu(pre_act, approximate=False).astype(jnp.bfloat16)
    produced = jnp.einsum(
        "erf,efd->erd", activated, expert_out, preferred_element_type=jnp.float32
    ).astype(jnp.bfloat16)
    returned = lax.all_to_all(
        produced.reshape(1, local_experts, slab_rows, model_width),
        "expert",
        split_axis=2,
        concat_axis=0,
        tiled=True,
    )
    expert_rows = returned.reshape(experts * capacity, model_width)[buffer_row].astype(jnp.float32)
    block_out = (resid + gate_value[:, None] * expert_rows).astype(jnp.bfloat16)
    grad_out = cotangent.astype(jnp.float32)
    grad_rows = (gate_value[:, None] * grad_out).astype(jnp.bfloat16)
    grad_logit = jnp.sum(grad_out * expert_rows, axis=1) * gate_value * (1.0 - gate_value)
    router_rows = jnp.einsum(
        "te,de->td", chosen.astype(jnp.bfloat16), router_w, preferred_element_type=jnp.float32
    )
    outgoing_grad = jnp.where(filled[:, None], grad_rows[source_rows], no_value).reshape(
        groups, local_experts, capacity, model_width
    )
    arrived_grad = lax.all_to_all(
        outgoing_grad, "expert", split_axis=0, concat_axis=2, tiled=True
    ).reshape(local_experts, slab_rows, model_width)
    units, arrived_grad = lax.optimization_barrier((arrived, arrived_grad))
    pre_again = jnp.einsum("erd,edf->erf", units, expert_in, preferred_element_type=jnp.float32)
    act_again = jax.nn.gelu(pre_again, approximate=False).astype(jnp.bfloat16)
    grad_act = jnp.einsum(
        "erd,efd->erf", arrived_grad, expert_out, preferred_element_type=jnp.float32
    )
    grad_pre = (grad_act * gelu_slope(pre_again)).astype(jnp.bfloat16)
    grad_first = jnp.einsum("erd,erf->edf", units, grad_pre, preferred_element_type=jnp.float32)
    grad_second = jnp.einsum(
        "erf,erd->efd", act_again, arrived_grad, preferred_element_type=jnp.float32
    )
    grad_units = jnp.einsum(
        "erf,edf->erd", grad_pre, expert_in, preferred_element_type=jnp.float32
    ).astype(jnp.bfloat16)
    first_share, second_share = (
        lax.psum_scatter(
            grad_first.astype(jnp.bfloat16), "dp", scatter_dimension=1, tiled=True
        ).astype(jnp.float32),
        lax.psum_scatter(
            grad_second.astype(jnp.bfloat16), "dp", scatter_dimension=1, tiled=True
        ).astype(jnp.float32),
    )
    grad_back = lax.all_to_all(
        grad_units.reshape(1, local_experts, slab_rows, model_width),
        "expert",
        split_axis=2,
        concat_axis=0,
        tiled=True,
    )
    grad_hidden = (
        grad_back.reshape(experts * capacity, model_width)[buffer_row].astype(jnp.float32)
        + grad_logit[:, None] * router_rows
    )
    grad_gain2 = jnp.sum(grad_hidden * normed2, axis=0)
    grad_bias2 = jnp.sum(grad_hidden, axis=0)
    grad_resid = grad_out + norm_back(grad_hidden, normed2, inverse2, norm2_gain)
    grad_attn = grad_resid.astype(jnp.bfloat16)
    grad_outw = jnp.einsum("td,te->de", mixture, grad_attn, preferred_element_type=jnp.float32)
    grad_mixture = jnp.einsum(
        "te,de->td", grad_attn, out_w, preferred_element_type=jnp.float32
    ).astype(jnp.bfloat16)
    grad_query, grad_keys, grad_values = attention_backward(
        queries, key_rows, value_rows, segment_ids, log_totals, grad_mixture
    )
    grad_qw = jnp.einsum("td,te->de", attn_in, grad_query, preferred_element_type=jnp.float32)
    grad_kw = jnp.einsum("td,te->de", attn_in, grad_keys, preferred_element_type=jnp.float32)
    grad_vw = jnp.einsum("td,te->de", attn_in, grad_values, preferred_element_type=jnp.float32)
    grad_in = jnp.einsum("te,de->td", grad_query, query_w, preferred_element_type=jnp.float32)
    grad_in = grad_in + jnp.einsum(
        "te,de->td", grad_keys, key_w, preferred_element_type=jnp.float32
    )
    grad_in = grad_in + jnp.einsum(
        "te,de->td", grad_values, value_w, preferred_element_type=jnp.float32
    )
    grad_gain1 = jnp.sum(grad_in * normed1, axis=0)
    grad_bias1 = jnp.sum(grad_in, axis=0)
    grad_tokens = grad_resid + norm_back(grad_in, normed1, inverse1, norm1_gain)
    summed = lax.psum(
        (grad_gain1, grad_bias1, grad_qw, grad_kw, grad_vw, grad_outw, grad_gain2, grad_bias2),
        ("dp", "expert"),
    )
    return (
        block_out,
        grad_tokens.astype(jnp.bfloat16),
        summed[0],
        summed[1],
        summed[2],
        summed[3],
        summed[4],
        summed[5],
        summed[6],
        summed[7],
        first_share,
        second_share,
    )


def solution(mesh):
    placed = (
        P(("dp", "expert"), None),
        P(("dp", "expert"), None),
        P(("dp", "expert")),
        P(("dp", "expert"), None),
        P(),
        P(),
        P(),
        P(),
        P(),
        P(),
        P(),
        P(),
        P(),
        P("expert", None, None),
        P("expert", None, None),
        P(("dp", "expert"), None),
    )
    return jax.shard_map(
        shards,
        mesh=mesh,
        in_specs=placed,
        out_specs=(
            P(("dp", "expert"), None),
            P(("dp", "expert"), None),
            P(),
            P(),
            P(),
            P(),
            P(),
            P(),
            P(),
            P(),
            P("expert", "dp", None),
            P("expert", "dp", None),
        ),
        check_vma=False,
    )
```

profile of v0, /device:TPU:0, one launch (start us, length us, event | category | flops | bytes accessed | tf_op | source)
XLA Modules:
  0.0 997.8 jit_solution(4456566644337120160)
XLA Ops:
  11.7 3.1 convolution_convert_fusion.3
  14.9 2.8 convolution_convert_fusion.2
  17.7 2.8 convolution_convert_fusion.4
  21.8 78.4 %while.40 = (s32[]{:T(128)}, bf16[2,512,12,64]{1,3,2,0:T(8,128)(2,1)}, f32[2,12,512]{2,1,0:T(8,128)S(1)}, s32[2]{0:T(128)S(1)}, s32[1,1024]{1,0:T(1,128)S(1)}, /...) while((s32[]{:T(128)}, ...), condition=%wide.region_5.6_spmd, body=%wide.region_2.0_spmd.sunk | while | flops 1688070656 | bytes 189504368 | solution.py:102
  25.2 12.1 %fusion.245 = (f32[12,512]{1,0:T(8,128)S(1)}, f32[12,512,1024]{2,1,0:T(8,128)}) fusion(pred[512,1024]{1,0:T(8,128)(4,1)S(1)} %fusion.244, bf16[1,1024,12,64]{1,3,2,0:T(8,128)(2,1)S(1)} %get-tuple-element.541, bf16[1,1024,12,64]{1,3,2,0:T(8,128)(2,1)} %get-tuple-element.540, s32[]{:T(128)S(6)} %select_n.162), kind=kOutput, calls=%fused_computation.9.clone.1 | convolution fusion | flops 824174592 | bytes 28073988 | tf_op jit(solution)/shard_map/while/body/eval_jaxpr/qhd,khd->hqk/dot_general | solution.py:89
  37.2 12.3 %fusion.246 = f32[12,512]{1,0:T(8,128)S(1)} fusion(f32[12,512,1024]{2,1,0:T(8,128)} %get-tuple-element.494, f32[12,512]{1,0:T(8,128)S(1)} %get-tuple-element.495, pred[512,1024]{1,0:T(8,128)(4,1)S(1)} %fusion.244), kind=kLoop, calls=%fused_computation.10.clone.1 | loop fusion | flops 25159680 | bytes 25739264 | tf_op jit(solution)/shard_map/while/body/eval_jaxpr/reduce_sum | solution.py:95
  49.6 3.0 copy-done.3
  52.6 8.5 fusion.247
  64.3 12.1 %fusion.245 = (f32[12,512]{1,0:T(8,128)S(1)}, f32[12,512,1024]{2,1,0:T(8,128)}) fusion(pred[512,1024]{1,0:T(8,128)(4,1)S(1)} %fusion.244, bf16[1,1024,12,64]{1,3,2,0:T(8,128)(2,1)S(1)} %get-tuple-element.541, bf16[1,1024,12,64]{1,3,2,0:T(8,128)(2,1)} %get-tuple-element.540, s32[]{:T(128)S(6)} %select_n.162), kind=kOutput, calls=%fused_computation.9.clone.1 | convolution fusion | flops 824174592 | bytes 28073988 | tf_op jit(solution)/shard_map/while/body/eval_jaxpr/qhd,khd->hqk/dot_general | solution.py:89
  76.4 12.3 %fusion.246 = f32[12,512]{1,0:T(8,128)S(1)} fusion(f32[12,512,1024]{2,1,0:T(8,128)} %get-tuple-element.494, f32[12,512]{1,0:T(8,128)S(1)} %get-tuple-element.495, pred[512,1024]{1,0:T(8,128)(4,1)S(1)} %fusion.244), kind=kLoop, calls=%fused_computation.10.clone.1 | loop fusion | flops 25159680 | bytes 25739264 | tf_op jit(solution)/shard_map/while/body/eval_jaxpr/reduce_sum | solution.py:95
  88.7 3.0 copy-done.3
  91.7 8.5 fusion.247
  100.3 3.7 copy.112
  111.9 8.6 gather_fusion
  122.4 9.4 gather_fusion.1
  134.3 41.6 %all_to_all.60 = bf16[4,2,256,768]{3,2,1,0:T(8,128)(2,1)S(1)} all-to-all(bf16[4,2,256,768]{3,2,1,0:T(8,128)(2,1)S(1)} %broadcast_select_fusion.1), channel_id=1, replica_groups=mesh['dp'=8,'expert'=4] {'expert'}, dimensions={0} | all-to-all | bytes 6291456 | tf_op jit(solution)/shard_map/all_to_all | solution.py:222
  177.9 25.0 %fusion.74 = (u8[1024,3072]{1,0:T(8,128)(4,1)}, u8[1024,3072]{1,0:T(8,128)(4,1)}, f32[2,1024,3072]{2,1,0:T(8,128)}) fusion(bf16[2,1024,768]{2,1,0:T(8,128)(2,1)} %bitcast.194, bf16[2,768,3072]{2,1,0:T(8,128)(2,1)} %param.33), kind=kOutput, calls=%fused_computation.110 | convolution fusion | flops 9739173888 | bytes 44040192 | tf_op jit(solution)/shard_map/erd,edf->erf/dot_general | solution.py:225
  202.8 69.0 %convert_bitcast_fusion.1 = bf16[1,2,1024,768]{3,2,1,0:T(8,128)(2,1)S(1)} fusion(bf16[2,3072,768]{2,1,0:T(8,128)(2,1)} %param.34, f32[2,1024,3072]{2,1,0:T(8,128)} %get-tuple-element.379, u8[1024,3072]{1,0:T(8,128)(4,1)} %get-tuple-element.312, u8[1024,3072]{1,0:T(8,128)(4,1)} %get-tuple-element.311), kind=kOutput, calls=%fused_computation.147 | convolution fusion | flops 10105651200 | bytes 44040192 | tf_op jit(solution)/shard_map/erf,efd->erd/dot_general | solution.py:227
  271.8 4.9 copy.115
  276.7 4.7 all-to-all-start.1
  284.2 4.3 scatter_custom_fusion
  289.7 26.7 %all-to-all-done.1 = bf16[1,2,1024,768]{3,1,0,2:T(2,128)(2,1)} async-done(((bf16[1,2,1024,768]{3,1,0,2:T(2,128)(2,1)}), bf16[1,2,1024,768]{3,1,0,2:T(2,128)(2,1)}, u32[]{:S(2)}, u32[]{:S(2)}) %all-to-all-start.1) | async-done | bytes 3145760 | tf_op jit(solution)/shard_map/all_to_all | solution.py:230
  316.4 4.0 copy.116
  320.4 7.9 gather_fusion.2
  330.9 3.8 fusion.94
  336.5 9.4 gather_fusion.3
  348.0 38.6 %all_to_all.61 = bf16[4,2,256,768]{3,2,1,0:T(8,128)(2,1)S(1)} all-to-all(bf16[4,2,256,768]{3,2,1,0:T(8,128)(2,1)S(1)} %broadcast_select_fusion), channel_id=1, replica_groups=mesh['dp'=8,'expert'=4] {'expert'}, dimensions={0} | all-to-all | bytes 6291456 | tf_op jit(solution)/shard_map/all_to_all | solution.py:248
  388.6 25.0 %fusion.75 = (u8[1024,3072]{1,0:T(8,128)(4,1)}, u8[1024,3072]{1,0:T(8,128)(4,1)}, f32[2,1024,3072]{2,1,0:T(8,128)}) fusion(bf16[2,1024,768]{2,1,0:T(8,128)(2,1)} %bitcast.195, bf16[2,768,3072]{2,1,0:T(8,128)(2,1)} %param.33), kind=kOutput, calls=%fused_computation.111 | convolution fusion | flops 9739173888 | bytes 44040192 | tf_op jit(solution)/shard_map/erd,edf->erf/dot_general | solution.py:252
  413.6 70.0 %fusion.69 = bf16[2,3072,768]{2,1,0:T(8,128)(2,1)} fusion(bf16[2,1024,768]{2,1,0:T(8,128)(2,1)} %bitcast.197, f32[2,1024,3072]{2,1,0:T(8,128)} %get-tuple-element.382, u8[1024,3072]{1,0:T(8,128)(4,1)} %get-tuple-element.310, u8[1024,3072]{1,0:T(8,128)(4,1)} %get-tuple-element.309), kind=kOutput, calls=%fused_computation.107 | convolution fusion | flops 10108796928 | bytes 44040192 | tf_op jit(solution)/shard_map/erf,erd->efd/dot_general | solution.py:259
  483.6 23.5 %fusion.49 = bf16[2,1024,3072]{2,1,0:T(8,128)(2,1)} fusion(f32[2,1024,3072]{2,1,0:T(8,128)} %get-tuple-element.382, bf16[2,1024,768]{2,1,0:T(8,128)(2,1)} %bitcast.198, bf16[2,3072,768]{2,1,0:T(8,128)(2,1)} %param.34), kind=kOutput, calls=%fused_computation.65 | convolution fusion | flops 9726590976 | bytes 50331648 | tf_op jit(solution)/shard_map/erd,efd->erf/dot_general | solution.py:254
  507.1 16.0 %convert_bitcast_fusion = bf16[1,2,1024,768]{3,2,1,0:T(8,128)(2,1)S(1)} fusion(bf16[2,1024,3072]{2,1,0:T(8,128)(2,1)} %fusion.49, bf16[2,768,3072]{2,1,0:T(8,128)(2,1)} %param.33), kind=kOutput, calls=%fused_computation.146 | convolution fusion | flops 9665249280 | bytes 25165824 | tf_op jit(solution)/shard_map/erf,edf->erd/dot_general | solution.py:262
  523.1 5.0 copy.121
  528.1 4.8 all-to-all-start.3
  533.0 18.1 %convolution_convert_fusion = bf16[2,768,3072]{2,1,0:T(8,128)(2,1)} fusion(bf16[2,1024,768]{2,1,0:T(8,128)(2,1)} %bitcast.196, bf16[2,1024,3072]{2,1,0:T(8,128)(2,1)} %fusion.49), kind=kOutput, calls=%fused_computation.106 | convolution fusion | flops 9668395008 | bytes 25165824 | tf_op jit(solution)/shard_map/erd,erf->edf/dot_general | solution.py:258
  551.1 17.4 %all-to-all-done.3 = bf16[1,2,1024,768]{3,1,0,2:T(2,128)(2,1)} async-done(((bf16[1,2,1024,768]{3,1,0,2:T(2,128)(2,1)}), bf16[1,2,1024,768]{3,1,0,2:T(2,128)(2,1)}, u32[]{:S(2)}, u32[]{:S(2)}) %all-to-all-start.3) | async-done | bytes 3145760 | tf_op jit(solution)/shard_map/all_to_all | solution.py:273
  568.5 4.0 copy.122
  572.5 6.9 gather_fusion.4
  581.2 4.8 multiply_reduce_fusion.1
  586.0 2.7 convert_add_fusion
  592.7 175.1 %while.41 = (s32[]{:T(128)}, f32[1024,12,64]{0,2,1:T(8,128)}, f32[1024,12,64]{0,2,1:T(8,128)}, bf16[2,512,12,64]{1,3,2,0:T(8,128)(2,1)}, s32[2]{0:T(128)S(1)}, /...) while((s32[]{:T(128)}, f32[1024,12,64]{0,2,1:T(8,128)}, ...), condition=%wide.region_18.19_spmd.clone, body=%wide.region_16.18_spmd.clone.sunk | while | flops 4127189504 | bytes 212261664 | solution.py:163
  594.8 11.5 %fusion.257 = f32[12,512,1024]{2,1,0:T(8,128)} fusion(bf16[1024,12,64]{0,2,1:T(8,128)(2,1)S(1)} %get-tuple-element.587, bf16[1024,12,64]{0,2,1:T(8,128)(2,1)} %get-tuple-element.585, s32[]{:T(128)S(6)} %select_n.166), kind=kOutput, calls=%fused_computation.45.clone.1 | convolution fusion | flops 805306368 | bytes 27525124 | tf_op jit(solution)/shard_map/while/body/eval_jaxpr/while/body/eval_jaxpr/qhd,khd->hqk/dot_general | solution.py:133
  608.2 18.3 %multiply_reduce_fusion.7 = (f32[12,512]{1,0:T(8,128)S(1)}, f32[12,512,1024]{2,1,0:T(8,128)}) fusion(f32[12,512,1024]{2,1,0:T(8,128)} %fusion.257, f32[12,512]{1,0:T(8,128)S(1)} %dynamic-slice_bitcast_fusion.2, pred[512,1024]{1,0:T(8,128)(4,1)S(1)} %fusion.258, bf16[1024,12,64]{0,2,1:T(8,128)(2,1)} %get-tuple-element.590, ...), kind=kOutput, calls=%fused_computation.29.clone.1 | convolution fusion | flops 836757504 | bytes 53264388 | tf_op jit(solution)/shard_map/while/body/eval_jaxpr/while/body/eval_jaxpr/qhd,khd->hqk/dot_general | solution.py:143
  626.5 21.7 %multiply_convert_fusion.3 = bf16[12,512,1024]{2,1,0:T(8,128)(2,1)} fusion(f32[12,512,1024]{2,1,0:T(8,128)} %get-tuple-element.507, f32[12,512,1024]{2,1,0:T(8,128)} %fusion.257, f32[12,512]{1,0:T(8,128)S(1)} %get-tuple-element.508, f32[12,512]{1,0:T(8,128)S(1)} %dynamic-slice_bitcast_fusion.2, pred[512,1024]{1,0:T(8,128)(4,1)S(1)} %fusion.258), kind=kLoop, calls=%fused_computation.28.clone.1 | loop fusion | flops 37748736 | bytes 63488000 | tf_op jit(solution)/shard_map/while/body/eval_jaxpr/while/body/eval_jaxpr/convert_element_type | solution.py:148
  648.2 9.0 bitcast_add_fusion.4
  657.2 9.6 fusion.259
  666.7 13.2 %bitcast_add_fusion.5 = f32[1024,12,64]{0,2,1:T(8,128)} fusion(f32[1024,12,64]{0,2,1:T(8,128)} %get-tuple-element.566, f32[12,512,1024]{2,1,0:T(8,128)} %fusion.257, f32[12,512]{1,0:T(8,128)S(1)} %dynamic-slice_bitcast_fusion.2, pred[512,1024]{1,0:T(8,128)(4,1)S(1)} %fusion.258, pred[]{:T(512)S(6)} %compare.6, ...), kind=kOutput, calls=%fused_computation.34.clone.1 | convolution fusion | flops 832045056 | bytes 32792580 | tf_op jit(solution)/shard_map/while/body/eval_jaxpr/while/body/eval_jaxpr/hqk,qhd->khd/dot_general | solution.py:137
  681.9 11.3 %fusion.257 = f32[12,512,1024]{2,1,0:T(8,128)} fusion(bf16[1024,12,64]{0,2,1:T(8,128)(2,1)S(1)} %get-tuple-element.587, bf16[1024,12,64]{0,2,1:T(8,128)(2,1)} %get-tuple-element.585, s32[]{:T(128)S(6)} %select_n.166), kind=kOutput, calls=%fused_computation.45.clone.1 | convolution fusion | flops 805306368 | bytes 27525124 | tf_op jit(solution)/shard_map/while/body/eval_jaxpr/while/body/eval_jaxpr/qhd,khd->hqk/dot_general | solution.py:133
  695.1 18.2 %multiply_reduce_fusion.7 = (f32[12,512]{1,0:T(8,128)S(1)}, f32[12,512,1024]{2,1,0:T(8,128)}) fusion(f32[12,512,1024]{2,1,0:T(8,128)} %fusion.257, f32[12,512]{1,0:T(8,128)S(1)} %dynamic-slice_bitcast_fusion.2, pred[512,1024]{1,0:T(8,128)(4,1)S(1)} %fusion.258, bf16[1024,12,64]{0,2,1:T(8,128)(2,1)} %get-tuple-element.590, ...), kind=kOutput, calls=%fused_computation.29.clone.1 | convolution fusion | flops 836757504 | bytes 53264388 | tf_op jit(solution)/shard_map/while/body/eval_jaxpr/while/body/eval_jaxpr/qhd,khd->hqk/dot_general | solution.py:143
  713.3 21.2 %multiply_convert_fusion.3 = bf16[12,512,1024]{2,1,0:T(8,128)(2,1)} fusion(f32[12,512,1024]{2,1,0:T(8,128)} %get-tuple-element.507, f32[12,512,1024]{2,1,0:T(8,128)} %fusion.257, f32[12,512]{1,0:T(8,128)S(1)} %get-tuple-element.508, f32[12,512]{1,0:T(8,128)S(1)} %dynamic-slice_bitcast_fusion.2, pred[512,1024]{1,0:T(8,128)(4,1)S(1)} %fusion.258), kind=kLoop, calls=%fused_computation.28.clone.1 | loop fusion | flops 37748736 | bytes 63488000 | tf_op jit(solution)/shard_map/while/body/eval_jaxpr/while/body/eval_jaxpr/convert_element_type | solution.py:148
  734.5 9.7 bitcast_add_fusion.4
  744.3 9.4 fusion.259
  753.6 14.0 %bitcast_add_fusion.5 = f32[1024,12,64]{0,2,1:T(8,128)} fusion(f32[1024,12,64]{0,2,1:T(8,128)} %get-tuple-element.566, f32[12,512,1024]{2,1,0:T(8,128)} %fusion.257, f32[12,512]{1,0:T(8,128)S(1)} %dynamic-slice_bitcast_fusion.2, pred[512,1024]{1,0:T(8,128)(4,1)S(1)} %fusion.258, pred[]{:T(512)S(6)} %compare.6, ...), kind=kOutput, calls=%fused_computation.34.clone.1 | convolution fusion | flops 832045056 | bytes 32792580 | tf_op jit(solution)/shard_map/while/body/eval_jaxpr/while/body/eval_jaxpr/hqk,qhd->khd/dot_general | solution.py:137
  767.8 3.2 copy.125
  771.7 2.7 copy-done.6
  775.9 2.8 fusion.102
  778.7 3.0 fusion.176
  781.8 3.0 fusion.172
  784.8 3.0 fusion.174
  787.9 3.3 fusion.182
  801.9 42.1 %all-reduce = (f32[768]{0:T(1024)}, f32[768]{0:T(1024)}, f32[768]{0:T(1024)}, f32[768]{0:T(1024)}) all-reduce(f32[768]{0:T(1024)S(1)} %get-tuple-element.315, f32[768]{0:T(1024)S(1)} %get-tuple-element.320, f32[768]{0:T(1024)S(1)} %copy-done.65, f32[768]{0:T(1024)S(1)} %copy-done.66), channel_id=1, replica_groups=mesh['dp'=8,'expert'=4] {'dp','expert'}, use_global_device_ids=true, to_apply=%region_22.23 | all-reduce | flops 3072 | bytes 24576 | tf_op jit(solution)/shard_map/psum | solution.py:308
  843.9 2.8 convert_element_type.133
  846.8 2.9 convert_element_type.130
  849.7 130.4 %all-reduce.4.cloned.1.call-done = (f32[768,768]{1,0:T(8,128)}, f32[768,768]{1,0:T(8,128)}, f32[768,768]{1,0:T(8,128)}, f32[768,768]{1,0:T(8,128)}) async-done(((f32[768,768]{1,0:T(8,128)}, f32[768,768]{1,0:T(8,128)}, f32[768,768]{1,0:T(8,128)}, f32[768,768]{1,0:T(8,128)}), (f32[768,768]{1,0:T(8,128)}, f32[768,768]{1,0:T(8,128)}, f32[768,768]{1,0:T(8,128)}, ...) | async-done | bytes 9437200 | tf_op jit(solution)/shard_map/psum | solution.py:308
  980.1 3.4 copy.170
  (247 shorter events, 61.2 us)
Async XLA Ops:
  8.0 6.9 copy-start
  8.0 3.0 copy-start.63
  8.0 3.0 copy-start.76
  10.2 7.5 copy-start.43
  11.7 6.0 copy-start.56
  11.7 3.2 copy-start.11
  14.9 2.8 copy-start.73
  17.7 4.1 copy-start.33
  25.2 24.4 %copy-start.7 = (bf16[1,1024,12,64]{1,3,2,0:T(8,128)(2,1)S(1)}, bf16[1,1024,12,64]{1,3,2,0:T(8,128)(2,1)}, u32[]{:S(2)}) copy-start(bf16[1,1024,12,64]{1,3,2,0:T(8,128)(2,1)} %get-tuple-element.542) | copy-start | bytes 4718596 | tf_op jit(solution)/shard_map/while
  37.2 15.4 %copy-start.3 = (f32[12,512,1024]{2,1,0:T(8,128)S(1)}, f32[12,512,1024]{2,1,0:T(8,128)}, u32[]{:S(2)}) copy-start(f32[12,512,1024]{2,1,0:T(8,128)} %get-tuple-element.494) | copy-start | bytes 75497472 | tf_op jit(solution)/shard_map/while
  64.3 24.4 %copy-start.7 = (bf16[1,1024,12,64]{1,3,2,0:T(8,128)(2,1)S(1)}, bf16[1,1024,12,64]{1,3,2,0:T(8,128)(2,1)}, u32[]{:S(2)}) copy-start(bf16[1,1024,12,64]{1,3,2,0:T(8,128)(2,1)} %get-tuple-element.542) | copy-start | bytes 4718596 | tf_op jit(solution)/shard_map/while
  76.4 15.4 %copy-start.3 = (f32[12,512,1024]{2,1,0:T(8,128)S(1)}, f32[12,512,1024]{2,1,0:T(8,128)}, u32[]{:S(2)}) copy-start(f32[12,512,1024]{2,1,0:T(8,128)} %get-tuple-element.494) | copy-start | bytes 75497472 | tf_op jit(solution)/shard_map/while
  100.2 4.1 copy-start.4
  100.2 4.1 copy-start.35
  100.2 4.1 copy-start.12
  100.2 4.1 copy-start.71
  108.2 3.4 copy-start.70
  108.2 3.7 copy-start.1
  111.8 9.3 copy-start.67
  120.5 11.3 %copy-start.37 = (s32[2048]{0:T(1024)}, s32[2048]{0:T(1024)S(1)}, u32[]{:S(2)}) copy-start(s32[2048]{0:T(1024)S(1)} %broadcast_clamp_fusion.1) | copy-start | bytes 24580
  122.4 9.5 copy-start.47
  276.7 39.6 %all-to-all-start.1 = ((bf16[1,2,1024,768]{3,1,0,2:T(2,128)(2,1)}), bf16[1,2,1024,768]{3,1,0,2:T(2,128)(2,1)}, u32[]{:S(2)}, u32[]{:S(2)}) async-start(bf16[1,2,1024,768]{3,1,0,2:T(2,128)(2,1)} %copy.115), calls=%async_computation.1 | async-start | bytes 6291456 | tf_op jit(solution)/shard_map/all_to_all | solution.py:230
  281.4 2.8 copy-start.2
  281.4 7.1 copy-start.68
  281.4 7.2 copy-start.69
  281.4 7.3 copy-start.14
  281.5 7.3 copy-start.60
  281.5 562.5 %reduce-scatter.5.cloned.1.call-start = ((), (), s32[]{:S(2)}) async-start(), calls=%async_computation.7 | async-start | bytes 10616832 | tf_op jit(solution)/shard_map/reduce_scatter | solution.py:269
  289.7 41.2 %copy-start.51 = (f32[1024]{0:T(1024)}, f32[1024]{0:T(1024)S(1)}, u32[]{:S(2)}) copy-start(f32[1024]{0:T(1024)S(1)} %add_divide_fusion) | copy-start | bytes 12292
  289.7 30.6 %copy-start.53 = (s32[1024]{0:T(1024)}, s32[1024]{0:T(1024)S(1)}, u32[]{:S(2)}) copy-start(s32[1024]{0:T(1024)S(1)} %fusion.106) | copy-start | bytes 12292
  330.9 5.5 copy-start.38
  336.5 9.5 copy-start.48
  528.1 4.9 copy-start.46
  528.1 4.9 copy-start.55
  528.1 40.5 %all-to-all-start.3 = ((bf16[1,2,1024,768]{3,1,0,2:T(2,128)(2,1)}), bf16[1,2,1024,768]{3,1,0,2:T(2,128)(2,1)}, u32[]{:S(2)}, u32[]{:S(2)}) async-start(bf16[1,2,1024,768]{3,1,0,2:T(2,128)(2,1)} %copy.121), calls=%async_computation.3 | async-start | bytes 6291456 | tf_op jit(solution)/shard_map/all_to_all | solution.py:273
  532.9 313.9 %reduce-scatter.3.cloned.1.call-start = ((), (), s32[]{:S(2)}) async-start(), calls=%async_computation.6 | async-start | bytes 10616832 | tf_op jit(solution)/shard_map/reduce_scatter | solution.py:266
  551.1 429.0 %all-reduce.4.cloned.1.call-start = ((), (), s32[]{:S(2)}) async-start(), calls=%async_computation.8 | async-start | bytes 18874368 | tf_op jit(solution)/shard_map/psum | solution.py:308
  568.5 4.0 copy-start.54
  581.1 4.9 copy-start.9
  581.1 4.9 copy-start.16
  581.1 4.8 copy-start.17
  581.2 4.8 copy-start.52
  586.0 2.8 copy-start.72
  588.8 3.9 copy-start.5
  588.8 3.9 copy-start.34
  588.8 3.9 copy-start.36
  767.8 3.6 copy-start.22
  771.4 7.3 copy-start.28
  771.4 3.0 copy-start.6
  771.7 10.1 %copy-start.29 = (bf16[1024,12,64]{0,2,1:T(8,128)(2,1)}, bf16[1024,12,64]{0,2,1:T(8,128)(2,1)S(1)}, u32[]{:S(2)}) copy-start(bf16[1024,12,64]{0,2,1:T(8,128)(2,1)S(1)} %convert_element_type.127) | copy-start | bytes 4718596
  771.7 3.7 copy-start.19
  771.7 4.1 copy-start.27
  775.8 9.0 copy-start.31
  775.8 2.9 copy-start.13
  775.8 2.9 copy-start.44
  775.8 2.9 copy-start.57
  775.8 2.9 copy-start.64
  775.9 2.9 copy-start.77
  787.8 3.3 copy-start.32
  787.9 3.3 copy-start.75
  797.6 2.7 copy-start.21
  797.6 4.3 copy-start.65
  797.6 4.3 copy-start.66
  980.1 3.4 copy-start.25
  (21 other events, 37.0 us)
Sparse Core Ops, SparseCore 0:
  483.7 99.1 reduce-scatter.4
  585.2 97.8 reduce-scatter.2
Sparse Core Ops, SparseCore 1:
  787.9 192.1 all-reduce.3
where the time goes:
time: 1000 us; the launch traced here: 998 us
  matrix products  449 us (45%)
  waiting for transfers between devices  174 us (17%)
  local copies, waits for them, and re-layouts  122 us (12%)
  blocking collectives  122 us (12%)
  other arithmetic  94.3 us (9%)
  between operations  16.9 us (2%)
    psum x1, waiting for transfers between devices, shards(): lax.psum((grad_gain1, grad_bias1, grad_qw, grad_kw, grad_vw, grad_outw, g...  130 us
    dot_general x1, matrix products, shards(): jnp.einsum('erf,erd->efd', act_again, arrived_grad, preferred_element_typ...  70 us
    dot_general x1, matrix products, shards(): jnp.einsum('erf,efd->erd', activated, expert_out, preferred_element_type=...  69 us
    convert_element_type x2, other arithmetic, step(): grad_scores = (attn_prob * (grad_prob - jnp.sum(attn_prob * grad_prob, ax...  42.9 us
    psum x1, blocking collectives, shards(): lax.psum((grad_gain1, grad_bias1, grad_qw, grad_kw, grad_vw, grad_outw, g...  42.1 us
    all_to_all x1, blocking collectives, shards(): lax.all_to_all(outgoing, 'expert', split_axis=0, concat_axis=2, tiled=True)  41.6 us
    all_to_all x1, blocking collectives, shards(): lax.all_to_all(outgoing_grad, 'expert', split_axis=0, concat_axis=2, tile...  38.6 us
    dot_general x2, matrix products, step(): jnp.einsum('qhd,khd->hqk', grad_block, value_seq, preferred_element_type=...  36.5 us
  transfers between devices with their start and end apart: 5, of which 3 were waited for; matrix products, arithmetic and copies ran while one was open for 30% of the time, Pallas kernels for 0%

commit v1 on v0

v1 whole, which is shorter than its diff:
```python
import functools
import math

import jax
import jax.numpy as jnp
from jax import lax
from jax.experimental import pallas as pl
from jax.experimental.pallas import tpu as pltpu
from jax.sharding import PartitionSpec as P

HEADS = 12
HEAD_DIM = 64
QUERY_ROWS = 256
WINDOW = 768
LANES = 256
EPSILON = 1e-05
NEG_LARGE = -1e30
ROOT_HALF = 0.7071067811865476
NORMAL_PEAK = 0.3989422804014327

f32 = jnp.float32
bf16 = jnp.bfloat16


def dot(left, right):
    return lax.dot_general(left, right, (((1,), (0,)), ((), ())), preferred_element_type=f32)


def dot_nt(left, right):
    return lax.dot_general(left, right, (((1,), (1,)), ((), ())), preferred_element_type=f32)


def dot_tn(left, right):
    return lax.dot_general(left, right, (((0,), (0,)), ((), ())), preferred_element_type=f32)


def full_spec(shape, buffers=2):
    zeros = (0,) * len(shape)
    return pl.BlockSpec(shape, lambda *_: zeros, pipeline_mode=pl.Buffered(buffers))


def smem():
    return pl.BlockSpec(memory_space=pltpu.SMEM)


def cost(flops, nbytes, trans=0):
    return pl.CostEstimate(flops=1, bytes_accessed=1, transcendentals=0)


def shape_of(shape, dtype):
    return jax.ShapeDtypeStruct(shape, dtype)


def column(row):
    return jnp.broadcast_to(row.astype(f32), (128, row.shape[1])).T[:, :1]


def norm_parts(values):
    centered = values - jnp.mean(values, axis=-1, keepdims=True)
    inverse_std = lax.rsqrt(jnp.mean(centered * centered, axis=-1, keepdims=True) + EPSILON)
    return centered * inverse_std, inverse_std


def norm_back(grad_normed, normed, inverse_std, gain_vec):
    scaled = grad_normed * gain_vec
    return inverse_std * (
        scaled
        - jnp.mean(scaled, axis=-1, keepdims=True)
        - normed * jnp.mean(scaled * normed, axis=-1, keepdims=True)
    )


def window_of(block):
    last = (block + 1) * QUERY_ROWS
    return max(0, last - WINDOW), last


def head_masks(width):
    lane = lax.broadcasted_iota(jnp.int32, (1, width), 1)
    return [jnp.where((lane // HEAD_DIM) % 2 == side, 1.0, 0.0).astype(bf16) for side in range(2)]


def attend_kernel(
    x_ref, gain_ref, bias_ref, wq_ref, wk_ref, wv_ref, seg_ref,
    attn_in_ref, q_ref, k_ref, v_ref, o_ref, lse_ref, mask_ref,
):
    length = x_ref.shape[0]
    blocks = length // QUERY_ROWS

    @pl.when(pl.program_id(0) == 0)
    def _():
        for block in range(blocks):
            rows = slice(block * QUERY_ROWS, (block + 1) * QUERY_ROWS)
            hat, _ = norm_parts(x_ref[rows, :].astype(f32))
            attn_in_ref[rows, :] = (hat * gain_ref[...] + bias_ref[...]).astype(bf16)
            start, stop = window_of(block)
            seg_col = column(seg_ref[:, rows])
            seg_row = seg_ref[:, start:stop].astype(f32)
            shape = (QUERY_ROWS, stop - start)
            query = lax.broadcasted_iota(jnp.int32, shape, 0) + rows.start
            key = lax.broadcasted_iota(jnp.int32, shape, 1) + start
            allowed = (seg_col == seg_row) & (key <= query)
            mask_ref[rows, : stop - start] = jnp.where(allowed, 0.0, NEG_LARGE)

    attn_in = attn_in_ref[...]
    q_ref[...] = (dot(attn_in, wq_ref[...]).astype(bf16) * (HEAD_DIM**-0.5)).astype(bf16)
    k_ref[...] = dot(attn_in, wk_ref[...]).astype(bf16)
    v_ref[...] = dot(attn_in, wv_ref[...]).astype(bf16)
    masks = head_masks(128)
    lane = lax.broadcasted_iota(jnp.int32, (QUERY_ROWS, 128), 1)
    for block in range(blocks):
        rows = slice(block * QUERY_ROWS, (block + 1) * QUERY_ROWS)
        start, stop = window_of(block)
        mask = mask_ref[rows, : stop - start]
        totals = jnp.zeros((QUERY_ROWS, 128), f32)
        for pair in range(LANES // 128):
            lanes = slice(pair * 128, (pair + 1) * 128)
            query = q_ref[rows, lanes]
            key = k_ref[start:stop, lanes]
            value = v_ref[start:stop, lanes]
            mixed = []
            for side in range(2):
                scores = dot_nt(query * masks[side], key) + mask
                row_max = jnp.max(scores, axis=1, keepdims=True)
                weights = jnp.exp(scores - row_max)
                total = jnp.sum(weights, axis=1, keepdims=True)
                prob = (weights * (1.0 / total)).astype(bf16)
                mixed.append(dot(prob, value))
                totals = jnp.where(lane == pair * 2 + side, row_max + jnp.log(total), totals)
            o_ref[rows, lanes] = jnp.where(lane < HEAD_DIM, mixed[0], mixed[1]).astype(bf16)
        lse_ref[0, :, rows] = totals.T[:8, :]


def attend_forward(tokens, gain, bias, wq, wk, wv, segment_ids):
    length, width = tokens.shape
    steps = width // LANES
    sliced = pl.BlockSpec((length, LANES), lambda i: (0, i))
    weight = pl.BlockSpec((width, LANES), lambda i: (0, i))
    act = shape_of((length, width), bf16)
    return pl.pallas_call(
        attend_kernel,
        grid=(steps,),
        in_specs=[
            full_spec((length, width)), full_spec((1, width)), full_spec((1, width)),
            weight, weight, weight, full_spec((1, length)),
        ],
        out_specs=[
            full_spec((length, width)), sliced, sliced, sliced, sliced,
            pl.BlockSpec((1, 8, length), lambda i: (i, 0, 0)),
        ],
        out_shape=[act, act, act, act, act, shape_of((steps, 8, length), f32)],
        scratch_shapes=[pltpu.VMEM((length, WINDOW), f32)],
        cost_estimate=cost(15e9, 15e6, 7e6),
        name="attend_forward",
    )(tokens, gain, bias, wq, wk, wv, segment_ids)


def attend_back_kernel(
    q_ref, k_ref, v_ref, do_ref, lse_ref, seg_ref, dq_ref, dk_ref, dv_ref,
    mask_ref, dk_sum, dv_sum,
):
    length = q_ref.shape[0]
    blocks = length // QUERY_ROWS
    for block in range(blocks):
        rows = slice(block * QUERY_ROWS, (block + 1) * QUERY_ROWS)
        start, stop = window_of(block)
        seg_col = column(seg_ref[:, start:stop])
        seg_row = seg_ref[:, rows].astype(f32)
        shape = (stop - start, QUERY_ROWS)
        query = lax.broadcasted_iota(jnp.int32, shape, 1) + rows.start
        key = lax.broadcasted_iota(jnp.int32, shape, 0) + start
        allowed = (seg_col == seg_row) & (key <= query)
        mask_ref[: stop - start, rows] = jnp.where(allowed, 0.0, NEG_LARGE)

    dk_sum[...] = jnp.zeros_like(dk_sum)
    dv_sum[...] = jnp.zeros_like(dv_sum)
    masks = head_masks(128)
    for pair in range(LANES // 128):
        lanes = slice(pair * 128, (pair + 1) * 128)
        key_turned = k_ref[:, lanes].T
        for block in range(blocks):
            rows = slice(block * QUERY_ROWS, (block + 1) * QUERY_ROWS)
            start, stop = window_of(block)
            mask = mask_ref[: stop - start, rows]
            key = k_ref[start:stop, lanes]
            value = v_ref[start:stop, lanes]
            grads = []
            for side in range(2):
                query = q_ref[rows, lanes] * masks[side]
                grad = do_ref[rows, lanes] * masks[side]
                total = lse_ref[0, pair * 2 + side : pair * 2 + side + 1, rows]
                prob = jnp.exp(dot_nt(key, query) + mask - total)
                grad_prob = dot_nt(value, grad)
                both = prob * grad_prob
                row_sum = jnp.sum(both, axis=0, keepdims=True)
                grad_scores = (both - prob * row_sum).astype(bf16)
                dv_sum[start:stop, lanes] += dot(prob.astype(bf16), grad)
                dk_sum[start:stop, lanes] += dot(grad_scores, query)
                turned = key_turned[side * HEAD_DIM : (side + 1) * HEAD_DIM, start:stop]
                grads.append(dot(turned, grad_scores))
            turned = jnp.concatenate(grads, axis=0) * (HEAD_DIM**-0.5)
            dq_ref[rows, lanes] = turned.T.astype(bf16)
    dk_ref[...] = dk_sum[...].astype(bf16)
    dv_ref[...] = dv_sum[...].astype(bf16)


def attend_backward(which, q, k, v, do, lse, segment_ids):
    length = q.shape[0]
    sliced = pl.BlockSpec((length, LANES), lambda i: (0, which))
    out = full_spec((length, LANES), 1)
    act = shape_of((length, LANES), bf16)
    return pl.pallas_call(
        attend_back_kernel,
        grid=(1,),
        in_specs=[
            sliced, sliced, sliced, sliced,
            pl.BlockSpec((1, 8, length), lambda i: (which, 0, 0)), full_spec((1, length)),
        ],
        out_specs=[out, out, out],
        out_shape=[act, act, act],
        scratch_shapes=[
            pltpu.VMEM((WINDOW, length), f32),
            pltpu.VMEM((length, LANES), f32), pltpu.VMEM((length, LANES), f32),
        ],
        cost_estimate=cost(10e9, 4e6, 2e6),
        name="attend_backward_%d" % which,
    )(q, k, v, do, lse, segment_ids)


def project_kernel(x_ref, o_ref, wo_ref, gain_ref, bias_ref, y_ref, h_ref):
    resid = x_ref[...].astype(f32) + dot(o_ref[...], wo_ref[...])
    hat, _ = norm_parts(resid)
    y_ref[...] = resid
    h_ref[...] = (hat * gain_ref[...] + bias_ref[...]).astype(bf16)


def project(tokens, o, wo, gain, bias):
    length, width = tokens.shape
    rows = 256
    block = pl.BlockSpec((rows, width), lambda i: (i, 0))
    return pl.pallas_call(
        project_kernel,
        grid=(length // rows,),
        in_specs=[block, block, full_spec((width, width)), full_spec((1, width)), full_spec((1, width))],
        out_specs=[block, block],
        out_shape=[shape_of((length, width), f32), shape_of((length, width), bf16)],
        cost_estimate=cost(1.3e9, 9e6),
        name="project",
    )(tokens, o, wo, gain, bias)


def slots_kernel(capacity, groups, local, me_ref, counts_ref, order_ref, slot_ref):
    tokens = order_ref.shape[1]
    me = me_ref[0, 0]
    place = lax.broadcasted_iota(jnp.int32, (1, tokens), 1)
    slot = jnp.zeros((1, tokens), jnp.int32)
    lower = jnp.int32(0)
    for expert in range(groups * local):
        count = counts_ref[0, expert]
        base = ((expert % local) * groups + lax.bitwise_xor(me, expert // local)) * capacity - lower
        inside = (place >= lower) & (place < lower + count)
        slot = jnp.where(inside, place + base, slot)
        lower = lower + count
    order_col = column(order_ref[...])
    slot_col = column(slot)
    place_f = place.astype(f32)
    total = jnp.zeros((1, tokens), f32)
    step = 256
    for first in range(0, tokens, step):
        hit = order_col[first : first + step] == place_f
        total = total + jnp.sum(jnp.where(hit, slot_col[first : first + step], 0.0), axis=0, keepdims=True)
    slot_ref[...] = total.astype(jnp.int32)


def token_slots(me, counts, order, capacity, groups, local):
    tokens = order.shape[1]
    return pl.pallas_call(
        functools.partial(slots_kernel, capacity, groups, local),
        in_specs=[smem(), smem(), pl.BlockSpec(memory_space=pltpu.VMEM)],
        out_specs=pl.BlockSpec(memory_space=pltpu.VMEM),
        out_shape=shape_of((1, tokens), jnp.int32),
        cost_estimate=cost(4e6, 1e4),
        name="token_slots",
    )(me, counts, order)


def dispatch_kernel(capacity, groups, owns, slot_ref, x_ref, *out_refs):
    tokens = x_ref.shape[0]
    rows = min(capacity * groups, 1024)
    x = x_ref[...]
    for place, own in enumerate(owns):
        at = slice(place * capacity, (place + 1) * capacity)
        for first in range(0, capacity * groups, rows):
            slot = lax.broadcasted_iota(jnp.int32, (rows, tokens), 0) + (own * groups * capacity + first)
            hit = jnp.where(slot == slot_ref[...], 1.0, 0.0).astype(bf16)
            found = dot(hit, x).astype(bf16)
            for part in range(rows // capacity):
                out_refs[first // capacity + part][at, :] = found[part * capacity : (part + 1) * capacity, :]


def dispatch(owns, slots, rows, capacity, groups):
    width = rows.shape[1]
    vmem = pl.BlockSpec(memory_space=pltpu.VMEM)
    return pl.pallas_call(
        functools.partial(dispatch_kernel, capacity, groups, owns),
        in_specs=[vmem, vmem],
        out_specs=[vmem] * groups,
        out_shape=[shape_of((len(owns) * capacity, width), bf16)] * groups,
        cost_estimate=cost(2e9, 3e6),
        name="dispatch_%d" % owns[0],
    )(slots, rows)


def collect_kernel(capacity, groups, own, slot_ref, *refs):
    part_refs, out_ref, all_parts = refs[:groups], refs[groups], refs[groups + 1]
    for which in range(groups):
        all_parts[which * capacity : (which + 1) * capacity, :] = part_refs[which][...]
    out_ref[...] = collected(slot_ref[...], all_parts[...], own).astype(bf16)


def collected(slot_row, parts, own):
    slot_col = column(slot_row).astype(jnp.int32)
    shape = (slot_col.shape[0], parts.shape[0])
    slot = lax.broadcasted_iota(jnp.int32, shape, 1) + own * parts.shape[0]
    return dot(jnp.where(slot == slot_col, 1.0, 0.0).astype(bf16), parts)


def collect(own, slots, parts, capacity, half=0):
    groups, width = len(parts), parts[0].shape[1]
    tokens = slots.shape[1]
    return pl.pallas_call(
        functools.partial(collect_kernel, capacity, groups, own),
        grid=(1,),
        in_specs=[full_spec((1, tokens), 1)]
        + [pl.BlockSpec((capacity, width), lambda i: (half, 0), pipeline_mode=pl.Buffered(1))] * groups,
        out_specs=full_spec((tokens, width), 1),
        out_shape=shape_of((tokens, width), bf16),
        scratch_shapes=[pltpu.VMEM((groups * capacity, width), bf16)],
        cost_estimate=cost(2e9, 3e6),
        name="collect_%d" % own,
    )(slots, *parts)


def gelu_parts(pre):
    cdf = 0.5 * (1.0 + lax.erf(pre * ROOT_HALF))
    density = NORMAL_PEAK * jnp.exp(-0.5 * pre * pre)
    return pre * cdf, cdf + pre * density


def expert_kernel(capacity, groups, local, own, joined, rows2, me_ref, counts_ref, router_ref, *refs):
    h_refs, g_refs = refs[:groups], refs[groups : 2 * groups]
    w1_ref, w2_ref = refs[2 * groups : 2 * groups + 2]
    refs = refs[2 * groups + 2 :]
    if joined:
        dh_refs = [ref.at[:capacity] for ref in refs[:groups]]
        z_refs = [ref.at[capacity:] for ref in refs[:groups]]
        refs = refs[groups:]
    else:
        dh_refs, z_refs = refs[:groups], refs[groups : 2 * groups]
        refs = refs[2 * groups :]
    dw_ref = refs[0]
    h_all, g_all, gz_all, h_turned, gate_all, z_sum, du_sum, z_low, dh_low, w1_stage, w2_stage, sems = refs[1:]
    slab = capacity * groups
    piece = 256
    step = pl.program_id(0)
    expert = me_ref[0, 0] * local + own
    starts = []
    lower = jnp.int32(0)
    for source in range(groups):
        starts.append(pl.multiple_of(lower, 16))
        lower = lower + (counts_ref[source, expert] + 15) // 16 * 16
    pieces = jnp.maximum((lower + piece - 1) // piece, 1)
    router = router_ref[pl.ds(expert, 1), :]

    _, shards_count, rows1, block = w1_stage.shape
    width = w2_stage.shape[2]
    sub = math.gcd(block, rows2)
    per_slab = width // block

    def copies(at, slot):
        found = [
            pltpu.make_async_copy(
                w1_stage.at[slot],
                dw_ref.at[
                    :,
                    pl.ds(pl.multiple_of(rows2 + at // per_slab * rows1, 16), rows1),
                    pl.ds(pl.multiple_of(at % per_slab * block, 128), block),
                ],
                sems.at[slot, 0],
            )
        ]
        for which in range(block // sub):
            place = at * (block // sub) + which
            shard = place * sub // rows2
            row = pl.multiple_of(place * sub - shard * rows2, 16)
            found.append(
                pltpu.make_async_copy(
                    w2_stage.at[slot, pl.ds(which * sub, sub)],
                    dw_ref.at[shard, pl.ds(row, sub)],
                    sems.at[slot, 1 + which],
                )
            )
        return found

    @pl.when(step == 0)
    def _():
        h_all[...] = jnp.zeros_like(h_all)
        g_all[...] = jnp.zeros_like(g_all)
        z_sum[...] = jnp.zeros_like(z_sum)
        du_sum[...] = jnp.zeros_like(du_sum)
        for source in range(groups):
            h_all[pl.ds(starts[source], capacity), :] = h_refs[source][...]
            g_all[pl.ds(starts[source], capacity), :] = g_refs[source][...]
        for first in range(0, slab, piece):
            rows = slice(first, first + piece)
            h = h_all[rows, :]
            gate = jax.nn.sigmoid(jnp.sum(h.astype(f32) * router, axis=1, keepdims=True))
            gate_all[rows, :] = jnp.broadcast_to(gate, (piece, 128))
            gz_all[rows, :] = (gate * g_all[rows, :].astype(f32)).astype(bf16)
            h_turned[:, rows] = h.T

    slot = lax.rem(step, 2)

    @pl.when(step >= 2)
    def _():
        for copy in copies(step - 2, slot):
            copy.wait()

    for count in range(1, slab // piece + 1):

        @pl.when(pieces == count)
        def _():
            rows = slice(0, count * piece)
            h, gz = h_all[rows, :], gz_all[rows, :]
            w1, w2 = w1_ref[0], w2_ref[0]
            hid, slope = gelu_parts(dot(h, w1))
            hid = hid.astype(bf16)
            z_sum[rows, :] += dot(hid, w2)
            dpre = (dot_nt(gz, w2) * slope).astype(bf16)
            w2_stage[slot] = dot_tn(hid, gz).astype(bf16)
            w1_stage[slot] = dot(h_turned[:, rows], dpre).astype(bf16).reshape(shards_count, rows1, block)
            du_sum[rows, :] += dot_nt(dpre, w1)

    for copy in copies(step, slot):
        copy.start()

    @pl.when(step == pl.num_programs(0) - 1)
    def _():
        for first in range(0, slab, piece):
            rows = slice(first, first + piece)
            gate = gate_all[rows, :1]
            z = z_sum[rows, :]
            dlogit = jnp.sum(g_all[rows, :].astype(f32) * z, axis=1, keepdims=True) * gate * (1.0 - gate)
            z_low[rows, :] = (gate * z).astype(bf16)
            dh_low[rows, :] = (du_sum[rows, :] + dlogit * router).astype(bf16)
        for source in range(groups):
            z_refs[source][...] = z_low[pl.ds(starts[source], capacity), :]
            dh_refs[source][...] = dh_low[pl.ds(starts[source], capacity), :]
        for copy in copies(step - 1, 1 - slot) + copies(step, slot):
            copy.wait()


def run_expert(own, me, counts, router, h_parts, g_parts, expert_in, expert_out, capacity, joined):
    groups = len(h_parts)
    local, width, hidden = expert_in.shape
    shards_count = lax.axis_size("dp")
    slab = capacity * groups
    block = 256
    rows1, rows2 = width // shards_count, hidden // shards_count
    part = full_spec((capacity, width), 1)
    own_part = pl.BlockSpec((capacity, width), lambda f: (own, 0), pipeline_mode=pl.Buffered(1))
    ends = groups if joined else 2 * groups
    end_rows = 2 * capacity if joined else capacity
    results = pl.pallas_call(
        functools.partial(expert_kernel, capacity, groups, local, own, joined, rows2),
        grid=(hidden // block,),
        in_specs=[smem(), smem(), full_spec(router.shape)] + [part] * groups + [own_part] * groups + [
            pl.BlockSpec((1, width, block), lambda f: (own, 0, f)),
            pl.BlockSpec((1, block, width), lambda f: (own, f, 0)),
        ],
        out_specs=[full_spec((end_rows, width), 1)] * ends + [pl.BlockSpec(memory_space=pl.ANY)],
        out_shape=[shape_of((end_rows, width), bf16)] * ends
        + [shape_of((shards_count, rows2 + rows1 * (hidden // width), width), bf16)],
        scratch_shapes=[
            pltpu.VMEM((slab, width), bf16), pltpu.VMEM((slab, width), bf16),
            pltpu.VMEM((slab, width), bf16), pltpu.VMEM((width, slab), bf16),
            pltpu.VMEM((slab, 128), f32),
            pltpu.VMEM((slab, width), f32), pltpu.VMEM((slab, width), f32),
            pltpu.VMEM((slab, width), bf16), pltpu.VMEM((slab, width), bf16),
            pltpu.VMEM((2, shards_count, rows1, block), bf16), pltpu.VMEM((2, block, width), bf16),
            pltpu.SemaphoreType.DMA((2, 1 + block // math.gcd(block, rows2))),
        ],
        cost_estimate=cost(25e9, 25e6, 6e6),
        name="expert_%d" % own,
    )(me, counts, router, *h_parts, *g_parts, expert_in, expert_out)
    return results[:-1], results[-1]


def shares_kernel(rows1, rows2, has_before, share_ref, *refs):
    first_ref, second_ref = refs[2:] if has_before else refs
    width = share_ref.shape[1]
    second_ref[0] = share_ref[:rows2, :].astype(f32)
    for slab in range(first_ref.shape[2] // width):
        rows = slice(rows2 + slab * rows1, rows2 + (slab + 1) * rows1)
        first_ref[0, :, slab * width : (slab + 1) * width] = share_ref[rows, :].astype(f32)


def unpack_shares(own, share, before, local, rows1, rows2, hidden):
    width = share.shape[1]
    anywhere = pl.BlockSpec(memory_space=pl.ANY)
    return pl.pallas_call(
        functools.partial(shares_kernel, rows1, rows2, before is not None),
        grid=(1,),
        in_specs=[full_spec(share.shape, 1)] + ([] if before is None else [anywhere, anywhere]),
        out_specs=[
            pl.BlockSpec((1, rows1, hidden), lambda i: (own, 0, 0)),
            pl.BlockSpec((1, rows2, width), lambda i: (own, 0, 0)),
        ],
        out_shape=[shape_of((local, rows1, hidden), f32), shape_of((local, rows2, width), f32)],
        input_output_aliases={} if before is None else {1: 0, 2: 1},
        cost_estimate=cost(1, 1),
        name="unpack_shares",
    )(share, *([] if before is None else before))


def norm2_kernel(
    dh0_ref, dh1_ref, y_ref, g_ref, o_ref, wo_ref, gain_ref,
    dy_ref, do_ref, dwo_ref, vec_ref, dwo_sum, gain_sum, bias_sum,
):
    step = pl.program_id(0)

    @pl.when(step == 0)
    def _():
        dwo_sum[...] = jnp.zeros_like(dwo_sum)
        gain_sum[...] = jnp.zeros_like(gain_sum)
        bias_sum[...] = jnp.zeros_like(bias_sum)

    dh = dh0_ref[...].astype(f32) + dh1_ref[...].astype(f32)
    hat, inverse_std = norm_parts(y_ref[...])
    gain_sum[...] += jnp.sum(dh * hat, axis=0, keepdims=True)
    bias_sum[...] += jnp.sum(dh, axis=0, keepdims=True)
    dy = g_ref[...].astype(f32) + norm_back(dh, hat, inverse_std, gain_ref[...])
    dy_ref[...] = dy
    dyb = dy.astype(bf16)
    do_ref[...] = dot_nt(dyb, wo_ref[...]).astype(bf16)
    dwo_sum[...] += dot_tn(o_ref[...], dyb)

    @pl.when(step == pl.num_programs(0) - 1)
    def _():
        dwo_ref[...] = dwo_sum[...].astype(bf16)
        vec_ref[0:1, :] = gain_sum[...]
        vec_ref[1:2, :] = bias_sum[...]


def norm2_back(dh_own, y, cotangent, o, wo, gain):
    length, width = y.shape
    rows = 256
    block = pl.BlockSpec((rows, width), lambda i: (i, 0))
    return pl.pallas_call(
        norm2_kernel,
        grid=(length // rows,),
        in_specs=[block] * 5 + [full_spec((width, width)), full_spec((1, width))],
        out_specs=[block, block, full_spec((width, width)), full_spec((2, width))],
        out_shape=[
            shape_of((length, width), f32), shape_of((length, width), bf16),
            shape_of((width, width), bf16), shape_of((2, width), f32),
        ],
        scratch_shapes=[pltpu.VMEM((width, width), f32), pltpu.VMEM((1, width), f32), pltpu.VMEM((1, width), f32)],
        cost_estimate=cost(3e9, 15e6),
        name="norm2_back",
    )(*dh_own, y, cotangent, o, wo, gain)


def result_kernel(y_ref, z0_ref, z1_ref, out_ref):
    out_ref[...] = (y_ref[...] + (z0_ref[...].astype(f32) + z1_ref[...].astype(f32))).astype(bf16)


def block_result(y, z_own):
    length, width = y.shape
    rows = 256
    block = pl.BlockSpec((rows, width), lambda i: (i, 0))
    return pl.pallas_call(
        result_kernel,
        grid=(length // rows,),
        in_specs=[block] * 3,
        out_specs=block,
        out_shape=shape_of((length, width), bf16),
        cost_estimate=cost(3e6, 8e6),
        name="block_result",
    )(y, *z_own)


def norm1_kernel(cuts, attn_in_ref, x_ref, dy_ref, wq_ref, wk_ref, wv_ref, gain_ref, vec2_ref, *refs):
    grad_refs = refs[: 3 * cuts]
    dx_ref, dw_ref, dw_sum, gain_sum, bias_sum = refs[3 * cuts :]
    step = pl.program_id(0)
    width = x_ref.shape[1]

    @pl.when(step == 0)
    def _():
        dw_sum[...] = jnp.zeros_like(dw_sum)
        gain_sum[...] = jnp.zeros_like(gain_sum)
        bias_sum[...] = jnp.zeros_like(bias_sum)

    da = None
    turned = attn_in_ref[...].T
    for which, w_ref in enumerate((wq_ref, wk_ref, wv_ref)):
        grad = jnp.concatenate([grad_refs[3 * cut + which][...] for cut in range(cuts)], axis=1)
        term = dot_nt(grad, w_ref[...])
        da = term if da is None else da + term
        dw_sum[which * width : (which + 1) * width, :] += dot(turned, grad)
    hat, inverse_std = norm_parts(x_ref[...].astype(f32))
    gain_sum[...] += jnp.sum(da * hat, axis=0, keepdims=True)
    bias_sum[...] += jnp.sum(da, axis=0, keepdims=True)
    dx_ref[...] = (dy_ref[...] + norm_back(da, hat, inverse_std, gain_ref[...])).astype(bf16)

    @pl.when(step == pl.num_programs(0) - 1)
    def _():
        dw_ref[: 3 * width, :] = dw_sum[...].astype(bf16)
        vectors = jnp.concatenate(
            [gain_sum[...], bias_sum[...], vec2_ref[...], jnp.zeros((12, width), f32)], axis=0
        )
        high = vectors.astype(bf16)
        dw_ref[3 * width : 3 * width + 16, :] = high
        dw_ref[3 * width + 16 : 3 * width + 32, :] = (vectors - high.astype(f32)).astype(bf16)
        rest = dw_ref.shape[0] - 3 * width - 32
        dw_ref[3 * width + 32 :, :] = jnp.zeros((rest, width), bf16)


def norm1_back(attn_in, grads, tokens, dy, wq, wk, wv, gain, vec2):
    length, width = tokens.shape
    rows = 256
    total = 3 * width + 256
    cuts = len(grads)
    block = pl.BlockSpec((rows, width), lambda i: (i, 0))
    part = pl.BlockSpec((rows, width // cuts), lambda i: (i, 0))
    weight = full_spec((width, width))
    return pl.pallas_call(
        functools.partial(norm1_kernel, cuts),
        grid=(length // rows,),
        in_specs=[block] * 3 + [weight] * 3 + [full_spec((1, width)), full_spec((2, width))] + [part] * (3 * cuts),
        out_specs=[block, full_spec((total, width), 1)],
        out_shape=[shape_of((length, width), bf16), shape_of((total, width), bf16)],
        scratch_shapes=[
            pltpu.VMEM((3 * width, width), f32), pltpu.VMEM((1, width), f32), pltpu.VMEM((1, width), f32),
        ],
        cost_estimate=cost(8e9, 20e6),
        name="norm1_back",
    )(attn_in, tokens, dy, wq, wk, wv, gain, vec2, *[grad for three in grads for grad in three])


def swap(array, axis, step):
    count = lax.axis_size(axis)
    return lax.ppermute(array, axis, [(i, i ^ step) for i in range(count)])


def add_picked_kernel(count, outs, base, me_ref, *refs):
    me = me_ref[0, 0]
    offset = me_ref[0, 1]
    for step in range(outs):
        index = offset * base + lax.bitwise_xor(me, step)
        total = refs[0][index].astype(f32)
        for ref in refs[1:count]:
            total = total + ref[index].astype(f32)
        refs[count + step][...] = total.astype(bf16)


def add_picked(arrays, outs, base, me, name):
    _, rows, width = arrays[0].shape
    vmem = pl.BlockSpec(memory_space=pltpu.VMEM)
    return pl.pallas_call(
        functools.partial(add_picked_kernel, len(arrays), outs, base),
        in_specs=[smem()] + [vmem] * len(arrays),
        out_specs=[vmem] * outs,
        out_shape=[shape_of((rows, width), bf16)] * outs,
        cost_estimate=cost(1e6, 2 * rows * width * outs * (len(arrays) + 1)),
        name=name,
    )(me, *arrays)


def add_kernel(*refs):
    total = refs[0][...].astype(f32)
    for ref in refs[1:-1]:
        total = total + ref[...].astype(f32)
    refs[-1][...] = total.astype(bf16)


def add_parts(arrays):
    vmem = pl.BlockSpec(memory_space=pltpu.VMEM)
    return pl.pallas_call(
        add_kernel,
        in_specs=[vmem] * len(arrays),
        out_specs=vmem,
        out_shape=shape_of(arrays[0].shape, bf16),
        cost_estimate=cost(1e6, arrays[0].size * 2 * (len(arrays) + 1)),
        name="add_parts",
    )(*arrays)


def line_kernel(count, me_ref, *refs):
    for step in range(count):
        refs[count][lax.bitwise_xor(me_ref[0, 0], step)] = refs[step][...]


def line_up(arrays, me):
    vmem = pl.BlockSpec(memory_space=pltpu.VMEM)
    count = len(arrays)
    return pl.pallas_call(
        functools.partial(line_kernel, count),
        in_specs=[smem()] + [vmem] * count,
        out_specs=vmem,
        out_shape=shape_of((count, *arrays[0].shape), bf16),
        cost_estimate=cost(1e3, arrays[0].size * 4 * count),
        name="line_up",
    )(me, *arrays)


def finish_kernel(groups, parts, has_vectors, me_ref, *refs):
    count = 2 * groups
    lines, outs, full = refs[:count], refs[count : count + parts], refs[-1]
    vec_ref = refs[count + parts]
    me, core = me_ref[0, 0], me_ref[0, 1]
    for side in range(2):
        for step in range(groups):
            index = lax.bitwise_xor(core, side) * groups + lax.bitwise_xor(me, step)
            full[index] = lines[side * groups + step][...]
    piece = full.shape[1]
    width = outs[0].shape[1]
    row = 0
    while row < parts * width:
        index, inside = row // piece, row % piece
        which, at = row // width, row % width
        size = min(piece - inside, width - at)
        outs[which][at : at + size, :] = full[index, inside : inside + size, :].astype(f32)
        row += size
    if not has_vectors:
        return
    row = parts * width
    sums = []
    for start in (row, row + 16):
        index, inside = start // piece, start % piece
        sums.append(full[index, inside : inside + 8, :].astype(f32))
    vec_ref[...] = sums[0] + sums[1]


def finish(lines, parts, groups, me):
    piece, width = lines[0].shape
    has_vectors = 2 * groups * piece > parts * width
    vmem = pl.BlockSpec(memory_space=pltpu.VMEM)
    return pl.pallas_call(
        functools.partial(finish_kernel, groups, parts, has_vectors),
        in_specs=[smem()] + [vmem] * len(lines),
        out_specs=[vmem] * (parts + has_vectors),
        out_shape=[shape_of((width, width), f32)] * parts + [shape_of((8, width), f32)] * has_vectors,
        scratch_shapes=[pltpu.VMEM((2 * groups, piece, width), bf16)],
        cost_estimate=cost(1e3, 15e6),
        name="finish",
    )(me, *lines)


def sum_all(array, parts):
    dp, groups = lax.axis_size("dp"), lax.axis_size("expert")
    depth = dp // 2
    me = lax.axis_index("expert").astype(jnp.int32)
    core = (lax.axis_index("dp") % 2).astype(jnp.int32)
    place = (lax.axis_index("dp") // 2).astype(jnp.int32)
    here = jnp.stack([me, core]).reshape(1, 2)
    there = jnp.stack([place, jnp.int32(0)]).reshape(1, 2)
    rows, width = array.shape
    piece = rows // (2 * groups)
    other = swap(array, "dp", 1)
    other = yield other
    shape = (2 * groups, piece, width)
    halves = add_picked([array.reshape(shape), other.reshape(shape)], groups, groups, here, "add_cores")
    shape = (depth, piece // depth, width)
    came = yield [halves[0]] + [swap(halves[step], "expert", step) for step in range(1, groups)]
    halves = add_picked([part.reshape(shape) for part in came], depth, 0, there, "add_groups")
    mine = yield [halves[0]] + [swap(halves[step], "dp", 2 * step) for step in range(1, depth)]
    mine = add_parts(mine)
    line = yield [mine] + [swap(mine, "dp", 2 * step) for step in range(1, depth)]
    line = line_up(line, there)
    line = line.reshape(piece, width)
    plane = yield [line] + [swap(line, "expert", step) for step in range(1, groups)]
    lines = yield plane + [swap(part, "dp", 1) for part in plane]
    yield finish(lines, parts, groups, here)


def last_of(rounds, value):
    while True:
        try:
            value = rounds.send(value)
        except StopIteration:
            return value


def shards(
    tokens, segment_ids, expert_order, expert_counts, norm1_gain, norm1_bias,
    query_w, key_w, value_w, out_w, norm2_gain, norm2_bias, router_w,
    expert_in, expert_out, cotangent,
):
    groups = lax.axis_size("expert")
    local = expert_in.shape[0]
    experts = expert_counts.shape[1]
    length, width = tokens.shape
    capacity = 2 * length // experts
    me_index = lax.axis_index("expert").astype(jnp.int32)
    me = me_index.reshape(1, 1)
    gain1, bias1 = norm1_gain.reshape(1, width), norm1_bias.reshape(1, width)
    gain2, bias2 = norm2_gain.reshape(1, width), norm2_bias.reshape(1, width)
    router = router_w.T.astype(f32)

    def exchange(parts):
        return [parts[0]] + [swap(parts[step], "expert", step) for step in range(1, groups)]

    barrier = lax.optimization_barrier
    counts_all = jnp.concatenate(
        [expert_counts] + [swap(expert_counts, "expert", step) for step in range(1, groups)], axis=0
    )
    slots = token_slots(me, expert_counts, expert_order.reshape(1, length), capacity, groups, local)
    g_parts = exchange(dispatch(tuple(range(local)), slots, cotangent, capacity, groups))
    attn_in, q, k, v, o, lse = attend_forward(tokens, gain1, bias1, query_w, key_w, value_w, segment_ids)
    o, g_parts, counts_all = barrier((o, g_parts, counts_all))
    y, h = project(tokens, o, out_w, gain2, bias2)
    h_out = [dispatch((own,), slots, h, capacity, groups) for own in range(local)]
    h_parts = [exchange(out) for out in h_out]
    h_parts[0], _ = barrier((h_parts[0], h_out))

    def expert(own, joined):
        return run_expert(
            own, me, counts_all, router, h_parts[own], g_parts, expert_in, expert_out, capacity, joined
        )

    def scatter(array):
        share = lax.psum_scatter(array, "dp", scatter_dimension=0, tiled=True)
        return share.reshape(share.shape[1:])

    joined_ins, grads_out = [], []
    for own in range(local - 1):
        out, dw = expert(own, True)
        dw, h_parts[own + 1] = barrier((dw, h_parts[own + 1]))
        h_parts[own + 1], _ = barrier((h_parts[own + 1], out))
        grads_out.append(scatter(dw))
        joined_ins.append(exchange(out))
    own = local - 1
    out, dw_last = expert(own, False)
    dh_out, z_out = out[:groups], out[groups:]
    dh_in = exchange(dh_out)
    dh_own = []
    for before in range(own):
        joined_ins[before], _ = barrier((joined_ins[before], dh_out))
        dh_own.append(collect(before, slots, joined_ins[before], capacity))
    dh_in, _ = barrier((dh_in, dh_own))
    dh_own.append(collect(own, slots, dh_in, capacity))
    dh_own, dw_last, z_out = barrier((dh_own, dw_last, z_out))
    grads_out.append(scatter(dw_last))
    z_in = exchange(z_out)
    dy, do, grad_out, vec2 = norm2_back(dh_own, y, cotangent, o, out_w, gain2)
    rounds = sum_all(grad_out, 1)
    early = next(rounds)
    grads = []
    for which in range(width // LANES):
        grads.append(attend_backward(which, q, k, v, do, lse, segment_ids))
        early, z_in, q, attn_in, grads = barrier((early, z_in, q, attn_in, grads))
        early = rounds.send(early)
        first, q, attn_in = barrier((early[0], q, attn_in))
        early = [first] + list(early[1:])
    dx, grad_qkv = norm1_back(attn_in, grads, tokens, dy, query_w, key_w, value_w, gain1, vec2)
    late = sum_all(grad_qkv, 3)
    swapped, early = barrier((next(late), early))
    early = rounds.send(early)
    came = late.send(swapped)
    z_own = [collect(before, slots, joined_ins[before], capacity, 1) for before in range(own)]
    z_own.append(collect(own, slots, z_in, capacity))
    block_out = block_result(y, z_own)
    came, early, block_out = barrier((came, early, block_out))
    grad_o = last_of(rounds, early)[0]
    grad_q, grad_k, grad_v, vectors = last_of(late, came)
    shares = None
    for which in range(local):
        shares = unpack_shares(
            which, grads_out[which], shares, local, width // lax.axis_size("dp"),
            expert_in.shape[2] // lax.axis_size("dp"), expert_in.shape[2],
        )
    return (
        block_out,
        dx,
        vectors[0],
        vectors[1],
        grad_q,
        grad_k,
        grad_v,
        grad_o,
        vectors[2],
        vectors[3],
        shares[0],
        shares[1],
    )


def solution(mesh):
    placed = (
        P(("dp", "expert"), None), P(("dp", "expert"), None), P(("dp", "expert")), P(("dp", "expert"), None),
        P(), P(), P(), P(), P(), P(), P(), P(), P(),
        P("expert", None, None), P("expert", None, None), P(("dp", "expert"), None),
    )
    return jax.shard_map(
        shards,
        mesh=mesh,
        in_specs=placed,
        out_specs=(
            P(("dp", "expert"), None), P(("dp", "expert"), None),
            P(), P(), P(), P(), P(), P(), P(), P(),
            P("expert", "dp", None), P("expert", "dp", None),
        ),
        check_vma=False,
    )
```

time: 1000 us -> 445 us (0.45)
  matrix products: 449 us -> 0 us
  Pallas kernels: 0 us -> 231 us
  blocking collectives: 122 us -> 0 us
  local copies, waits for them, and re-layouts: 122 us -> 15.5 us
  other arithmetic: 94.3 us -> 2.46 us
  waiting for transfers between devices: 174 us -> 89.8 us
  starting transfers between devices: 9.56 us -> 90.8 us
    dot_general x35 -> x0, matrix products: 449 us -> none  [the longest x1 70 us: shards(): jnp.einsum('erf,erd->efd', act_again, arrived_grad, preferred_element_typ...]
    pallas_call x0 -> x30, Pallas kernels: none -> 231 us  [the longest x2 59.8 us: run_expert(): pl.pallas_call(functools.partial(expert_kernel, capacity, groups, local,...]
    psum x1 -> x0, waiting for transfers between devices: 130 us -> none  [shards(): lax.psum((grad_gain1, grad_bias1, grad_qw, grad_kw, grad_vw, grad_outw, g...]
    ppermute x0 -> x55, starting transfers between devices: none -> 90.7 us  [swap(): return lax.ppermute(array, axis, [(i, i ^ step) for i in range(count)])]
    ppermute x0 -> x55, waiting for transfers between devices: none -> 89.7 us  [swap(): return lax.ppermute(array, axis, [(i, i ^ step) for i in range(count)])]
    all_to_all x2 -> x0, blocking collectives: 80.2 us -> none  [the longest x1 41.6 us: shards(): lax.all_to_all(outgoing, 'expert', split_axis=0, concat_axis=2, tiled=True)]
    convert_element_type x8 -> x1, other arithmetic: 53.3 us -> 0.66 us  [shards(): router = router_w.T.astype(f32)]
    gather x7 -> x0, local copies, waits for them, and re-layouts: 46.5 us -> none  [the longest x2 10.6 us: shards(): returned.reshape(experts * capacity, model_width)[buffer_row]]
  transfers between devices with their start and end apart: 5 -> 57, of which waited for: 3 -> 19; matrix products, arithmetic and copies ran while one was open for 30% -> 1% of each run, Pallas kernels for 0% -> 47%
where the time goes in v1:
time: 445 us; the launch traced here: 444 us
  Pallas kernels  231 us (52%)
  starting transfers between devices  90.8 us (20%)
  waiting for transfers between devices  89.8 us (20%)
  local copies, waits for them, and re-layouts  15.5 us (3%)
  between operations  14.9 us (3%)
    ppermute x55, starting transfers between devices, swap(): return lax.ppermute(array, axis, [(i, i ^ step) for i in range(count)])  90.7 us
    ppermute x55, waiting for transfers between devices, swap(): return lax.ppermute(array, axis, [(i, i ^ step) for i in range(count)])  89.7 us
    pallas_call x2, Pallas kernels, run_expert(): pl.pallas_call(functools.partial(expert_kernel, capacity, groups, local,...  59.8 us
    pallas_call x3, Pallas kernels, attend_backward(): pl.pallas_call(attend_back_kernel, grid=(1,), in_specs=[sliced, sliced, s...  32.7 us
    pallas_call x1, Pallas kernels, attend_forward(): pl.pallas_call(attend_kernel, grid=(steps,), in_specs=[full_spec((length,...  32.2 us
    pallas_call x4, Pallas kernels, collect(): pl.pallas_call(functools.partial(collect_kernel, capacity, groups, own),...  19 us
    pallas_call x1, Pallas kernels, norm1_back(): pl.pallas_call(functools.partial(norm1_kernel, cuts), grid=(length // row...  15.5 us
    pallas_call x3, Pallas kernels, dispatch(): pl.pallas_call(functools.partial(dispatch_kernel, capacity, groups, owns)...  14.7 us
  transfers between devices with their start and end apart: 57, of which 19 were waited for; matrix products, arithmetic and copies ran while one was open for 1% of the time, Pallas kernels for 47%

profile of v1, /device:TPU:0, one launch (start us, length us, event | category | flops | bytes accessed | tf_op | source)
XLA Modules:
  0.0 444.2 jit_solution(6401244036481754164)
XLA Ops:
  7.3 2.1 token_slots.1.slot_ref
  9.4 6.4 %dispatch_0.2 = (bf16[512,768]{1,0:T(8,128)(2,1)}, bf16[512,768]{1,0:T(8,128)(2,1)}, bf16[512,768]{1,0:T(8,128)(2,1)}, bf16[512,768]{1,0:T(8,128)(2,1)}) custom-call(s32[1,1024]{1,0:T(1,128)} %token_slots.1.slot_ref, bf16[1024,768]{1,0:T(8,128)(2,1)} %g_ref.1), custom_call_target="tpu_custom_call" | custom-call | flops 1 | bytes 1 | tf_op jit(solution)/shard_map/dispatch_0/pallas_call | solution.py:304
  15.8 3.0 collective-permute-start
  18.7 1.5 collective-permute-start.1
  20.2 2.0 collective-permute-start.4
  22.2 1.5 collective-permute-start.3
  24.9 32.2 %attend_forward.1 = (bf16[1024,768]{1,0:T(8,128)(2,1)}, bf16[1024,768]{1,0:T(8,128)(2,1)}, bf16[1024,768]{1,0:T(8,128)(2,1)}, bf16[1024,768]{1,0:T(8,128)(2,1)},...) custom-call(bf16[1024,768]{1,0:T(8,128)(2,1)} %x_ref.7, f32[1,768]{1,0:T(1,128)} %reshape.102.gain_ref, ...), custom_call_target="tpu_custom_call" | custom-call | flops 1 | bytes 1 | tf_op jit(solution)/shard_map/attend_forward/pallas_call | solution.py:140
  58.3 4.5 %collective-permute-done.5 = s32[1,8]{1,0:T(1,128)S(1)} collective-permute-done((s32[1,8]{1,0:T(1,128)S(1)}, s32[1,8]{1,0:T(1,128)S(1)}, u32[]{:S(2)}, u32[]{:S(2)}) %collective-permute-start.5) | collective-permute-done | bytes 64 | tf_op jit(solution)/shard_map/ppermute | solution.py:654
  63.4 7.0 %project.1 = (f32[1024,768]{1,0:T(8,128)}, bf16[1024,768]{1,0:T(8,128)(2,1)}) custom-call(bf16[1024,768]{1,0:T(8,128)(2,1)} %x_ref.7, bf16[1024,768]{1,0:T(8,128)(2,1)} %get-tuple-element.191.o_ref, bf16[768,768]{1,0:T(8,128)(2,1)} %wo_ref.3, f32[1,768]{1,0:T(1,128)} %reshape.104.gain_ref, f32[1,768]{1,0:T(1,128)} %reshape.105.bias_ref), custom_call_target="tpu_custom_call" | custom-call | flops 1 | bytes 1 | tf_op jit(solution)/shard_map/project/pallas_call | solution.py:241
  70.5 4.2 dispatch_0.3
  75.2 2.9 collective-permute-start.8
  78.1 4.2 dispatch_1.1
  82.9 4.0 collective-permute-done.6.refs_1_
  87.5 6.5 %collective-permute-done.7.refs_2_ = bf16[256,768]{1,0:T(8,128)(2,1)S(1)} collective-permute-done((bf16[256,768]{1,0:T(8,128)(2,1)}, bf16[256,768]{1,0:T(8,128)(2,1)S(1)}, u32[]{:S(2)}, u32[]{:S(2)}) %collective-permute-start.7) | collective-permute-done | bytes 393248 | tf_op jit(solution)/shard_map/ppermute | solution.py:654
  96.0 29.7 %expert_0.1 = (bf16[512,768]{1,0:T(8,128)(2,1)}, bf16[512,768]{1,0:T(8,128)(2,1)}, bf16[512,768]{1,0:T(8,128)(2,1)}, bf16[512,768]{1,0:T(8,128)(2,1)}, bf16[8,768,768]{2,1,0:T(8,128)(2,1)}) custom-call(s32[1,1]{1,0:T(1,128)} %bitcast.5.me_ref, s32[4,8]{1,0:T(4,128)} %pad_add_fusion.counts_ref, f32[8,768]{1,0:T(8,128)} %convert_bitcast_fusion.router_ref, ...), custom_call_target="tpu_custom_call" | custom-call | flops 1 | bytes 1 | tf_op jit(solution)/shard_map/expert_0/pallas_call | solution.py:474
  126.8 19.6 %collective-permute-start.9 = (bf16[512,768]{1,0:T(8,128)(2,1)}, bf16[512,768]{1,0:T(8,128)(2,1)S(1)}, u32[]{:S(2)}, u32[]{:S(2)}) collective-permute-start(bf16[512,768]{1,0:T(8,128)(2,1)} %get-tuple-element.210), channel_id=1, source_target_pairs={{0,1},{1,0},{2,3},{3,2},{4,5},{5,4},{6,7},{7,6},{8,9},{9,8},{10,11... | collective-permute-start | bytes 2359304 | tf_op jit(solution)/shard_map/ppermute | solution.py:654
  147.8 30.1 %expert_1.1 = (bf16[256,768]{1,0:T(8,128)(2,1)}, bf16[256,768]{1,0:T(8,128)(2,1)}, bf16[256,768]{1,0:T(8,128)(2,1)}, bf16[256,768]{1,0:T(8,128)(2,1)}, bf16[256,...) custom-call(s32[1,1]{1,0:T(1,128)} %bitcast.5.me_ref, ...), custom_call_target="tpu_custom_call" | custom-call | flops 1 | bytes 1 | tf_op jit(solution)/shard_map/expert_1/pallas_call | solution.py:474
  177.9 2.1 collective-permute-start.15
  182.8 4.8 %collect_0.2.dh0_ref = bf16[1024,768]{1,0:T(8,128)(2,1)} custom-call(s32[1,1024]{1,0:T(1,128)} %token_slots.1.slot_ref, bf16[512,768]{1,0:T(8,128)(2,1)} %get-tuple-element.226.refs_0_, bf16[512,768]{1,0:T(8,128)(2,1)} %copy-done.3, bf16[512,768]{1,0:T(8,128)(2,1)} %copy-done.4, bf16[512,768]{1,0:T(8,128)(2,1)} %copy-done.5), custom_call_target="tpu_custom_call" | custom-call | flops 1 | bytes 1 | tf_op jit(solution)/shard_map/collect_0/pallas_call | solution.py:331
  187.6 4.6 %collective-permute-done.16.refs_2_ = bf16[256,768]{1,0:T(8,128)(2,1)S(1)} collective-permute-done((bf16[256,768]{1,0:T(8,128)(2,1)}, bf16[256,768]{1,0:T(8,128)(2,1)S(1)}, u32[]{:S(2)}, u32[]{:S(2)}) %collective-permute-start.16) | collective-permute-done | bytes 393248 | tf_op jit(solution)/shard_map/ppermute | solution.py:654
  193.8 4.7 %collect_1.2.dh1_ref = bf16[1024,768]{1,0:T(8,128)(2,1)} custom-call(s32[1,1024]{1,0:T(1,128)} %token_slots.1.slot_ref, bf16[256,768]{1,0:T(8,128)(2,1)} %get-tuple-element.230.refs_0_, bf16[256,768]{1,0:T(8,128)(2,1)} %copy-done.20, bf16[256,768]{1,0:T(8,128)(2,1)} %copy-done.21, bf16[256,768]{1,0:T(8,128)(2,1)} %copy-done.22), custom_call_target="tpu_custom_call" | custom-call | flops 1 | bytes 1 | tf_op jit(solution)/shard_map/collect_1/pallas_call | solution.py:331
  198.5 10.9 %norm2_back.1 = (f32[1024,768]{1,0:T(8,128)}, bf16[1024,768]{1,0:T(8,128)(2,1)}, bf16[768,768]{1,0:T(8,128)(2,1)}, f32[2,768]{1,0:T(2,128)}) custom-call(bf16[1024,768]{1,0:T(8,128)(2,1)} %collect_0.2.dh0_ref, bf16[1024,768]{1,0:T(8,128)(2,1)} %collect_1.2.dh1_ref, f32[1024,768]{1,0:T(8,128)} %get-tuple-element.241.y_ref, bf16[1024,768]{1,0:T(8,128)(2,1)} %g_ref.1, ...), custom_call_target="tpu_custom_call" | custom-call | flops 1 | bytes 1 | tf_op jit(solution)/shard_map/norm2_back/pallas_call | solution.py:559
  210.2 2.8 collective-permute-start.21
  213.6 10.8 %attend_backward_0.1 = (bf16[1024,256]{1,0:T(8,128)(2,1)}, bf16[1024,256]{1,0:T(8,128)(2,1)}, bf16[1024,256]{1,0:T(8,128)(2,1)}) custom-call(bf16[1024,768]{1,0:T(8,128)(2,1)} %get-tuple-element.291.q_ref, bf16[1024,768]{1,0:T(8,128)(2,1)} %get-tuple-element.249.k_ref, bf16[1024,768]{1,0:T(8,128)(2,1)} %get-tuple-element.250.v_ref, ...), custom_call_target="tpu_custom_call" | custom-call | flops 1 | bytes 1 | tf_op jit(solution)/shard_map/attend_backward_0/pallas_call | solution.py:212
  224.5 5.0 %collective-permute-done.21.refs_3_ = bf16[256,768]{1,0:T(8,128)(2,1)S(1)} collective-permute-done((bf16[256,768]{1,0:T(8,128)(2,1)S(1)}, bf16[256,768]{1,0:T(8,128)(2,1)S(1)}, u32[]{:S(2)}, u32[]{:S(2)}) %collective-permute-start.21) | collective-permute-done | bytes 393248 | tf_op jit(solution)/shard_map/ppermute | solution.py:654
  230.5 2.5 add_cores.2
  233.1 1.7 collective-permute-start.22
  237.2 11.0 %attend_backward_1.1 = (bf16[1024,256]{1,0:T(8,128)(2,1)}, bf16[1024,256]{1,0:T(8,128)(2,1)}, bf16[1024,256]{1,0:T(8,128)(2,1)}) custom-call(bf16[1024,768]{1,0:T(8,128)(2,1)} %get-tuple-element.291.q_ref, bf16[1024,768]{1,0:T(8,128)(2,1)} %get-tuple-element.249.k_ref, bf16[1024,768]{1,0:T(8,128)(2,1)} %get-tuple-element.250.v_ref, ...), custom_call_target="tpu_custom_call" | custom-call | flops 1 | bytes 1 | tf_op jit(solution)/shard_map/attend_backward_1/pallas_call | solution.py:212
  249.0 1.8 add_groups.2
  250.8 9.9 %collective-permute-start.25 = (bf16[24,768]{1,0:T(8,128)(2,1)}, bf16[24,768]{1,0:T(8,128)(2,1)S(1)}, u32[]{:S(2)}, u32[]{:S(2)}) collective-permute-start(bf16[24,768]{1,0:T(8,128)(2,1)} %get-tuple-element.284), channel_id=1, source_target_pairs={{0,8},{4,12},{8,0},{12,4},{16,24},{20,28},{24,16},{28,20},{1,9},{5... | collective-permute-start | bytes 110600 | tf_op jit(solution)/shard_map/ppermute | solution.py:654
  260.7 9.7 %collective-permute-start.26 = (bf16[24,768]{1,0:T(8,128)(2,1)}, bf16[24,768]{1,0:T(8,128)(2,1)S(1)}, u32[]{:S(2)}, u32[]{:S(2)}) collective-permute-start(bf16[24,768]{1,0:T(8,128)(2,1)} %get-tuple-element.285), channel_id=1, source_target_pairs={{0,16},{4,20},{8,24},{12,28},{16,0},{20,4},{24,8},{28,12},{1,17},{... | collective-permute-start | bytes 110600 | tf_op jit(solution)/shard_map/ppermute | solution.py:654
  271.9 10.9 %attend_backward_2.1 = (bf16[1024,256]{1,0:T(8,128)(2,1)}, bf16[1024,256]{1,0:T(8,128)(2,1)}, bf16[1024,256]{1,0:T(8,128)(2,1)}) custom-call(bf16[1024,768]{1,0:T(8,128)(2,1)} %get-tuple-element.291.q_ref, bf16[1024,768]{1,0:T(8,128)(2,1)} %get-tuple-element.249.k_ref, bf16[1024,768]{1,0:T(8,128)(2,1)} %get-tuple-element.250.v_ref, ...), custom_call_target="tpu_custom_call" | custom-call | flops 1 | bytes 1 | tf_op jit(solution)/shard_map/attend_backward_2/pallas_call | solution.py:212
  283.4 1.5 add_parts.2.refs_0_
  284.9 15.5 %norm1_back.1 = (bf16[1024,768]{1,0:T(8,128)(2,1)}, bf16[2560,768]{1,0:T(8,128)(2,1)}) custom-call(bf16[1024,768]{1,0:T(8,128)(2,1)} %get-tuple-element.307.attn_in_ref, bf16[1024,768]{1,0:T(8,128)(2,1)} %x_ref.7, f32[1024,768]{1,0:T(8,128)} %get-tuple-element.308.dy_ref, bf16[768,768]{1,0:T(8,128)(2,1)} %wq_ref.3, bf16[768,768]{1,0:T(8,128)(2,1)} %wk_ref.3, ...), custom_call_target="tpu_custom_call" | custom-call | flops 1 | bytes 1 | tf_op jit(solution)/shard_map/norm1_back/pallas_call | solution.py:638
  300.5 2.5 collective-permute-start.31
  303.0 2.0 collective-permute-start.29
  304.9 2.6 collective-permute-done.31.refs_3_
  307.5 2.4 collective-permute-done.30.refs_2_
  309.9 5.0 %add_cores.3 = (bf16[320,768]{1,0:T(8,128)(2,1)}, bf16[320,768]{1,0:T(8,128)(2,1)}, bf16[320,768]{1,0:T(8,128)(2,1)}, bf16[320,768]{1,0:T(8,128)(2,1)}) custom-call(s32[1,2]{1,0:T(1,128)} %add_bitcast_fusion.me_ref, bf16[8,320,768]{2,1,0:T(8,128)(2,1)} %bitcast.27, bf16[8,320,768]{2,1,0:T(8,128)(2,1)} %bitcast.15.refs_1_), custom_call_target="tpu_custom_call" | custom-call | flops 1 | bytes 1 | tf_op jit(solution)/shard_map/add_cores/pallas_call | solution.py:671
  318.4 1.5 line_up.2
  320.0 1.8 collective-permute-start.37
  322.7 19.8 %collective-permute-done.37.refs_3_ = bf16[96,768]{1,0:T(8,128)(2,1)S(1)} collective-permute-done((bf16[96,768]{1,0:T(8,128)(2,1)}, bf16[96,768]{1,0:T(8,128)(2,1)S(1)}, u32[]{:S(2)}, u32[]{:S(2)}) %collective-permute-start.37) | collective-permute-done | bytes 147488 | tf_op jit(solution)/shard_map/ppermute | solution.py:654
  343.9 4.8 %collect_0.3.z0_ref = bf16[1024,768]{1,0:T(8,128)(2,1)} custom-call(s32[1,1024]{1,0:T(1,128)} %token_slots.1.slot_ref, bf16[512,768]{1,0:T(8,128)(2,1)} %get-tuple-element.226.refs_0_, bf16[512,768]{1,0:T(8,128)(2,1)} %copy-done.3, bf16[512,768]{1,0:T(8,128)(2,1)} %copy-done.4, bf16[512,768]{1,0:T(8,128)(2,1)} %copy-done.5), custom_call_target="tpu_custom_call" | custom-call | flops 1 | bytes 1 | tf_op jit(solution)/shard_map/collect_0/pallas_call | solution.py:331
  348.6 4.7 %collect_1.3.z1_ref = bf16[1024,768]{1,0:T(8,128)(2,1)} custom-call(s32[1,1024]{1,0:T(1,128)} %token_slots.1.slot_ref, bf16[256,768]{1,0:T(8,128)(2,1)} %get-tuple-element.330.refs_0_, bf16[256,768]{1,0:T(8,128)(2,1)} %copy-done.17, bf16[256,768]{1,0:T(8,128)(2,1)} %copy-done.18, bf16[256,768]{1,0:T(8,128)(2,1)} %copy-done.19), custom_call_target="tpu_custom_call" | custom-call | flops 1 | bytes 1 | tf_op jit(solution)/shard_map/collect_1/pallas_call | solution.py:331
  353.4 4.5 %block_result.1 = bf16[1024,768]{1,0:T(8,128)(2,1)} custom-call(f32[1024,768]{1,0:T(8,128)} %get-tuple-element.241.y_ref, bf16[1024,768]{1,0:T(8,128)(2,1)} %collect_0.3.z0_ref, bf16[1024,768]{1,0:T(8,128)(2,1)} %collect_1.3.z1_ref), custom_call_target="tpu_custom_call" | custom-call | flops 1 | bytes 1 | tf_op jit(solution)/shard_map/block_result/pallas_call | solution.py:582
  359.1 2.4 add_groups.3
  362.6 2.0 collective-permute-start.39
  365.9 1.5 collective-permute-done.38.refs_1_
  367.4 6.5 %collective-permute-done.39.refs_2_ = bf16[80,768]{1,0:T(8,128)(2,1)S(1)} collective-permute-done((bf16[80,768]{1,0:T(8,128)(2,1)}, bf16[80,768]{1,0:T(8,128)(2,1)S(1)}, u32[]{:S(2)}, u32[]{:S(2)}) %collective-permute-start.39) | collective-permute-done | bytes 122912 | tf_op jit(solution)/shard_map/ppermute | solution.py:654
  374.6 1.8 add_parts.3.refs_0_
  376.4 1.7 collective-permute-start.43
  378.1 1.7 collective-permute-start.42
  380.8 3.5 collective-permute-done.43.refs_3_
  384.3 4.3 collective-permute-done.42.refs_2_
  389.9 1.9 line_up.3
  392.4 1.5 collective-permute-start.45
  395.8 11.2 %collective-permute-done.46.refs_3_ = bf16[320,768]{1,0:T(8,128)(2,1)S(1)} collective-permute-done((bf16[320,768]{1,0:T(8,128)(2,1)}, bf16[320,768]{1,0:T(8,128)(2,1)S(1)}, u32[]{:S(2)}, u32[]{:S(2)}) %collective-permute-start.46) | collective-permute-done | bytes 491552 | tf_op jit(solution)/shard_map/ppermute | solution.py:654
  407.0 7.8 %collective-permute-done.45.refs_2_ = bf16[320,768]{1,0:T(8,128)(2,1)S(1)} collective-permute-done((bf16[320,768]{1,0:T(8,128)(2,1)}, bf16[320,768]{1,0:T(8,128)(2,1)S(1)}, u32[]{:S(2)}, u32[]{:S(2)}) %collective-permute-start.45) | collective-permute-done | bytes 491552 | tf_op jit(solution)/shard_map/ppermute | solution.py:654
  415.5 2.1 collective-permute-done.52.refs_5_
  420.5 3.0 finish.3
  424.7 5.4 %finish.2 = (f32[768,768]{1,0:T(8,128)}, f32[768,768]{1,0:T(8,128)}, f32[768,768]{1,0:T(8,128)}, f32[8,768]{1,0:T(8,128)}) custom-call(s32[1,2]{1,0:T(1,128)} %add_bitcast_fusion.me_ref, bf16[320,768]{1,0:T(8,128)(2,1)} %bitcast.32, bf16[320,768]{1,0:T(8,128)(2,1)} %copy-done.10, bf16[320,768]{1,0:T(8,128)(2,1)} %copy-done.9, bf16[320,768]{1,0:T(8,128)(2,1)} %copy-done.8, ...), custom_call_target="tpu_custom_call" | custom-call | flops 1 | bytes 1 | tf_op jit(solution)/shard_map/finish/pallas_call | solution.py:750
  430.1 1.5 slice_reduce_fusion
  431.6 2.8 unpack_shares.2
  434.4 2.8 unpack_shares.3
  (211 shorter events, 41.0 us)
Async XLA Ops:
  7.2 424.4 %reduce-scatter.5.cloned.1.call-start = ((), (), s32[]{:S(2)}) async-start(), calls=%async_computation.3 | async-start | bytes 10616832 | tf_op jit(solution)/shard_map/reduce_scatter | solution.py:834
  15.8 47.6 %collective-permute-start = (bf16[512,768]{1,0:T(8,128)(2,1)}, bf16[512,768]{1,0:T(8,128)(2,1)S(1)}, u32[]{:S(2)}, u32[]{:S(2)}) collective-permute-start(bf16[512,768]{1,0:T(8,128)(2,1)} %get-tuple-element.187), channel_id=1, source_target_pairs={{0,1},{1,0},{2,3},{3,2},{4,5},{5,4},{6,7},{7,6},{8,9},{9,8},{10,11... | collective-permute-start | bytes 2359304 | tf_op jit(solution)/shard_map/ppermute | solution.py:654
  18.7 44.6 %collective-permute-start.1 = (bf16[512,768]{1,0:T(8,128)(2,1)}, bf16[512,768]{1,0:T(8,128)(2,1)S(1)}, u32[]{:S(2)}, u32[]{:S(2)}) collective-permute-start(bf16[512,768]{1,0:T(8,128)(2,1)} %get-tuple-element.188), channel_id=1, source_target_pairs={{0,2},{1,3},{2,0},{3,1},{4,6},{5,7},{6,4},{7,5},{8,10},{9,11},{10,... | collective-permute-start | bytes 2359304 | tf_op jit(solution)/shard_map/ppermute | solution.py:654
  20.2 43.1 %collective-permute-start.2 = (bf16[512,768]{1,0:T(8,128)(2,1)}, bf16[512,768]{1,0:T(8,128)(2,1)S(1)}, u32[]{:S(2)}, u32[]{:S(2)}) collective-permute-start(bf16[512,768]{1,0:T(8,128)(2,1)} %get-tuple-element.189), channel_id=1, source_target_pairs={{0,3},{1,2},{2,1},{3,0},{4,7},{5,6},{6,5},{7,4},{8,11},{9,10},{10,... | collective-permute-start | bytes 2359304 | tf_op jit(solution)/shard_map/ppermute | solution.py:654
  20.2 38.0 %collective-permute-start.4 = (s32[1,8]{1,0:T(1,128)S(1)}, s32[1,8]{1,0:T(1,128)S(1)}, u32[]{:S(2)}, u32[]{:S(2)}) collective-permute-start(s32[1,8]{1,0:T(1,128)S(1)} %copy-done.56), channel_id=1, source_target_pairs={{0,2},{1,3},{2,0},{3,1},{4,6},{5,7},{6,4},{7,5},{8,10},{9,11},{10,... | collective-permute-start | bytes 104 | tf_op jit(solution)/shard_map/ppermute | solution.py:654
  22.2 36.1 %collective-permute-start.3 = (s32[1,8]{1,0:T(1,128)S(1)}, s32[1,8]{1,0:T(1,128)S(1)}, u32[]{:S(2)}, u32[]{:S(2)}) collective-permute-start(s32[1,8]{1,0:T(1,128)S(1)} %copy-done.56), channel_id=1, source_target_pairs={{0,1},{1,0},{2,3},{3,2},{4,5},{5,4},{6,7},{7,6},{8,9},{9,8},{10,11... | collective-permute-start | bytes 104 | tf_op jit(solution)/shard_map/ppermute | solution.py:654
  58.3 4.5 %collective-permute-start.5 = (s32[1,8]{1,0:T(1,128)S(1)}, s32[1,8]{1,0:T(1,128)S(1)}, u32[]{:S(2)}, u32[]{:S(2)}) collective-permute-start(s32[1,8]{1,0:T(1,128)S(1)} %copy-done.56), channel_id=1, source_target_pairs={{0,3},{1,2},{2,1},{3,0},{4,7},{5,6},{6,5},{7,4},{8,11},{9,10},{10,... | collective-permute-start | bytes 104 | tf_op jit(solution)/shard_map/ppermute | solution.py:654
  74.6 12.2 %collective-permute-start.6 = (bf16[256,768]{1,0:T(8,128)(2,1)}, bf16[256,768]{1,0:T(8,128)(2,1)S(1)}, u32[]{:S(2)}, u32[]{:S(2)}) collective-permute-start(bf16[256,768]{1,0:T(8,128)(2,1)} %get-tuple-element.194), channel_id=1, source_target_pairs={{0,1},{1,0},{2,3},{3,2},{4,5},{5,4},{6,7},{7,6},{8,9},{9,8},{10,11... | collective-permute-start | bytes 1179656 | tf_op jit(solution)/shard_map/ppermute | solution.py:654
  75.2 18.9 %collective-permute-start.7 = (bf16[256,768]{1,0:T(8,128)(2,1)}, bf16[256,768]{1,0:T(8,128)(2,1)S(1)}, u32[]{:S(2)}, u32[]{:S(2)}) collective-permute-start(bf16[256,768]{1,0:T(8,128)(2,1)} %get-tuple-element.195), channel_id=1, source_target_pairs={{0,2},{1,3},{2,0},{3,1},{4,6},{5,7},{6,4},{7,5},{8,10},{9,11},{10,... | collective-permute-start | bytes 1179656 | tf_op jit(solution)/shard_map/ppermute | solution.py:654
  75.2 20.0 %collective-permute-start.8 = (bf16[256,768]{1,0:T(8,128)(2,1)}, bf16[256,768]{1,0:T(8,128)(2,1)S(1)}, u32[]{:S(2)}, u32[]{:S(2)}) collective-permute-start(bf16[256,768]{1,0:T(8,128)(2,1)} %get-tuple-element.196), channel_id=1, source_target_pairs={{0,3},{1,2},{2,1},{3,0},{4,7},{5,6},{6,5},{7,4},{8,11},{9,10},{10,... | collective-permute-start | bytes 1179656 | tf_op jit(solution)/shard_map/ppermute | solution.py:654
  82.3 43.5 %collective-permute-start.12 = (bf16[256,768]{1,0:T(8,128)(2,1)}, bf16[256,768]{1,0:T(8,128)(2,1)S(1)}, u32[]{:S(2)}, u32[]{:S(2)}) collective-permute-start(bf16[256,768]{1,0:T(8,128)(2,1)} %get-tuple-element.198), channel_id=1, source_target_pairs={{0,1},{1,0},{2,3},{3,2},{4,5},{5,4},{6,7},{7,6},{8,9},{9,8},{10,11... | collective-permute-start | bytes 1179656 | tf_op jit(solution)/shard_map/ppermute | solution.py:654
  82.8 43.0 %collective-permute-start.13 = (bf16[256,768]{1,0:T(8,128)(2,1)}, bf16[256,768]{1,0:T(8,128)(2,1)S(1)}, u32[]{:S(2)}, u32[]{:S(2)}) collective-permute-start(bf16[256,768]{1,0:T(8,128)(2,1)} %get-tuple-element.199), channel_id=1, source_target_pairs={{0,2},{1,3},{2,0},{3,1},{4,6},{5,7},{6,4},{7,5},{8,10},{9,11},{10,... | collective-permute-start | bytes 1179656 | tf_op jit(solution)/shard_map/ppermute | solution.py:654
  86.8 39.0 %collective-permute-start.14 = (bf16[256,768]{1,0:T(8,128)(2,1)}, bf16[256,768]{1,0:T(8,128)(2,1)S(1)}, u32[]{:S(2)}, u32[]{:S(2)}) collective-permute-start(bf16[256,768]{1,0:T(8,128)(2,1)} %get-tuple-element.200), channel_id=1, source_target_pairs={{0,3},{1,2},{2,1},{3,0},{4,7},{5,6},{6,5},{7,4},{8,11},{9,10},{10,... | collective-permute-start | bytes 1179656 | tf_op jit(solution)/shard_map/ppermute | solution.py:654
  126.8 307.6 %reduce-scatter.3.cloned.1.call-start = ((), (), s32[]{:S(2)}) async-start(), calls=%async_computation.2 | async-start | bytes 10616832 | tf_op jit(solution)/shard_map/reduce_scatter | solution.py:834
  126.8 53.8 %collective-permute-start.9 = (bf16[512,768]{1,0:T(8,128)(2,1)}, bf16[512,768]{1,0:T(8,128)(2,1)S(1)}, u32[]{:S(2)}, u32[]{:S(2)}) collective-permute-start(bf16[512,768]{1,0:T(8,128)(2,1)} %get-tuple-element.210), channel_id=1, source_target_pairs={{0,1},{1,0},{2,3},{3,2},{4,5},{5,4},{6,7},{7,6},{8,9},{9,8},{10,11... | collective-permute-start | bytes 2359304 | tf_op jit(solution)/shard_map/ppermute | solution.py:654
  146.4 35.2 %collective-permute-start.10 = (bf16[512,768]{1,0:T(8,128)(2,1)}, bf16[512,768]{1,0:T(8,128)(2,1)S(1)}, u32[]{:S(2)}, u32[]{:S(2)}) collective-permute-start(bf16[512,768]{1,0:T(8,128)(2,1)} %get-tuple-element.211), channel_id=1, source_target_pairs={{0,2},{1,3},{2,0},{3,1},{4,6},{5,7},{6,4},{7,5},{8,10},{9,11},{10,... | collective-permute-start | bytes 2359304 | tf_op jit(solution)/shard_map/ppermute | solution.py:654
  147.0 34.6 %collective-permute-start.11 = (bf16[512,768]{1,0:T(8,128)(2,1)}, bf16[512,768]{1,0:T(8,128)(2,1)S(1)}, u32[]{:S(2)}, u32[]{:S(2)}) collective-permute-start(bf16[512,768]{1,0:T(8,128)(2,1)} %get-tuple-element.212), channel_id=1, source_target_pairs={{0,3},{1,2},{2,1},{3,0},{4,7},{5,6},{6,5},{7,4},{8,11},{9,10},{10,... | collective-permute-start | bytes 2359304 | tf_op jit(solution)/shard_map/ppermute | solution.py:654
  177.9 9.7 %collective-permute-start.15 = (bf16[256,768]{1,0:T(8,128)(2,1)}, bf16[256,768]{1,0:T(8,128)(2,1)S(1)}, u32[]{:S(2)}, u32[]{:S(2)}) collective-permute-start(bf16[256,768]{1,0:T(8,128)(2,1)} %get-tuple-element.223), channel_id=1, source_target_pairs={{0,1},{1,0},{2,3},{3,2},{4,5},{5,4},{6,7},{7,6},{8,9},{9,8},{10,11... | collective-permute-start | bytes 1179656 | tf_op jit(solution)/shard_map/ppermute | solution.py:654
  180.0 12.2 %collective-permute-start.16 = (bf16[256,768]{1,0:T(8,128)(2,1)}, bf16[256,768]{1,0:T(8,128)(2,1)S(1)}, u32[]{:S(2)}, u32[]{:S(2)}) collective-permute-start(bf16[256,768]{1,0:T(8,128)(2,1)} %get-tuple-element.224), channel_id=1, source_target_pairs={{0,2},{1,3},{2,0},{3,1},{4,6},{5,7},{6,4},{7,5},{8,10},{9,11},{10,... | collective-permute-start | bytes 1179656 | tf_op jit(solution)/shard_map/ppermute | solution.py:654
  180.6 11.7 %collective-permute-start.17 = (bf16[256,768]{1,0:T(8,128)(2,1)}, bf16[256,768]{1,0:T(8,128)(2,1)S(1)}, u32[]{:S(2)}, u32[]{:S(2)}) collective-permute-start(bf16[256,768]{1,0:T(8,128)(2,1)} %get-tuple-element.225), channel_id=1, source_target_pairs={{0,3},{1,2},{2,1},{3,0},{4,7},{5,6},{6,5},{7,4},{8,11},{9,10},{10,... | collective-permute-start | bytes 1179656 | tf_op jit(solution)/shard_map/ppermute | solution.py:654
  209.4 20.1 %collective-permute-start.18 = (bf16[768,768]{1,0:T(8,128)(2,1)}, bf16[768,768]{1,0:T(8,128)(2,1)S(1)}, u32[]{:S(2)}, u32[]{:S(2)}) collective-permute-start(bf16[768,768]{1,0:T(8,128)(2,1)} %get-tuple-element.242), channel_id=1, source_target_pairs={{0,4},{4,0},{8,12},{12,8},{16,20},{20,16},{24,28},{28,24},{1,5},{5... | collective-permute-start | bytes 3538952 | tf_op jit(solution)/shard_map/ppermute | solution.py:654
  209.5 14.9 %collective-permute-start.19 = (bf16[256,768]{1,0:T(8,128)(2,1)S(1)}, bf16[256,768]{1,0:T(8,128)(2,1)S(1)}, u32[]{:S(2)}, u32[]{:S(2)}) collective-permute-start(bf16[256,768]{1,0:T(8,128)(2,1)S(1)} %copy-done.59), channel_id=1, source_target_pairs={{0,1},{1,0},{2,3},{3,2},{4,5},{5,4},{6,7},{7,6},{8,9},{9,8},{10,11... | collective-permute-start | bytes 1179656 | tf_op jit(solution)/shard_map/ppermute | solution.py:654
  209.6 14.9 %collective-permute-start.20 = (bf16[256,768]{1,0:T(8,128)(2,1)S(1)}, bf16[256,768]{1,0:T(8,128)(2,1)S(1)}, u32[]{:S(2)}, u32[]{:S(2)}) collective-permute-start(bf16[256,768]{1,0:T(8,128)(2,1)S(1)} %copy-done.58), channel_id=1, source_target_pairs={{0,2},{1,3},{2,0},{3,1},{4,6},{5,7},{6,4},{7,5},{8,10},{9,11},{10,... | collective-permute-start | bytes 1179656 | tf_op jit(solution)/shard_map/ppermute | solution.py:654
  210.2 19.3 %collective-permute-start.21 = (bf16[256,768]{1,0:T(8,128)(2,1)S(1)}, bf16[256,768]{1,0:T(8,128)(2,1)S(1)}, u32[]{:S(2)}, u32[]{:S(2)}) collective-permute-start(bf16[256,768]{1,0:T(8,128)(2,1)S(1)} %copy-done.57), channel_id=1, source_target_pairs={{0,3},{1,2},{2,1},{3,0},{4,7},{5,6},{6,5},{7,4},{8,11},{9,10},{10,... | collective-permute-start | bytes 1179656 | tf_op jit(solution)/shard_map/ppermute | solution.py:654
  224.4 58.3 %copy-start.17 = (bf16[256,768]{1,0:T(8,128)(2,1)}, bf16[256,768]{1,0:T(8,128)(2,1)S(1)}, u32[]{:S(2)}) copy-start(bf16[256,768]{1,0:T(8,128)(2,1)S(1)} %collective-permute-done.19.refs_1_) | copy-start | bytes 1179652
  224.4 58.3 %copy-start.18 = (bf16[256,768]{1,0:T(8,128)(2,1)}, bf16[256,768]{1,0:T(8,128)(2,1)S(1)}, u32[]{:S(2)}) copy-start(bf16[256,768]{1,0:T(8,128)(2,1)S(1)} %collective-permute-done.20.refs_2_) | copy-start | bytes 1179652
  229.5 53.2 %copy-start.19 = (bf16[256,768]{1,0:T(8,128)(2,1)}, bf16[256,768]{1,0:T(8,128)(2,1)S(1)}, u32[]{:S(2)}) copy-start(bf16[256,768]{1,0:T(8,128)(2,1)S(1)} %collective-permute-done.21.refs_3_) | copy-start | bytes 1179652
  233.1 15.1 %collective-permute-start.22 = (bf16[96,768]{1,0:T(8,128)(2,1)}, bf16[96,768]{1,0:T(8,128)(2,1)S(1)}, u32[]{:S(2)}, u32[]{:S(2)}) collective-permute-start(bf16[96,768]{1,0:T(8,128)(2,1)} %get-tuple-element.261), channel_id=1, source_target_pairs={{0,1},{1,0},{2,3},{3,2},{4,5},{5,4},{6,7},{7,6},{8,9},{9,8},{10,11... | collective-permute-start | bytes 442376 | tf_op jit(solution)/shard_map/ppermute | solution.py:654
  234.7 13.5 %collective-permute-start.23 = (bf16[96,768]{1,0:T(8,128)(2,1)}, bf16[96,768]{1,0:T(8,128)(2,1)S(1)}, u32[]{:S(2)}, u32[]{:S(2)}) collective-permute-start(bf16[96,768]{1,0:T(8,128)(2,1)} %get-tuple-element.262), channel_id=1, source_target_pairs={{0,2},{1,3},{2,0},{3,1},{4,6},{5,7},{6,4},{7,5},{8,10},{9,11},{10,... | collective-permute-start | bytes 442376 | tf_op jit(solution)/shard_map/ppermute | solution.py:654
  235.3 12.9 %collective-permute-start.24 = (bf16[96,768]{1,0:T(8,128)(2,1)}, bf16[96,768]{1,0:T(8,128)(2,1)S(1)}, u32[]{:S(2)}, u32[]{:S(2)}) collective-permute-start(bf16[96,768]{1,0:T(8,128)(2,1)} %get-tuple-element.263), channel_id=1, source_target_pairs={{0,3},{1,2},{2,1},{3,0},{4,7},{5,6},{6,5},{7,4},{8,11},{9,10},{10,... | collective-permute-start | bytes 442376 | tf_op jit(solution)/shard_map/ppermute | solution.py:654
  250.8 32.0 %collective-permute-start.25 = (bf16[24,768]{1,0:T(8,128)(2,1)}, bf16[24,768]{1,0:T(8,128)(2,1)S(1)}, u32[]{:S(2)}, u32[]{:S(2)}) collective-permute-start(bf16[24,768]{1,0:T(8,128)(2,1)} %get-tuple-element.284), channel_id=1, source_target_pairs={{0,8},{4,12},{8,0},{12,4},{16,24},{20,28},{24,16},{28,20},{1,9},{5... | collective-permute-start | bytes 110600 | tf_op jit(solution)/shard_map/ppermute | solution.py:654
  260.7 22.0 %collective-permute-start.26 = (bf16[24,768]{1,0:T(8,128)(2,1)}, bf16[24,768]{1,0:T(8,128)(2,1)S(1)}, u32[]{:S(2)}, u32[]{:S(2)}) collective-permute-start(bf16[24,768]{1,0:T(8,128)(2,1)} %get-tuple-element.285), channel_id=1, source_target_pairs={{0,16},{4,20},{8,24},{12,28},{16,0},{20,4},{24,8},{28,12},{1,17},{... | collective-permute-start | bytes 110600 | tf_op jit(solution)/shard_map/ppermute | solution.py:654
  270.4 12.4 %collective-permute-start.27 = (bf16[24,768]{1,0:T(8,128)(2,1)}, bf16[24,768]{1,0:T(8,128)(2,1)S(1)}, u32[]{:S(2)}, u32[]{:S(2)}) collective-permute-start(bf16[24,768]{1,0:T(8,128)(2,1)} %get-tuple-element.286), channel_id=1, source_target_pairs={{0,24},{4,28},{8,16},{12,20},{16,8},{20,12},{24,0},{28,4},{1,25},{... | collective-permute-start | bytes 110600 | tf_op jit(solution)/shard_map/ppermute | solution.py:654
  300.4 9.5 %collective-permute-start.28 = (bf16[2560,768]{1,0:T(8,128)(2,1)}, bf16[2560,768]{1,0:T(8,128)(2,1)}, u32[]{:S(2)}, u32[]{:S(2)}) collective-permute-start(bf16[2560,768]{1,0:T(8,128)(2,1)} %get-tuple-element.319), channel_id=1, source_target_pairs={{0,4},{4,0},{8,12},{12,8},{16,20},{20,16},{24,28},{28,24},{1,5},{5... | collective-permute-start | bytes 11796488 | tf_op jit(solution)/shard_map/ppermute | solution.py:654
  300.5 7.0 %collective-permute-start.31 = (bf16[24,768]{1,0:T(8,128)(2,1)S(1)}, bf16[24,768]{1,0:T(8,128)(2,1)S(1)}, u32[]{:S(2)}, u32[]{:S(2)}) collective-permute-start(bf16[24,768]{1,0:T(8,128)(2,1)S(1)} %copy-done.29), channel_id=1, source_target_pairs={{0,24},{4,28},{8,16},{12,20},{16,8},{20,12},{24,0},{28,4},{1,25},{... | collective-permute-start | bytes 110600 | tf_op jit(solution)/shard_map/ppermute | solution.py:654
  303.0 6.9 %collective-permute-start.30 = (bf16[24,768]{1,0:T(8,128)(2,1)S(1)}, bf16[24,768]{1,0:T(8,128)(2,1)S(1)}, u32[]{:S(2)}, u32[]{:S(2)}) collective-permute-start(bf16[24,768]{1,0:T(8,128)(2,1)S(1)} %copy-done.29), channel_id=1, source_target_pairs={{0,16},{4,20},{8,24},{12,28},{16,0},{20,4},{24,8},{28,12},{1,17},{... | collective-permute-start | bytes 110600 | tf_op jit(solution)/shard_map/ppermute | solution.py:654
  303.0 6.9 %collective-permute-start.29 = (bf16[24,768]{1,0:T(8,128)(2,1)S(1)}, bf16[24,768]{1,0:T(8,128)(2,1)S(1)}, u32[]{:S(2)}, u32[]{:S(2)}) collective-permute-start(bf16[24,768]{1,0:T(8,128)(2,1)S(1)} %copy-done.29), channel_id=1, source_target_pairs={{0,8},{4,12},{8,0},{12,4},{16,24},{20,28},{24,16},{28,20},{1,9},{5... | collective-permute-start | bytes 110600 | tf_op jit(solution)/shard_map/ppermute | solution.py:654
  314.9 43.0 %collective-permute-start.32 = (bf16[320,768]{1,0:T(8,128)(2,1)}, bf16[320,768]{1,0:T(8,128)(2,1)S(1)}, u32[]{:S(2)}, u32[]{:S(2)}) collective-permute-start(bf16[320,768]{1,0:T(8,128)(2,1)} %get-tuple-element.323), channel_id=1, source_target_pairs={{0,1},{1,0},{2,3},{3,2},{4,5},{5,4},{6,7},{7,6},{8,9},{9,8},{10,11... | collective-permute-start | bytes 1474568 | tf_op jit(solution)/shard_map/ppermute | solution.py:654
  316.2 41.7 %collective-permute-start.33 = (bf16[320,768]{1,0:T(8,128)(2,1)}, bf16[320,768]{1,0:T(8,128)(2,1)S(1)}, u32[]{:S(2)}, u32[]{:S(2)}) collective-permute-start(bf16[320,768]{1,0:T(8,128)(2,1)} %get-tuple-element.324), channel_id=1, source_target_pairs={{0,2},{1,3},{2,0},{3,1},{4,6},{5,7},{6,4},{7,5},{8,10},{9,11},{10,... | collective-permute-start | bytes 1474568 | tf_op jit(solution)/shard_map/ppermute | solution.py:654
  317.3 40.6 %collective-permute-start.34 = (bf16[320,768]{1,0:T(8,128)(2,1)}, bf16[320,768]{1,0:T(8,128)(2,1)S(1)}, u32[]{:S(2)}, u32[]{:S(2)}) collective-permute-start(bf16[320,768]{1,0:T(8,128)(2,1)} %get-tuple-element.325), channel_id=1, source_target_pairs={{0,3},{1,2},{2,1},{3,0},{4,7},{5,6},{6,5},{7,4},{8,11},{9,10},{10,... | collective-permute-start | bytes 1474568 | tf_op jit(solution)/shard_map/ppermute | solution.py:654
  320.0 22.5 %collective-permute-start.37 = (bf16[96,768]{1,0:T(8,128)(2,1)}, bf16[96,768]{1,0:T(8,128)(2,1)S(1)}, u32[]{:S(2)}, u32[]{:S(2)}) collective-permute-start(bf16[96,768]{1,0:T(8,128)(2,1)} %bitcast.37), channel_id=1, source_target_pairs={{0,3},{1,2},{2,1},{3,0},{4,7},{5,6},{6,5},{7,4},{8,11},{9,10},{10,... | collective-permute-start | bytes 442376 | tf_op jit(solution)/shard_map/ppermute | solution.py:654
  321.8 36.1 %collective-permute-start.36 = (bf16[96,768]{1,0:T(8,128)(2,1)}, bf16[96,768]{1,0:T(8,128)(2,1)S(1)}, u32[]{:S(2)}, u32[]{:S(2)}) collective-permute-start(bf16[96,768]{1,0:T(8,128)(2,1)} %bitcast.38), channel_id=1, source_target_pairs={{0,2},{1,3},{2,0},{3,1},{4,6},{5,7},{6,4},{7,5},{8,10},{9,11},{10,... | collective-permute-start | bytes 442376 | tf_op jit(solution)/shard_map/ppermute | solution.py:654
  342.5 76.4 %copy-start.33 = (bf16[96,768]{1,0:T(8,128)(2,1)}, bf16[96,768]{1,0:T(8,128)(2,1)S(1)}, u32[]{:S(2)}) copy-start(bf16[96,768]{1,0:T(8,128)(2,1)S(1)} %collective-permute-done.37.refs_3_) | copy-start | bytes 442372
  342.5 15.4 %collective-permute-start.35 = (bf16[96,768]{1,0:T(8,128)(2,1)}, bf16[96,768]{1,0:T(8,128)(2,1)S(1)}, u32[]{:S(2)}, u32[]{:S(2)}) collective-permute-start(bf16[96,768]{1,0:T(8,128)(2,1)} %bitcast.39), channel_id=1, source_target_pairs={{0,1},{1,0},{2,3},{3,2},{4,5},{5,4},{6,7},{7,6},{8,9},{9,8},{10,11... | collective-permute-start | bytes 442376 | tf_op jit(solution)/shard_map/ppermute | solution.py:654
  357.9 62.5 %copy-start.34 = (bf16[96,768]{1,0:T(8,128)(2,1)}, bf16[96,768]{1,0:T(8,128)(2,1)S(1)}, u32[]{:S(2)}) copy-start(bf16[96,768]{1,0:T(8,128)(2,1)S(1)} %collective-permute-done.36.refs_2_) | copy-start | bytes 442372
  357.9 62.5 %copy-start.35 = (bf16[96,768]{1,0:T(8,128)(2,1)}, bf16[96,768]{1,0:T(8,128)(2,1)S(1)}, u32[]{:S(2)}) copy-start(bf16[96,768]{1,0:T(8,128)(2,1)S(1)} %collective-permute-done.35.refs_1_) | copy-start | bytes 442372
  359.1 36.2 %copy-start.7 = (bf16[4,24,768]{2,1,0:T(8,128)(2,1)S(1)}, bf16[4,24,768]{2,1,0:T(8,128)(2,1)}, u32[]{:S(2)}) copy-start(bf16[4,24,768]{2,1,0:T(8,128)(2,1)} %line_up.2) | copy-start | bytes 442372
  361.5 5.9 %collective-permute-start.38 = (bf16[80,768]{1,0:T(8,128)(2,1)}, bf16[80,768]{1,0:T(8,128)(2,1)S(1)}, u32[]{:S(2)}, u32[]{:S(2)}) collective-permute-start(bf16[80,768]{1,0:T(8,128)(2,1)} %get-tuple-element.341), channel_id=1, source_target_pairs={{0,8},{4,12},{8,0},{12,4},{16,24},{20,28},{24,16},{28,20},{1,9},{5... | collective-permute-start | bytes 368648 | tf_op jit(solution)/shard_map/ppermute | solution.py:654
  362.6 11.3 %collective-permute-start.39 = (bf16[80,768]{1,0:T(8,128)(2,1)}, bf16[80,768]{1,0:T(8,128)(2,1)S(1)}, u32[]{:S(2)}, u32[]{:S(2)}) collective-permute-start(bf16[80,768]{1,0:T(8,128)(2,1)} %get-tuple-element.342), channel_id=1, source_target_pairs={{0,16},{4,20},{8,24},{12,28},{16,0},{20,4},{24,8},{28,12},{1,17},{... | collective-permute-start | bytes 368648 | tf_op jit(solution)/shard_map/ppermute | solution.py:654
  364.5 9.4 %collective-permute-start.40 = (bf16[80,768]{1,0:T(8,128)(2,1)}, bf16[80,768]{1,0:T(8,128)(2,1)S(1)}, u32[]{:S(2)}, u32[]{:S(2)}) collective-permute-start(bf16[80,768]{1,0:T(8,128)(2,1)} %get-tuple-element.343), channel_id=1, source_target_pairs={{0,24},{4,28},{8,16},{12,20},{16,8},{20,12},{24,0},{28,4},{1,25},{... | collective-permute-start | bytes 368648 | tf_op jit(solution)/shard_map/ppermute | solution.py:654
  376.4 7.9 %collective-permute-start.43 = (bf16[80,768]{1,0:T(8,128)(2,1)}, bf16[80,768]{1,0:T(8,128)(2,1)S(1)}, u32[]{:S(2)}, u32[]{:S(2)}) collective-permute-start(bf16[80,768]{1,0:T(8,128)(2,1)} %add_parts.3.refs_0_), channel_id=1, source_target_pairs={{0,24},{4,28},{8,16},{12,20},{16,8},{20,12},{24,0},{28,4},{1,25},{... | collective-permute-start | bytes 368648 | tf_op jit(solution)/shard_map/ppermute | solution.py:654
  378.1 10.5 %collective-permute-start.42 = (bf16[80,768]{1,0:T(8,128)(2,1)}, bf16[80,768]{1,0:T(8,128)(2,1)S(1)}, u32[]{:S(2)}, u32[]{:S(2)}) collective-permute-start(bf16[80,768]{1,0:T(8,128)(2,1)} %add_parts.3.refs_0_), channel_id=1, source_target_pairs={{0,16},{4,20},{8,24},{12,28},{16,0},{20,4},{24,8},{28,12},{1,17},{... | collective-permute-start | bytes 368648 | tf_op jit(solution)/shard_map/ppermute | solution.py:654
  379.8 8.8 %collective-permute-start.41 = (bf16[80,768]{1,0:T(8,128)(2,1)}, bf16[80,768]{1,0:T(8,128)(2,1)S(1)}, u32[]{:S(2)}, u32[]{:S(2)}) collective-permute-start(bf16[80,768]{1,0:T(8,128)(2,1)} %add_parts.3.refs_0_), channel_id=1, source_target_pairs={{0,8},{4,12},{8,0},{12,4},{16,24},{20,28},{24,16},{28,20},{1,9},{5... | collective-permute-start | bytes 368648 | tf_op jit(solution)/shard_map/ppermute | solution.py:654
  391.8 15.2 %collective-permute-start.46 = (bf16[320,768]{1,0:T(8,128)(2,1)}, bf16[320,768]{1,0:T(8,128)(2,1)S(1)}, u32[]{:S(2)}, u32[]{:S(2)}) collective-permute-start(bf16[320,768]{1,0:T(8,128)(2,1)} %bitcast.28), channel_id=1, source_target_pairs={{0,3},{1,2},{2,1},{3,0},{4,7},{5,6},{6,5},{7,4},{8,11},{9,10},{10,... | collective-permute-start | bytes 1474568 | tf_op jit(solution)/shard_map/ppermute | solution.py:654
  392.4 22.4 %collective-permute-start.45 = (bf16[320,768]{1,0:T(8,128)(2,1)}, bf16[320,768]{1,0:T(8,128)(2,1)S(1)}, u32[]{:S(2)}, u32[]{:S(2)}) collective-permute-start(bf16[320,768]{1,0:T(8,128)(2,1)} %bitcast.29), channel_id=1, source_target_pairs={{0,2},{1,3},{2,0},{3,1},{4,6},{5,7},{6,4},{7,5},{8,10},{9,11},{10,... | collective-permute-start | bytes 1474568 | tf_op jit(solution)/shard_map/ppermute | solution.py:654
  393.8 21.1 %collective-permute-start.44 = (bf16[320,768]{1,0:T(8,128)(2,1)}, bf16[320,768]{1,0:T(8,128)(2,1)S(1)}, u32[]{:S(2)}, u32[]{:S(2)}) collective-permute-start(bf16[320,768]{1,0:T(8,128)(2,1)} %bitcast.30), channel_id=1, source_target_pairs={{0,1},{1,0},{2,3},{3,2},{4,5},{5,4},{6,7},{7,6},{8,9},{9,8},{10,11... | collective-permute-start | bytes 1474568 | tf_op jit(solution)/shard_map/ppermute | solution.py:654
  395.3 20.0 %collective-permute-start.51 = (bf16[96,768]{1,0:T(8,128)(2,1)S(1)}, bf16[96,768]{1,0:T(8,128)(2,1)S(1)}, u32[]{:S(2)}, u32[]{:S(2)}) collective-permute-start(bf16[96,768]{1,0:T(8,128)(2,1)S(1)} %bitcast.41), channel_id=1, source_target_pairs={{0,4},{4,0},{8,12},{12,8},{16,20},{20,16},{24,28},{28,24},{1,5},{5... | collective-permute-start | bytes 442376 | tf_op jit(solution)/shard_map/ppermute | solution.py:654
  395.3 28.2 %collective-permute-start.47 = (bf16[320,768]{1,0:T(8,128)(2,1)}, bf16[320,768]{1,0:T(8,128)(2,1)S(1)}, u32[]{:S(2)}, u32[]{:S(2)}) collective-permute-start(bf16[320,768]{1,0:T(8,128)(2,1)} %bitcast.31), channel_id=1, source_target_pairs={{0,4},{4,0},{8,12},{12,8},{16,20},{20,16},{24,28},{28,24},{1,5},{5... | collective-permute-start | bytes 1474568 | tf_op jit(solution)/shard_map/ppermute | solution.py:654
  407.0 16.5 %collective-permute-start.50 = (bf16[320,768]{1,0:T(8,128)(2,1)S(1)}, bf16[320,768]{1,0:T(8,128)(2,1)S(1)}, u32[]{:S(2)}, u32[]{:S(2)}) collective-permute-start(bf16[320,768]{1,0:T(8,128)(2,1)S(1)} %collective-permute-done.46.refs_3_), channel_id=1, source_target_pairs={{0,4},{4,0},{8,12},{12,8},{16,20},{20,16},{24,28},{28,24},{1,5},{5... | collective-permute-start | bytes 1474568 | tf_op jit(solution)/shard_map/ppermute | solution.py:654
  414.8 8.7 %collective-permute-start.49 = (bf16[320,768]{1,0:T(8,128)(2,1)S(1)}, bf16[320,768]{1,0:T(8,128)(2,1)S(1)}, u32[]{:S(2)}, u32[]{:S(2)}) collective-permute-start(bf16[320,768]{1,0:T(8,128)(2,1)S(1)} %collective-permute-done.45.refs_2_), channel_id=1, source_target_pairs={{0,4},{4,0},{8,12},{12,8},{16,20},{20,16},{24,28},{28,24},{1,5},{5... | collective-permute-start | bytes 1474568 | tf_op jit(solution)/shard_map/ppermute | solution.py:654
  415.0 8.5 %collective-permute-start.48 = (bf16[320,768]{1,0:T(8,128)(2,1)S(1)}, bf16[320,768]{1,0:T(8,128)(2,1)}, u32[]{:S(2)}, u32[]{:S(2)}) collective-permute-start(bf16[320,768]{1,0:T(8,128)(2,1)S(1)} %collective-permute-done.44.refs_1_), channel_id=1, source_target_pairs={{0,4},{4,0},{8,12},{12,8},{16,20},{20,16},{24,28},{28,24},{1,5},{5... | collective-permute-start | bytes 1474568 | tf_op jit(solution)/shard_map/ppermute | solution.py:654
  415.3 2.3 collective-permute-start.52
  417.6 1.4 collective-permute-start.53
  418.9 1.5 collective-permute-start.54
  (53 other events, 303.7 us)
Sparse Core Ops, SparseCore 0:
  126.0 117.8 reduce-scatter.4
  246.2 102.5 reduce-scatter.2

commit v2 on v1

--- a/solution.py
+++ b/solution.py
@@ -13,6 +13,7 @@
 QUERY_ROWS = 256
 WINDOW = 768
 LANES = 256
+VECTOR_ROWS = 128
 EPSILON = 1e-05
 NEG_LARGE = -1e30
 ROOT_HALF = 0.7071067811865476
@@ -53,6 +54,12 @@
 
 def column(row):
     return jnp.broadcast_to(row.astype(f32), (128, row.shape[1])).T[:, :1]
+
+
+def split_cores(core, sums_ref, keep_ref, send_ref):
+    half = keep_ref.shape[0]
+    keep_ref[...] = sums_ref[pl.ds(pl.multiple_of(core * half, half), half), :].astype(bf16)
+    send_ref[...] = sums_ref[pl.ds(pl.multiple_of((1 - core) * half, half), half), :].astype(bf16)
 
 
 def norm_parts(values):
@@ -156,8 +163,8 @@
 
 
 def attend_back_kernel(
-    q_ref, k_ref, v_ref, do_ref, lse_ref, seg_ref, dq_ref, dk_ref, dv_ref,
-    mask_ref, dk_sum, dv_sum,
+    here_ref, q_ref, k_ref, v_ref, do_ref, lse_ref, seg_ref, attn_in_ref,
+    dq_ref, dk_ref, dv_ref, keep_ref, send_ref, mask_ref, dk_sum, dv_sum, dw_sum,
 ):
     length = q_ref.shape[0]
     blocks = length // QUERY_ROWS
@@ -202,10 +209,16 @@
             dq_ref[rows, lanes] = turned.T.astype(bf16)
     dk_ref[...] = dk_sum[...].astype(bf16)
     dv_ref[...] = dv_sum[...].astype(bf16)
-
-
-def attend_backward(which, q, k, v, do, lse, segment_ids):
-    length = q.shape[0]
+    turned = attn_in_ref[...].T
+    for which, grad_ref in enumerate((dq_ref, dk_ref, dv_ref)):
+        dw_sum[:, which * LANES : (which + 1) * LANES] = dot(turned, grad_ref[...])
+    split_cores(here_ref[0, 1], dw_sum, keep_ref, send_ref)
+
+
+def attend_backward(which, here, q, k, v, do, lse, segment_ids, attn_in):
+    length, width = q.shape
+    half = full_spec((width // 2, 3 * LANES), 1)
+    half_shape = shape_of((width // 2, 3 * LANES), bf16)
     sliced = pl.BlockSpec((length, LANES), lambda i: (0, which))
     out = full_spec((length, LANES), 1)
     act = shape_of((length, LANES), bf16)
@@ -213,18 +226,20 @@
         attend_back_kernel,
         grid=(1,),
         in_specs=[
-            sliced, sliced, sliced, sliced,
+            smem(), sliced, sliced, sliced, sliced,
             pl.BlockSpec((1, 8, length), lambda i: (which, 0, 0)), full_spec((1, length)),
+            full_spec((length, width), 1),
         ],
-        out_specs=[out, out, out],
-        out_shape=[act, act, act],
+        out_specs=[out, out, out, half, half],
+        out_shape=[act, act, act, half_shape, half_shape],
         scratch_shapes=[
             pltpu.VMEM((WINDOW, length), f32),
             pltpu.VMEM((length, LANES), f32), pltpu.VMEM((length, LANES), f32),
+            pltpu.VMEM((width, 3 * LANES), f32),
         ],
         cost_estimate=cost(10e9, 4e6, 2e6),
         name="attend_backward_%d" % which,
-    )(q, k, v, do, lse, segment_ids)
+    )(here, q, k, v, do, lse, segment_ids, attn_in)
 
 
 def project_kernel(x_ref, o_ref, wo_ref, gain_ref, bias_ref, y_ref, h_ref):
@@ -524,8 +539,8 @@
 
 
 def norm2_kernel(
-    dh0_ref, dh1_ref, y_ref, g_ref, o_ref, wo_ref, gain_ref,
-    dy_ref, do_ref, dwo_ref, vec_ref, dwo_sum, gain_sum, bias_sum,
+    here_ref, dh0_ref, dh1_ref, y_ref, g_ref, o_ref, wo_ref, gain_ref,
+    dy_ref, do_ref, keep_ref, send_ref, vec_ref, dwo_sum, gain_sum, bias_sum,
 ):
     step = pl.program_id(0)
 
@@ -547,28 +562,28 @@
 
     @pl.when(step == pl.num_programs(0) - 1)
     def _():
-        dwo_ref[...] = dwo_sum[...].astype(bf16)
+        split_cores(here_ref[0, 1], dwo_sum, keep_ref, send_ref)
         vec_ref[0:1, :] = gain_sum[...]
         vec_ref[1:2, :] = bias_sum[...]
 
 
-def norm2_back(dh_own, y, cotangent, o, wo, gain):
+def norm2_back(here, dh_own, y, cotangent, o, wo, gain):
     length, width = y.shape
     rows = 256
     block = pl.BlockSpec((rows, width), lambda i: (i, 0))
     return pl.pallas_call(
         norm2_kernel,
         grid=(length // rows,),
-        in_specs=[block] * 5 + [full_spec((width, width)), full_spec((1, width))],
-        out_specs=[block, block, full_spec((width, width)), full_spec((2, width))],
+        in_specs=[smem()] + [block] * 5 + [full_spec((width, width)), full_spec((1, width))],
+        out_specs=[block, block] + [full_spec((width // 2, width), 1)] * 2 + [full_spec((2, width))],
         out_shape=[
             shape_of((length, width), f32), shape_of((length, width), bf16),
-            shape_of((width, width), bf16), shape_of((2, width), f32),
+            shape_of((width // 2, width), bf16), shape_of((width // 2, width), bf16), shape_of((2, width), f32),
         ],
         scratch_shapes=[pltpu.VMEM((width, width), f32), pltpu.VMEM((1, width), f32), pltpu.VMEM((1, width), f32)],
         cost_estimate=cost(3e9, 15e6),
         name="norm2_back",
-    )(*dh_own, y, cotangent, o, wo, gain)
+    )(here, *dh_own, y, cotangent, o, wo, gain)
 
 
 def result_kernel(y_ref, z0_ref, z1_ref, out_ref):
@@ -590,25 +605,21 @@
     )(y, *z_own)
 
 
-def norm1_kernel(cuts, attn_in_ref, x_ref, dy_ref, wq_ref, wk_ref, wv_ref, gain_ref, vec2_ref, *refs):
+def norm1_kernel(cuts, here_ref, x_ref, dy_ref, wq_ref, wk_ref, wv_ref, gain_ref, vec2_ref, *refs):
     grad_refs = refs[: 3 * cuts]
-    dx_ref, dw_ref, dw_sum, gain_sum, bias_sum = refs[3 * cuts :]
+    dx_ref, keep_ref, send_ref, vec_sum, gain_sum, bias_sum = refs[3 * cuts :]
     step = pl.program_id(0)
-    width = x_ref.shape[1]
 
     @pl.when(step == 0)
     def _():
-        dw_sum[...] = jnp.zeros_like(dw_sum)
         gain_sum[...] = jnp.zeros_like(gain_sum)
         bias_sum[...] = jnp.zeros_like(bias_sum)
 
     da = None
-    turned = attn_in_ref[...].T
     for which, w_ref in enumerate((wq_ref, wk_ref, wv_ref)):
         grad = jnp.concatenate([grad_refs[3 * cut + which][...] for cut in range(cuts)], axis=1)
         term = dot_nt(grad, w_ref[...])
         da = term if da is None else da + term
-        dw_sum[which * width : (which + 1) * width, :] += dot(turned, grad)
     hat, inverse_std = norm_parts(x_ref[...].astype(f32))
     gain_sum[...] += jnp.sum(da * hat, axis=0, keepdims=True)
     bias_sum[...] += jnp.sum(da, axis=0, keepdims=True)
@@ -616,37 +627,38 @@
 
     @pl.when(step == pl.num_programs(0) - 1)
     def _():
-        dw_ref[: 3 * width, :] = dw_sum[...].astype(bf16)
+        vec_sum[...] = jnp.zeros_like(vec_sum)
         vectors = jnp.concatenate(
-            [gain_sum[...], bias_sum[...], vec2_ref[...], jnp.zeros((12, width), f32)], axis=0
+            [gain_sum[...], bias_sum[...], vec2_ref[...], jnp.zeros((12, vec_sum.shape[1]), f32)], axis=0
         )
-        high = vectors.astype(bf16)
-        dw_ref[3 * width : 3 * width + 16, :] = high
-        dw_ref[3 * width + 16 : 3 * width + 32, :] = (vectors - high.astype(f32)).astype(bf16)
-        rest = dw_ref.shape[0] - 3 * width - 32
-        dw_ref[3 * width + 32 :, :] = jnp.zeros((rest, width), bf16)
-
-
-def norm1_back(attn_in, grads, tokens, dy, wq, wk, wv, gain, vec2):
+        high = vectors.astype(bf16).astype(f32)
+        vec_sum[0:16, :] = high
+        vec_sum[16:32, :] = vectors - high
+        split_cores(here_ref[0, 1], vec_sum, keep_ref, send_ref)
+
+
+def norm1_back(here, grads, tokens, dy, wq, wk, wv, gain, vec2):
     length, width = tokens.shape
     rows = 256
-    total = 3 * width + 256
     cuts = len(grads)
     block = pl.BlockSpec((rows, width), lambda i: (i, 0))
     part = pl.BlockSpec((rows, width // cuts), lambda i: (i, 0))
     weight = full_spec((width, width))
+    half = full_spec((VECTOR_ROWS, width), 1)
+    half_shape = shape_of((VECTOR_ROWS, width), bf16)
     return pl.pallas_call(
         functools.partial(norm1_kernel, cuts),
         grid=(length // rows,),
-        in_specs=[block] * 3 + [weight] * 3 + [full_spec((1, width)), full_spec((2, width))] + [part] * (3 * cuts),
-        out_specs=[block, full_spec((total, width), 1)],
-        out_shape=[shape_of((length, width), bf16), shape_of((total, width), bf16)],
+        in_specs=[smem()] + [block] * 2 + [weight] * 3 + [full_spec((1, width)), full_spec((2, width))]
+        + [part] * (3 * cuts),
+        out_specs=[block, half, half],
+        out_shape=[shape_of((length, width), bf16), half_shape, half_shape],
         scratch_shapes=[
-            pltpu.VMEM((3 * width, width), f32), pltpu.VMEM((1, width), f32), pltpu.VMEM((1, width), f32),
+            pltpu.VMEM((2 * VECTOR_ROWS, width), f32), pltpu.VMEM((1, width), f32), pltpu.VMEM((1, width), f32),
         ],
         cost_estimate=cost(8e9, 20e6),
         name="norm1_back",
-    )(attn_in, tokens, dy, wq, wk, wv, gain, vec2, *[grad for three in grads for grad in three])
+    )(here, tokens, dy, wq, wk, wv, gain, vec2, *[grad for three in grads for grad in three])
 
 
 def swap(array, axis, step):
@@ -654,28 +666,33 @@
     return lax.ppermute(array, axis, [(i, i ^ step) for i in range(count)])
 
 
-def add_picked_kernel(count, outs, base, me_ref, *refs):
+def add_picked_kernel(sets, terms, outs, me_ref, *refs):
     me = me_ref[0, 0]
-    offset = me_ref[0, 1]
     for step in range(outs):
-        index = offset * base + lax.bitwise_xor(me, step)
-        total = refs[0][index].astype(f32)
-        for ref in refs[1:count]:
-            total = total + ref[index].astype(f32)
-        refs[count + step][...] = total.astype(bf16)
-
-
-def add_picked(arrays, outs, base, me, name):
-    _, rows, width = arrays[0].shape
+        index = lax.bitwise_xor(me, step)
+        out_ref = refs[sets * terms + step]
+        row = 0
+        for which in range(sets):
+            total = refs[which * terms][index].astype(f32)
+            for ref in refs[which * terms + 1 : (which + 1) * terms]:
+                total = total + ref[index].astype(f32)
+            out_ref[row : row + total.shape[0], :] = total.astype(bf16)
+            row += total.shape[0]
+
+
+def add_picked(sets, pieces, me, name):
+    width = sets[0][0].shape[1]
+    arrays = [array.reshape(pieces, array.shape[0] // pieces, width) for terms in sets for array in terms]
+    rows = sum(terms[0].shape[0] // pieces for terms in sets)
     vmem = pl.BlockSpec(memory_space=pltpu.VMEM)
-    return pl.pallas_call(
-        functools.partial(add_picked_kernel, len(arrays), outs, base),
+    return list(pl.pallas_call(
+        functools.partial(add_picked_kernel, len(sets), len(sets[0]), pieces),
         in_specs=[smem()] + [vmem] * len(arrays),
-        out_specs=[vmem] * outs,
-        out_shape=[shape_of((rows, width), bf16)] * outs,
-        cost_estimate=cost(1e6, 2 * rows * width * outs * (len(arrays) + 1)),
+        out_specs=[vmem] * pieces,
+        out_shape=[shape_of((rows, width), bf16)] * pieces,
+        cost_estimate=cost(1, 1),
         name=name,
-    )(me, *arrays)
+    )(me, *arrays))
 
 
 def add_kernel(*refs):
@@ -692,105 +709,80 @@
         in_specs=[vmem] * len(arrays),
         out_specs=vmem,
         out_shape=shape_of(arrays[0].shape, bf16),
-        cost_estimate=cost(1e6, arrays[0].size * 2 * (len(arrays) + 1)),
+        cost_estimate=cost(1, 1),
         name="add_parts",
     )(*arrays)
 
 
-def line_kernel(count, me_ref, *refs):
+def line_kernel(sizes, me_ref, *refs):
+    count = len(refs) - 1
     for step in range(count):
-        refs[count][lax.bitwise_xor(me_ref[0, 0], step)] = refs[step][...]
-
-
-def line_up(arrays, me):
+        place = lax.bitwise_xor(me_ref[0, 0], step)
+        row, start = 0, 0
+        for size in sizes:
+            at = pl.multiple_of(start + place * size, 8)
+            refs[count][pl.ds(at, size), :] = refs[step][row : row + size, :]
+            row += size
+            start += size * count
+
+
+def line_up(arrays, sizes, me):
     vmem = pl.BlockSpec(memory_space=pltpu.VMEM)
     count = len(arrays)
-    return pl.pallas_call(
-        functools.partial(line_kernel, count),
+    rows, width = arrays[0].shape
+    if any(size % 8 for size in sizes):
+        ordered = jnp.stack(arrays)[lax.bitwise_xor(me[0, 0], jnp.arange(count, dtype=jnp.int32))]
+        starts = [sum(sizes[:which]) for which in range(len(sizes))]
+        return jnp.concatenate(
+            [ordered[:, start : start + size].reshape(-1, width) for start, size in zip(starts, sizes)]
+        )
+    return pl.pallas_call(
+        functools.partial(line_kernel, sizes),
         in_specs=[smem()] + [vmem] * count,
         out_specs=vmem,
-        out_shape=shape_of((count, *arrays[0].shape), bf16),
-        cost_estimate=cost(1e3, arrays[0].size * 4 * count),
+        out_shape=shape_of((count * rows, width), bf16),
+        cost_estimate=cost(1, 1),
         name="line_up",
     )(me, *arrays)
 
 
-def finish_kernel(groups, parts, has_vectors, me_ref, *refs):
-    count = 2 * groups
-    lines, outs, full = refs[:count], refs[count : count + parts], refs[-1]
-    vec_ref = refs[count + parts]
-    me, core = me_ref[0, 0], me_ref[0, 1]
+def finish_kernel(groups, here_ref, *refs):
+    lines, refs = refs[: 2 * groups], refs[2 * groups :]
+    out_ref, head_refs, vec_ref, vec_all = refs[0], refs[1:4], refs[4], refs[5]
+    me, core = here_ref[0, 0], here_ref[0, 1]
+    width = out_ref.shape[0]
+    size = width // (2 * groups)
+    vec_size = VECTOR_ROWS // groups
     for side in range(2):
         for step in range(groups):
+            line = lines[side * groups + step]
             index = lax.bitwise_xor(core, side) * groups + lax.bitwise_xor(me, step)
-            full[index] = lines[side * groups + step][...]
-    piece = full.shape[1]
-    width = outs[0].shape[1]
-    row = 0
-    while row < parts * width:
-        index, inside = row // piece, row % piece
-        which, at = row // width, row % width
-        size = min(piece - inside, width - at)
-        outs[which][at : at + size, :] = full[index, inside : inside + size, :].astype(f32)
-        row += size
-    if not has_vectors:
-        return
-    row = parts * width
-    sums = []
-    for start in (row, row + 16):
-        index, inside = start // piece, start % piece
-        sums.append(full[index, inside : inside + 8, :].astype(f32))
-    vec_ref[...] = sums[0] + sums[1]
-
-
-def finish(lines, parts, groups, me):
-    piece, width = lines[0].shape
-    has_vectors = 2 * groups * piece > parts * width
+            rows = pl.ds(pl.multiple_of(index * size, 8), size)
+            out_ref[rows, :] = line[:size, :].astype(f32)
+            for cut in range(width // LANES):
+                block = line[(cut + 1) * size : (cut + 2) * size, :].astype(f32)
+                for which in range(3):
+                    head_refs[which][rows, cut * LANES : (cut + 1) * LANES] = (
+                        block[:, which * LANES : (which + 1) * LANES]
+                    )
+            first = (1 + width // LANES) * size
+            vec_all[pl.ds(pl.multiple_of(index * vec_size, 8), vec_size), :] = (
+                line[first : first + vec_size, :].astype(f32)
+            )
+    vec_ref[...] = vec_all[0:8, :] + vec_all[16:24, :]
+
+
+def finish(lines, width, groups, here):
     vmem = pl.BlockSpec(memory_space=pltpu.VMEM)
     return pl.pallas_call(
-        functools.partial(finish_kernel, groups, parts, has_vectors),
+        functools.partial(finish_kernel, groups),
         in_specs=[smem()] + [vmem] * len(lines),
-        out_specs=[vmem] * (parts + has_vectors),
-        out_shape=[shape_of((width, width), f32)] * parts + [shape_of((8, width), f32)] * has_vectors,
-        scratch_shapes=[pltpu.VMEM((2 * groups, piece, width), bf16)],
-        cost_estimate=cost(1e3, 15e6),
+        out_specs=[vmem] * 5,
+        out_shape=[shape_of((width, width), f32)] * 4 + [shape_of((8, width), f32)],
+        scratch_shapes=[pltpu.VMEM((2 * VECTOR_ROWS, width), f32)],
+        cost_estimate=cost(1, 1),
         name="finish",
-    )(me, *lines)
-
-
-def sum_all(array, parts):
-    dp, groups = lax.axis_size("dp"), lax.axis_size("expert")
-    depth = dp // 2
-    me = lax.axis_index("expert").astype(jnp.int32)
-    core = (lax.axis_index("dp") % 2).astype(jnp.int32)
-    place = (lax.axis_index("dp") // 2).astype(jnp.int32)
-    here = jnp.stack([me, core]).reshape(1, 2)
-    there = jnp.stack([place, jnp.int32(0)]).reshape(1, 2)
-    rows, width = array.shape
-    piece = rows // (2 * groups)
-    other = swap(array, "dp", 1)
-    other = yield other
-    shape = (2 * groups, piece, width)
-    halves = add_picked([array.reshape(shape), other.reshape(shape)], groups, groups, here, "add_cores")
-    shape = (depth, piece // depth, width)
-    came = yield [halves[0]] + [swap(halves[step], "expert", step) for step in range(1, groups)]
-    halves = add_picked([part.reshape(shape) for part in came], depth, 0, there, "add_groups")
-    mine = yield [halves[0]] + [swap(halves[step], "dp", 2 * step) for step in range(1, depth)]
-    mine = add_parts(mine)
-    line = yield [mine] + [swap(mine, "dp", 2 * step) for step in range(1, depth)]
-    line = line_up(line, there)
-    line = line.reshape(piece, width)
-    plane = yield [line] + [swap(line, "expert", step) for step in range(1, groups)]
-    lines = yield plane + [swap(part, "dp", 1) for part in plane]
-    yield finish(lines, parts, groups, here)
-
-
-def last_of(rounds, value):
-    while True:
-        try:
-            value = rounds.send(value)
-        except StopIteration:
-            return value
+    )(here, *lines)
 
 
 def shards(
@@ -805,6 +797,10 @@
     capacity = 2 * length // experts
     me_index = lax.axis_index("expert").astype(jnp.int32)
     me = me_index.reshape(1, 1)
+    depth = lax.axis_size("dp") // 2
+    core_index = (lax.axis_index("dp") % 2).astype(jnp.int32)
+    here = jnp.stack([me_index, core_index]).reshape(1, 2)
+    place = (lax.axis_index("dp") // 2).astype(jnp.int32).reshape(1, 1)
     gain1, bias1 = norm1_gain.reshape(1, width), norm1_bias.reshape(1, width)
     gain2, bias2 = norm2_gain.reshape(1, width), norm2_bias.reshape(1, width)
     router = router_w.T.astype(f32)
@@ -854,33 +850,54 @@
     dh_own, dw_last, z_out = barrier((dh_own, dw_last, z_out))
     grads_out.append(scatter(dw_last))
     z_in = exchange(z_out)
-    dy, do, grad_out, vec2 = norm2_back(dh_own, y, cotangent, o, out_w, gain2)
-    rounds = sum_all(grad_out, 1)
-    early = next(rounds)
+    def spread(parts, axis, stride=1):
+        return [parts[0]] + [swap(parts[step], axis, stride * step) for step in range(1, len(parts))]
+
+    dy, do, keep_out, send_out, vec2 = norm2_back(here, dh_own, y, cotangent, o, out_w, gain2)
+    kept, came = [keep_out], [swap(send_out, "dp", 1)]
     grads = []
     for which in range(width // LANES):
-        grads.append(attend_backward(which, q, k, v, do, lse, segment_ids))
-        early, z_in, q, attn_in, grads = barrier((early, z_in, q, attn_in, grads))
-        early = rounds.send(early)
-        first, q, attn_in = barrier((early[0], q, attn_in))
-        early = [first] + list(early[1:])
-    dx, grad_qkv = norm1_back(attn_in, grads, tokens, dy, query_w, key_w, value_w, gain1, vec2)
-    late = sum_all(grad_qkv, 3)
-    swapped, early = barrier((next(late), early))
-    early = rounds.send(early)
-    came = late.send(swapped)
+        *grad, keep, send = attend_backward(which, here, q, k, v, do, lse, segment_ids, attn_in)
+        send, grad, q = barrier((send, grad, q))
+        grads.append(grad)
+        kept.append(keep)
+        came.append(swap(send, "dp", 1))
+    z_in, came[:-1], send, q = barrier((z_in, came[:-1], send, q))
+    early = add_picked([[keep, other] for keep, other in zip(kept[:-1], came[:-1])], groups, here, "add_cores")
+    early[0], grads = barrier((early[0], grads))
+    early = spread(early, "expert")
+    dx, keep, send = norm1_back(here, grads, tokens, dy, query_w, key_w, value_w, gain1, vec2)
+    other = swap(send, "dp", 1)
+    slots, send = barrier((slots, send))
     z_own = [collect(before, slots, joined_ins[before], capacity, 1) for before in range(own)]
+    other, z_own, came[-1] = barrier((other, z_own, came[-1]))
+    late = add_picked([[kept[-1], came[-1]], [keep, other]], groups, here, "add_cores")
+    late[0], slots = barrier((late[0], slots))
+    late = spread(late, "expert")
     z_own.append(collect(own, slots, z_in, capacity))
     block_out = block_result(y, z_own)
-    came, early, block_out = barrier((came, early, block_out))
-    grad_o = last_of(rounds, early)[0]
-    grad_q, grad_k, grad_v, vectors = last_of(late, came)
-    shares = None
-    for which in range(local):
-        shares = unpack_shares(
+    early, late, block_out = barrier((early, late, block_out))
+    parts = add_picked([early, late], depth, place, "add_groups")
+    mine = add_parts(spread(parts, "dp", 2))
+    line = line_up(
+        spread([mine] * depth, "dp", 2), [early[0].shape[0] // depth, late[0].shape[0] // depth], place
+    )
+    plane = spread([line] * groups, "expert")
+
+    def unpack(which, shares):
+        return unpack_shares(
             which, grads_out[which], shares, local, width // lax.axis_size("dp"),
             expert_in.shape[2] // lax.axis_size("dp"), expert_in.shape[2],
         )
+
+    line, grads_out = barrier((line, grads_out))
+    shares = None
+    for which in range(local - 1):
+        shares = unpack(which, shares)
+    plane, shares = barrier((plane, shares))
+    lines = plane + [swap(part, "dp", 1) for part in plane]
+    grad_o, grad_q, grad_k, grad_v, vectors = finish(lines, width, groups, here)
+    shares = unpack(local - 1, shares)
     return (
         block_out,
         dx,

time: 445 us -> 423 us (0.951)
  starting transfers between devices: 90.8 us -> 61.4 us
    ppermute x55 -> x45, starting transfers between devices: 90.7 us -> 61.4 us  [swap(): return lax.ppermute(array, axis, [(i, i ^ step) for i in range(count)])]
    pallas_call x2, Pallas kernels: 59.8 us -> 69.7 us  [run_expert(): pl.pallas_call(functools.partial(expert_kernel, capacity, groups, local,...]
    pallas_call x1, Pallas kernels: 15.5 us -> 10.2 us  [norm1_back(): pl.pallas_call(functools.partial(norm1_kernel, cuts), grid=(length // row...]
    ppermute x55 -> x45, waiting for transfers between devices: 89.7 us -> 91.2 us  [swap(): return lax.ppermute(array, axis, [(i, i ^ step) for i in range(count)])]
    unnamed x120 -> x98, local copies, waits for them, and re-layouts: 11.6 us -> 10.8 us
    pallas_call x12 -> x9, Pallas kernels: 67.1 us -> 67.3 us  [the longest x3 39.8 us: attend_backward(): pl.pallas_call(attend_back_kernel, grid=(1,), in_specs=[smem(), sliced, s...]
  transfers between devices with their start and end apart: 57 -> 47, of which waited for: 19 -> 15; matrix products, arithmetic and copies ran while one was open for 1% -> 1% of each run, Pallas kernels for 47% -> 50%
where the time goes in v2:
time: 423 us; the launch traced here: 418 us
  Pallas kernels  234 us (55%)
  waiting for transfers between devices  91.2 us (22%)
  starting transfers between devices  61.4 us (15%)
  between operations  14.8 us (3%)
  local copies, waits for them, and re-layouts  14.6 us (3%)
    ppermute x45, waiting for transfers between devices, swap(): return lax.ppermute(array, axis, [(i, i ^ step) for i in range(count)])  91.2 us
    pallas_call x2, Pallas kernels, run_expert(): pl.pallas_call(functools.partial(expert_kernel, capacity, groups, local,...  69.7 us
    ppermute x45, starting transfers between devices, swap(): return lax.ppermute(array, axis, [(i, i ^ step) for i in range(count)])  61.4 us
    pallas_call x3, Pallas kernels, attend_backward(): pl.pallas_call(attend_back_kernel, grid=(1,), in_specs=[smem(), sliced, s...  39.8 us
    pallas_call x1, Pallas kernels, attend_forward(): pl.pallas_call(attend_kernel, grid=(steps,), in_specs=[full_spec((length,...  32.2 us
    pallas_call x4, Pallas kernels, collect(): pl.pallas_call(functools.partial(collect_kernel, capacity, groups, own),...  19 us
    pallas_call x3, Pallas kernels, dispatch(): pl.pallas_call(functools.partial(dispatch_kernel, capacity, groups, owns)...  14.6 us
    unnamed x98, local copies, waits for them, and re-layouts  10.8 us
  transfers between devices with their start and end apart: 47, of which 15 were waited for; matrix products, arithmetic and copies ran while one was open for 1% of the time, Pallas kernels for 50%

profile of v2, /device:TPU:0, one launch (start us, length us, event | category | flops | bytes accessed | tf_op | source)
XLA Modules:
  0.0 418.2 jit_solution(9402776026708821775)
XLA Ops:
  7.3 2.1 token_slots.1.slot_ref
  9.4 6.3 %dispatch_0.2 = (bf16[512,768]{1,0:T(8,128)(2,1)}, bf16[512,768]{1,0:T(8,128)(2,1)}, bf16[512,768]{1,0:T(8,128)(2,1)}, bf16[512,768]{1,0:T(8,128)(2,1)}) custom-call(s32[1,1024]{1,0:T(1,128)} %token_slots.1.slot_ref, bf16[1024,768]{1,0:T(8,128)(2,1)} %g_ref.1), custom_call_target="tpu_custom_call" | custom-call | flops 1 | bytes 1 | tf_op jit(solution)/shard_map/dispatch_0/pallas_call | solution.py:319
  15.7 3.0 collective-permute-start
  18.7 1.5 collective-permute-start.1
  20.2 2.0 collective-permute-start.4
  22.2 1.5 collective-permute-start.3
  24.9 32.2 %attend_forward.1 = (bf16[1024,768]{1,0:T(8,128)(2,1)}, bf16[1024,768]{1,0:T(8,128)(2,1)}, bf16[1024,768]{1,0:T(8,128)(2,1)}, bf16[1024,768]{1,0:T(8,128)(2,1)},...) custom-call(bf16[1024,768]{1,0:T(8,128)(2,1)} %x_ref.7, f32[1,768]{1,0:T(1,128)} %reshape.111.gain_ref, ...), custom_call_target="tpu_custom_call" | custom-call | flops 1 | bytes 1 | tf_op jit(solution)/shard_map/attend_forward/pallas_call | solution.py:147
  58.3 4.5 %collective-permute-done.5 = s32[1,8]{1,0:T(1,128)S(1)} collective-permute-done((s32[1,8]{1,0:T(1,128)S(1)}, s32[1,8]{1,0:T(1,128)S(1)}, u32[]{:S(2)}, u32[]{:S(2)}) %collective-permute-start.5) | collective-permute-done | bytes 64 | tf_op jit(solution)/shard_map/ppermute | solution.py:666
  63.4 7.0 %project.1 = (f32[1024,768]{1,0:T(8,128)}, bf16[1024,768]{1,0:T(8,128)(2,1)}) custom-call(bf16[1024,768]{1,0:T(8,128)(2,1)} %x_ref.7, bf16[1024,768]{1,0:T(8,128)(2,1)} %get-tuple-element.184.o_ref, bf16[768,768]{1,0:T(8,128)(2,1)} %wo_ref.3, f32[1,768]{1,0:T(1,128)} %reshape.113.gain_ref, f32[1,768]{1,0:T(1,128)} %reshape.114.bias_ref), custom_call_target="tpu_custom_call" | custom-call | flops 1 | bytes 1 | tf_op jit(solution)/shard_map/project/pallas_call | solution.py:256
  70.5 4.2 dispatch_0.3
  75.2 2.9 collective-permute-start.8
  78.1 4.2 dispatch_1.1
  82.9 4.0 collective-permute-done.6.refs_1_
  87.5 6.5 %collective-permute-done.7.refs_2_ = bf16[256,768]{1,0:T(8,128)(2,1)S(1)} collective-permute-done((bf16[256,768]{1,0:T(8,128)(2,1)}, bf16[256,768]{1,0:T(8,128)(2,1)S(1)}, u32[]{:S(2)}, u32[]{:S(2)}) %collective-permute-start.7) | collective-permute-done | bytes 393248 | tf_op jit(solution)/shard_map/ppermute | solution.py:666
  94.0 1.2 collective-permute-done.8.refs_3_
  96.0 29.8 %expert_0.1 = (bf16[512,768]{1,0:T(8,128)(2,1)}, bf16[512,768]{1,0:T(8,128)(2,1)}, bf16[512,768]{1,0:T(8,128)(2,1)}, bf16[512,768]{1,0:T(8,128)(2,1)}, bf16[8,768,768]{2,1,0:T(8,128)(2,1)}) custom-call(s32[1,1]{1,0:T(1,128)} %bitcast.3.me_ref, s32[4,8]{1,0:T(4,128)} %pad_add_fusion.counts_ref, f32[8,768]{1,0:T(8,128)} %convert_bitcast_fusion.router_ref, ...), custom_call_target="tpu_custom_call" | custom-call | flops 1 | bytes 1 | tf_op jit(solution)/shard_map/expert_0/pallas_call | solution.py:489
  126.8 10.5 %collective-permute-start.9 = (bf16[512,768]{1,0:T(8,128)(2,1)}, bf16[512,768]{1,0:T(8,128)(2,1)S(1)}, u32[]{:S(2)}, u32[]{:S(2)}) collective-permute-start(bf16[512,768]{1,0:T(8,128)(2,1)} %get-tuple-element.203), channel_id=1, source_target_pairs={{0,1},{1,0},{2,3},{3,2},{4,5},{5,4},{6,7},{7,6},{8,9},{9,8},{10,11... | collective-permute-start | bytes 2359304 | tf_op jit(solution)/shard_map/ppermute | solution.py:666
  138.8 39.9 %expert_1.1 = (bf16[256,768]{1,0:T(8,128)(2,1)}, bf16[256,768]{1,0:T(8,128)(2,1)}, bf16[256,768]{1,0:T(8,128)(2,1)}, bf16[256,768]{1,0:T(8,128)(2,1)}, bf16[256,...) custom-call(s32[1,1]{1,0:T(1,128)} %bitcast.3.me_ref, ...), custom_call_target="tpu_custom_call" | custom-call | flops 1 | bytes 1 | tf_op jit(solution)/shard_map/expert_1/pallas_call | solution.py:489
  178.7 2.1 collective-permute-start.15
  180.9 8.9 %collective-permute-start.16 = (bf16[256,768]{1,0:T(8,128)(2,1)}, bf16[256,768]{1,0:T(8,128)(2,1)S(1)}, u32[]{:S(2)}, u32[]{:S(2)}) collective-permute-start(bf16[256,768]{1,0:T(8,128)(2,1)} %get-tuple-element.217), channel_id=1, source_target_pairs={{0,2},{1,3},{2,0},{3,1},{4,6},{5,7},{6,4},{7,5},{8,10},{9,11},{10,... | collective-permute-start | bytes 1179656 | tf_op jit(solution)/shard_map/ppermute | solution.py:666
  189.8 0.9 copy-done.3
  191.2 4.8 %collect_0.2.dh0_ref = bf16[1024,768]{1,0:T(8,128)(2,1)} custom-call(s32[1,1024]{1,0:T(1,128)} %token_slots.1.slot_ref, bf16[512,768]{1,0:T(8,128)(2,1)} %get-tuple-element.219.refs_0_, bf16[512,768]{1,0:T(8,128)(2,1)} %copy-done.3, bf16[512,768]{1,0:T(8,128)(2,1)} %copy-done.4, bf16[512,768]{1,0:T(8,128)(2,1)} %copy-done.5), custom_call_target="tpu_custom_call" | custom-call | flops 1 | bytes 1 | tf_op jit(solution)/shard_map/collect_0/pallas_call | solution.py:346
  195.9 4.0 collective-permute-done.16.refs_2_
  201.4 4.8 %collect_1.2.dh1_ref = bf16[1024,768]{1,0:T(8,128)(2,1)} custom-call(s32[1,1024]{1,0:T(1,128)} %token_slots.1.slot_ref, bf16[256,768]{1,0:T(8,128)(2,1)} %get-tuple-element.223.refs_0_, bf16[256,768]{1,0:T(8,128)(2,1)} %copy-done.21, bf16[256,768]{1,0:T(8,128)(2,1)} %copy-done.22, bf16[256,768]{1,0:T(8,128)(2,1)} %copy-done.23), custom_call_target="tpu_custom_call" | custom-call | flops 1 | bytes 1 | tf_op jit(solution)/shard_map/collect_1/pallas_call | solution.py:346
  206.2 1.0 copy-done.48
  207.9 1.5 collective-permute-start.19
  210.0 10.6 %norm2_back.1 = (f32[1024,768]{1,0:T(8,128)}, bf16[1024,768]{1,0:T(8,128)(2,1)}, bf16[384,768]{1,0:T(8,128)(2,1)}, bf16[384,768]{1,0:T(8,128)(2,1)}, f32[2,768]{1,0:T(2,128)}) custom-call(s32[1,2]{1,0:T(1,128)} %add_bitcast_fusion.here_ref.me_ref, bf16[1024,768]{1,0:T(8,128)(2,1)} %collect_0.2.dh0_ref, bf16[1024,768]{1,0:T(8,128)(2,1)} %collect_1.2.dh1_ref, ...), custom_call_target="tpu_custom_call" | custom-call | flops 1 | bytes 1 | tf_op jit(solution)/shard_map/norm2_back/pallas_call | solution.py:574
  220.7 13.1 %attend_backward_0.1 = (bf16[1024,256]{1,0:T(8,128)(2,1)}, bf16[1024,256]{1,0:T(8,128)(2,1)}, bf16[1024,256]{1,0:T(8,128)(2,1)}, bf16[384,768]{1,0:T(8,128)(2,1)}, bf16[384,768]{1,0:T(8,128)(2,1)}) custom-call(s32[1,2]{1,0:T(1,128)} %add_bitcast_fusion.here_ref.me_ref, bf16[1024,768]{1,0:T(8,128)(2,1)} %get-tuple-element.258.q_ref, ...), custom_call_target="tpu_custom_call" | custom-call | flops 1 | bytes 1 | tf_op jit(solution)/shard_map/attend_backward_0/pallas_call | solution.py:225
  234.4 13.3 %attend_backward_1.1 = (bf16[1024,256]{1,0:T(8,128)(2,1)}, bf16[1024,256]{1,0:T(8,128)(2,1)}, bf16[1024,256]{1,0:T(8,128)(2,1)}, bf16[384,768]{1,0:T(8,128)(2,1)}, bf16[384,768]{1,0:T(8,128)(2,1)}) custom-call(s32[1,2]{1,0:T(1,128)} %add_bitcast_fusion.here_ref.me_ref, bf16[1024,768]{1,0:T(8,128)(2,1)} %get-tuple-element.258.q_ref, ...), custom_call_target="tpu_custom_call" | custom-call | flops 1 | bytes 1 | tf_op jit(solution)/shard_map/attend_backward_1/pallas_call | solution.py:225
  247.7 1.4 collective-permute-start.20
  249.1 13.4 %attend_backward_2.1 = (bf16[1024,256]{1,0:T(8,128)(2,1)}, bf16[1024,256]{1,0:T(8,128)(2,1)}, bf16[1024,256]{1,0:T(8,128)(2,1)}, bf16[384,768]{1,0:T(8,128)(2,1)}, bf16[384,768]{1,0:T(8,128)(2,1)}) custom-call(s32[1,2]{1,0:T(1,128)} %add_bitcast_fusion.here_ref.me_ref, bf16[1024,768]{1,0:T(8,128)(2,1)} %get-tuple-element.258.q_ref, ...), custom_call_target="tpu_custom_call" | custom-call | flops 1 | bytes 1 | tf_op jit(solution)/shard_map/attend_backward_2/pallas_call | solution.py:225
  264.1 3.5 add_cores.2
  267.7 10.2 %norm1_back.1 = (bf16[1024,768]{1,0:T(8,128)(2,1)}, bf16[128,768]{1,0:T(8,128)(2,1)}, bf16[128,768]{1,0:T(8,128)(2,1)}) custom-call(s32[1,2]{1,0:T(1,128)} %add_bitcast_fusion.here_ref.me_ref, bf16[1024,768]{1,0:T(8,128)(2,1)} %x_ref.7, f32[1024,768]{1,0:T(8,128)} %get-tuple-element.284.dy_ref, bf16[768,768]{1,0:T(8,128)(2,1)} %wq_ref.3, ...), custom_call_target="tpu_custom_call" | custom-call | flops 1 | bytes 1 | tf_op jit(solution)/shard_map/norm1_back/pallas_call | solution.py:649
  278.3 0.9 collective-permute-start.24
  279.2 1.3 collective-permute-start.25
  280.5 1.4 collective-permute-start.26
  281.9 4.8 %collect_0.3.z0_ref = bf16[1024,768]{1,0:T(8,128)(2,1)} custom-call(s32[1,1024]{1,0:T(1,128)} %token_slots.1.slot_ref, bf16[512,768]{1,0:T(8,128)(2,1)} %get-tuple-element.219.refs_0_, bf16[512,768]{1,0:T(8,128)(2,1)} %copy-done.3, bf16[512,768]{1,0:T(8,128)(2,1)} %copy-done.4, bf16[512,768]{1,0:T(8,128)(2,1)} %copy-done.5), custom_call_target="tpu_custom_call" | custom-call | flops 1 | bytes 1 | tf_op jit(solution)/shard_map/collect_0/pallas_call | solution.py:346
  287.5 2.3 add_cores.3
  290.7 1.3 collective-permute-start.30
  292.0 12.5 %collective-permute-done.29 = bf16[128,768]{1,0:T(8,128)(2,1)S(1)} collective-permute-done((bf16[128,768]{1,0:T(8,128)(2,1)}, bf16[128,768]{1,0:T(8,128)(2,1)S(1)}, u32[]{:S(2)}, u32[]{:S(2)}) %collective-permute-start.29) | collective-permute-done | bytes 196640 | tf_op jit(solution)/shard_map/ppermute | solution.py:666
  304.5 1.8 collective-permute-start.31
  306.3 4.7 %collect_1.3.z1_ref = bf16[1024,768]{1,0:T(8,128)(2,1)} custom-call(s32[1,1024]{1,0:T(1,128)} %token_slots.1.slot_ref, bf16[256,768]{1,0:T(8,128)(2,1)} %get-tuple-element.307.refs_0_, bf16[256,768]{1,0:T(8,128)(2,1)} %copy-done.18, bf16[256,768]{1,0:T(8,128)(2,1)} %copy-done.19, bf16[256,768]{1,0:T(8,128)(2,1)} %copy-done.20), custom_call_target="tpu_custom_call" | custom-call | flops 1 | bytes 1 | tf_op jit(solution)/shard_map/collect_1/pallas_call | solution.py:346
  311.0 4.6 %block_result.1 = bf16[1024,768]{1,0:T(8,128)(2,1)} custom-call(f32[1024,768]{1,0:T(8,128)} %get-tuple-element.234.y_ref, bf16[1024,768]{1,0:T(8,128)(2,1)} %collect_0.3.z0_ref, bf16[1024,768]{1,0:T(8,128)(2,1)} %collect_1.3.z1_ref), custom_call_target="tpu_custom_call" | custom-call | flops 1 | bytes 1 | tf_op jit(solution)/shard_map/block_result/pallas_call | solution.py:597
  316.8 2.7 add_groups.1
  319.6 1.8 collective-permute-start.32
  321.3 1.1 collective-permute-start.33
  322.5 1.5 collective-permute-start.34
  323.9 10.7 %collective-permute-done.32.refs_1_ = bf16[104,768]{1,0:T(8,128)(2,1)S(1)} collective-permute-done((bf16[104,768]{1,0:T(8,128)(2,1)}, bf16[104,768]{1,0:T(8,128)(2,1)S(1)}, u32[]{:S(2)}, u32[]{:S(2)}) %collective-permute-start.32) | collective-permute-done | bytes 159776 | tf_op jit(solution)/shard_map/ppermute | solution.py:666
  334.7 1.6 collective-permute-done.33.refs_2_
  336.3 6.9 %collective-permute-done.34.refs_3_ = bf16[104,768]{1,0:T(8,128)(2,1)S(1)} collective-permute-done((bf16[104,768]{1,0:T(8,128)(2,1)}, bf16[104,768]{1,0:T(8,128)(2,1)S(1)}, u32[]{:S(2)}, u32[]{:S(2)}) %collective-permute-start.34) | collective-permute-done | bytes 159776 | tf_op jit(solution)/shard_map/ppermute | solution.py:666
  343.9 1.9 add_parts.1.refs_0_
  346.2 4.5 %collective-permute-start.36 = (bf16[104,768]{1,0:T(8,128)(2,1)}, bf16[104,768]{1,0:T(8,128)(2,1)S(1)}, u32[]{:S(2)}, u32[]{:S(2)}) collective-permute-start(bf16[104,768]{1,0:T(8,128)(2,1)} %add_parts.1.refs_0_), channel_id=1, source_target_pairs={{0,16},{4,20},{8,24},{12,28},{16,0},{20,4},{24,8},{28,12},{1,17},{... | collective-permute-start | bytes 479240 | tf_op jit(solution)/shard_map/ppermute | solution.py:666
  350.7 4.1 collective-permute-done.37.refs_3_
  354.8 8.8 %collective-permute-done.36.refs_2_ = bf16[104,768]{1,0:T(8,128)(2,1)S(1)} collective-permute-done((bf16[104,768]{1,0:T(8,128)(2,1)}, bf16[104,768]{1,0:T(8,128)(2,1)S(1)}, u32[]{:S(2)}, u32[]{:S(2)}) %collective-permute-start.36) | collective-permute-done | bytes 159776 | tf_op jit(solution)/shard_map/ppermute | solution.py:666
  365.0 2.0 line_up.1.refs_0_
  367.0 2.0 collective-permute-start.40
  369.0 0.9 collective-permute-start.39
  370.5 2.8 unpack_shares.2
  373.3 12.2 %collective-permute-done.40.refs_3_ = bf16[416,768]{1,0:T(8,128)(2,1)S(1)} collective-permute-done((bf16[416,768]{1,0:T(8,128)(2,1)}, bf16[416,768]{1,0:T(8,128)(2,1)S(1)}, u32[]{:S(2)}, u32[]{:S(2)}) %collective-permute-start.40) | collective-permute-done | bytes 639008 | tf_op jit(solution)/shard_map/ppermute | solution.py:666
  385.4 12.7 %collective-permute-done.39.refs_2_ = bf16[416,768]{1,0:T(8,128)(2,1)S(1)} collective-permute-done((bf16[416,768]{1,0:T(8,128)(2,1)}, bf16[416,768]{1,0:T(8,128)(2,1)S(1)}, u32[]{:S(2)}, u32[]{:S(2)}) %collective-permute-start.39) | collective-permute-done | bytes 639008 | tf_op jit(solution)/shard_map/ppermute | solution.py:666
  399.2 2.7 unpack_shares.3
  402.4 0.9 collective-permute-done.44.refs_7_
  403.4 6.3 %finish.1 = (f32[768,768]{1,0:T(8,128)}, f32[768,768]{1,0:T(8,128)}, f32[768,768]{1,0:T(8,128)}, f32[768,768]{1,0:T(8,128)}, f32[8,768]{1,0:T(8,128)}) custom-call(s32[1,2]{1,0:T(1,128)} %add_bitcast_fusion.here_ref.me_ref, bf16[416,768]{1,0:T(8,128)(2,1)} %line_up.1.refs_0_, bf16[416,768]{1,0:T(8,128)(2,1)} %copy-done.8, bf16[416,768]{1,0:T(8,128)(2,1)} %copy-done.7, ...), custom_call_target="tpu_custom_call" | custom-call | flops 1 | bytes 1 | tf_op jit(solution)/shard_map/finish/pallas_call | solution.py:777
  409.6 1.5 slice_reduce_fusion
  (164 shorter events, 21.4 us)
Async XLA Ops:
  7.2 13.0 %copy-start.45 = (s32[1,8]{1,0:T(1,128)S(1)}, s32[1,8]{1,0:T(1,128)}, u32[]{:S(2)}) copy-start(s32[1,8]{1,0:T(1,128)} %counts_ref.1) | copy-start | bytes 100
  7.2 16.5 %copy-start.41 = (f32[768]{0:T(1024)S(1)}, f32[768]{0:T(1024)}, u32[]{:S(2)}) copy-start(f32[768]{0:T(1024)} %param.20) | copy-start | bytes 9220
  7.2 17.1 %copy-start.42 = (f32[768]{0:T(1024)S(1)}, f32[768]{0:T(1024)}, u32[]{:S(2)}) copy-start(f32[768]{0:T(1024)} %param.21) | copy-start | bytes 9220
  7.2 363.3 %reduce-scatter.3.cloned.1.call-start = ((), (), s32[]{:S(2)}) async-start(), calls=%async_computation.2 | async-start | bytes 10616832 | tf_op jit(solution)/shard_map/reduce_scatter | solution.py:830
  15.7 47.6 %collective-permute-start = (bf16[512,768]{1,0:T(8,128)(2,1)}, bf16[512,768]{1,0:T(8,128)(2,1)S(1)}, u32[]{:S(2)}, u32[]{:S(2)}) collective-permute-start(bf16[512,768]{1,0:T(8,128)(2,1)} %get-tuple-element.180), channel_id=1, source_target_pairs={{0,1},{1,0},{2,3},{3,2},{4,5},{5,4},{6,7},{7,6},{8,9},{9,8},{10,11... | collective-permute-start | bytes 2359304 | tf_op jit(solution)/shard_map/ppermute | solution.py:666
  18.7 44.7 %collective-permute-start.1 = (bf16[512,768]{1,0:T(8,128)(2,1)}, bf16[512,768]{1,0:T(8,128)(2,1)S(1)}, u32[]{:S(2)}, u32[]{:S(2)}) collective-permute-start(bf16[512,768]{1,0:T(8,128)(2,1)} %get-tuple-element.181), channel_id=1, source_target_pairs={{0,2},{1,3},{2,0},{3,1},{4,6},{5,7},{6,4},{7,5},{8,10},{9,11},{10,... | collective-permute-start | bytes 2359304 | tf_op jit(solution)/shard_map/ppermute | solution.py:666
  20.2 43.2 %collective-permute-start.2 = (bf16[512,768]{1,0:T(8,128)(2,1)}, bf16[512,768]{1,0:T(8,128)(2,1)S(1)}, u32[]{:S(2)}, u32[]{:S(2)}) collective-permute-start(bf16[512,768]{1,0:T(8,128)(2,1)} %get-tuple-element.182), channel_id=1, source_target_pairs={{0,3},{1,2},{2,1},{3,0},{4,7},{5,6},{6,5},{7,4},{8,11},{9,10},{10,... | collective-permute-start | bytes 2359304 | tf_op jit(solution)/shard_map/ppermute | solution.py:666
  20.2 38.1 %collective-permute-start.4 = (s32[1,8]{1,0:T(1,128)S(1)}, s32[1,8]{1,0:T(1,128)S(1)}, u32[]{:S(2)}, u32[]{:S(2)}) collective-permute-start(s32[1,8]{1,0:T(1,128)S(1)} %copy-done.45), channel_id=1, source_target_pairs={{0,2},{1,3},{2,0},{3,1},{4,6},{5,7},{6,4},{7,5},{8,10},{9,11},{10,... | collective-permute-start | bytes 104 | tf_op jit(solution)/shard_map/ppermute | solution.py:666
  22.2 36.1 %collective-permute-start.3 = (s32[1,8]{1,0:T(1,128)S(1)}, s32[1,8]{1,0:T(1,128)S(1)}, u32[]{:S(2)}, u32[]{:S(2)}) collective-permute-start(s32[1,8]{1,0:T(1,128)S(1)} %copy-done.45), channel_id=1, source_target_pairs={{0,1},{1,0},{2,3},{3,2},{4,5},{5,4},{6,7},{7,6},{8,9},{9,8},{10,11... | collective-permute-start | bytes 104 | tf_op jit(solution)/shard_map/ppermute | solution.py:666
  24.9 32.2 %copy-start.43 = (f32[768]{0:T(1024)S(1)}, f32[768]{0:T(1024)}, u32[]{:S(2)}) copy-start(f32[768]{0:T(1024)} %param.26) | copy-start | bytes 9220
  24.9 32.8 %copy-start.44 = (f32[768]{0:T(1024)S(1)}, f32[768]{0:T(1024)}, u32[]{:S(2)}) copy-start(f32[768]{0:T(1024)} %param.27) | copy-start | bytes 9220
  58.3 4.5 %collective-permute-start.5 = (s32[1,8]{1,0:T(1,128)S(1)}, s32[1,8]{1,0:T(1,128)S(1)}, u32[]{:S(2)}, u32[]{:S(2)}) collective-permute-start(s32[1,8]{1,0:T(1,128)S(1)} %copy-done.45), channel_id=1, source_target_pairs={{0,3},{1,2},{2,1},{3,0},{4,7},{5,6},{6,5},{7,4},{8,11},{9,10},{10,... | collective-permute-start | bytes 104 | tf_op jit(solution)/shard_map/ppermute | solution.py:666
  63.3 7.1 %copy-start = (bf16[512,768]{1,0:T(8,128)(2,1)}, bf16[512,768]{1,0:T(8,128)(2,1)S(1)}, u32[]{:S(2)}) copy-start(bf16[512,768]{1,0:T(8,128)(2,1)S(1)} %collective-permute-done.refs_5_) | copy-start | bytes 2359300
  63.3 7.1 %copy-start.1 = (bf16[512,768]{1,0:T(8,128)(2,1)}, bf16[512,768]{1,0:T(8,128)(2,1)S(1)}, u32[]{:S(2)}) copy-start(bf16[512,768]{1,0:T(8,128)(2,1)S(1)} %collective-permute-done.1.refs_6_) | copy-start | bytes 2359300
  63.4 7.1 %copy-start.2 = (bf16[512,768]{1,0:T(8,128)(2,1)}, bf16[512,768]{1,0:T(8,128)(2,1)S(1)}, u32[]{:S(2)}) copy-start(bf16[512,768]{1,0:T(8,128)(2,1)S(1)} %collective-permute-done.2.refs_7_) | copy-start | bytes 2359300
  70.4 16.4 %copy-start.40 = (bf16[768,8]{0,1:T(8,128)(2,1)S(1)}, bf16[768,8]{0,1:T(8,128)(2,1)}, u32[]{:S(2)}) copy-start(bf16[768,8]{0,1:T(8,128)(2,1)} %param.28) | copy-start | bytes 36868
  74.6 12.2 %collective-permute-start.6 = (bf16[256,768]{1,0:T(8,128)(2,1)}, bf16[256,768]{1,0:T(8,128)(2,1)S(1)}, u32[]{:S(2)}, u32[]{:S(2)}) collective-permute-start(bf16[256,768]{1,0:T(8,128)(2,1)} %get-tuple-element.187), channel_id=1, source_target_pairs={{0,1},{1,0},{2,3},{3,2},{4,5},{5,4},{6,7},{7,6},{8,9},{9,8},{10,11... | collective-permute-start | bytes 1179656 | tf_op jit(solution)/shard_map/ppermute | solution.py:666
  75.2 18.9 %collective-permute-start.7 = (bf16[256,768]{1,0:T(8,128)(2,1)}, bf16[256,768]{1,0:T(8,128)(2,1)S(1)}, u32[]{:S(2)}, u32[]{:S(2)}) collective-permute-start(bf16[256,768]{1,0:T(8,128)(2,1)} %get-tuple-element.188), channel_id=1, source_target_pairs={{0,2},{1,3},{2,0},{3,1},{4,6},{5,7},{6,4},{7,5},{8,10},{9,11},{10,... | collective-permute-start | bytes 1179656 | tf_op jit(solution)/shard_map/ppermute | solution.py:666
  75.2 20.0 %collective-permute-start.8 = (bf16[256,768]{1,0:T(8,128)(2,1)}, bf16[256,768]{1,0:T(8,128)(2,1)S(1)}, u32[]{:S(2)}, u32[]{:S(2)}) collective-permute-start(bf16[256,768]{1,0:T(8,128)(2,1)} %get-tuple-element.189), channel_id=1, source_target_pairs={{0,3},{1,2},{2,1},{3,0},{4,7},{5,6},{6,5},{7,4},{8,11},{9,10},{10,... | collective-permute-start | bytes 1179656 | tf_op jit(solution)/shard_map/ppermute | solution.py:666
  82.3 43.5 %collective-permute-start.12 = (bf16[256,768]{1,0:T(8,128)(2,1)}, bf16[256,768]{1,0:T(8,128)(2,1)S(1)}, u32[]{:S(2)}, u32[]{:S(2)}) collective-permute-start(bf16[256,768]{1,0:T(8,128)(2,1)} %get-tuple-element.191), channel_id=1, source_target_pairs={{0,1},{1,0},{2,3},{3,2},{4,5},{5,4},{6,7},{7,6},{8,9},{9,8},{10,11... | collective-permute-start | bytes 1179656 | tf_op jit(solution)/shard_map/ppermute | solution.py:666
  82.8 43.0 %collective-permute-start.13 = (bf16[256,768]{1,0:T(8,128)(2,1)}, bf16[256,768]{1,0:T(8,128)(2,1)S(1)}, u32[]{:S(2)}, u32[]{:S(2)}) collective-permute-start(bf16[256,768]{1,0:T(8,128)(2,1)} %get-tuple-element.192), channel_id=1, source_target_pairs={{0,2},{1,3},{2,0},{3,1},{4,6},{5,7},{6,4},{7,5},{8,10},{9,11},{10,... | collective-permute-start | bytes 1179656 | tf_op jit(solution)/shard_map/ppermute | solution.py:666
  86.8 8.4 %copy-start.27 = (bf16[256,768]{1,0:T(8,128)(2,1)}, bf16[256,768]{1,0:T(8,128)(2,1)S(1)}, u32[]{:S(2)}) copy-start(bf16[256,768]{1,0:T(8,128)(2,1)S(1)} %collective-permute-done.6.refs_1_) | copy-start | bytes 1179652
  86.8 39.0 %collective-permute-start.14 = (bf16[256,768]{1,0:T(8,128)(2,1)}, bf16[256,768]{1,0:T(8,128)(2,1)S(1)}, u32[]{:S(2)}, u32[]{:S(2)}) collective-permute-start(bf16[256,768]{1,0:T(8,128)(2,1)} %get-tuple-element.193), channel_id=1, source_target_pairs={{0,3},{1,2},{2,1},{3,0},{4,7},{5,6},{6,5},{7,4},{8,11},{9,10},{10,... | collective-permute-start | bytes 1179656 | tf_op jit(solution)/shard_map/ppermute | solution.py:666
  126.8 243.7 %reduce-scatter.5.cloned.1.call-start = ((), (), s32[]{:S(2)}) async-start(), calls=%async_computation.3 | async-start | bytes 10616832 | tf_op jit(solution)/shard_map/reduce_scatter | solution.py:830
  126.8 63.0 %collective-permute-start.9 = (bf16[512,768]{1,0:T(8,128)(2,1)}, bf16[512,768]{1,0:T(8,128)(2,1)S(1)}, u32[]{:S(2)}, u32[]{:S(2)}) collective-permute-start(bf16[512,768]{1,0:T(8,128)(2,1)} %get-tuple-element.203), channel_id=1, source_target_pairs={{0,1},{1,0},{2,3},{3,2},{4,5},{5,4},{6,7},{7,6},{8,9},{9,8},{10,11... | collective-permute-start | bytes 2359304 | tf_op jit(solution)/shard_map/ppermute | solution.py:666
  137.3 52.5 %collective-permute-start.10 = (bf16[512,768]{1,0:T(8,128)(2,1)}, bf16[512,768]{1,0:T(8,128)(2,1)S(1)}, u32[]{:S(2)}, u32[]{:S(2)}) collective-permute-start(bf16[512,768]{1,0:T(8,128)(2,1)} %get-tuple-element.204), channel_id=1, source_target_pairs={{0,2},{1,3},{2,0},{3,1},{4,6},{5,7},{6,4},{7,5},{8,10},{9,11},{10,... | collective-permute-start | bytes 2359304 | tf_op jit(solution)/shard_map/ppermute | solution.py:666
  137.9 51.9 %collective-permute-start.11 = (bf16[512,768]{1,0:T(8,128)(2,1)}, bf16[512,768]{1,0:T(8,128)(2,1)S(1)}, u32[]{:S(2)}, u32[]{:S(2)}) collective-permute-start(bf16[512,768]{1,0:T(8,128)(2,1)} %get-tuple-element.205), channel_id=1, source_target_pairs={{0,3},{1,2},{2,1},{3,0},{4,7},{5,6},{6,5},{7,4},{8,11},{9,10},{10,... | collective-permute-start | bytes 2359304 | tf_op jit(solution)/shard_map/ppermute | solution.py:666
  178.7 17.2 %collective-permute-start.15 = (bf16[256,768]{1,0:T(8,128)(2,1)}, bf16[256,768]{1,0:T(8,128)(2,1)S(1)}, u32[]{:S(2)}, u32[]{:S(2)}) collective-permute-start(bf16[256,768]{1,0:T(8,128)(2,1)} %get-tuple-element.216), channel_id=1, source_target_pairs={{0,1},{1,0},{2,3},{3,2},{4,5},{5,4},{6,7},{7,6},{8,9},{9,8},{10,11... | collective-permute-start | bytes 1179656 | tf_op jit(solution)/shard_map/ppermute | solution.py:666
  180.9 19.1 %collective-permute-start.16 = (bf16[256,768]{1,0:T(8,128)(2,1)}, bf16[256,768]{1,0:T(8,128)(2,1)S(1)}, u32[]{:S(2)}, u32[]{:S(2)}) collective-permute-start(bf16[256,768]{1,0:T(8,128)(2,1)} %get-tuple-element.217), channel_id=1, source_target_pairs={{0,2},{1,3},{2,0},{3,1},{4,6},{5,7},{6,4},{7,5},{8,10},{9,11},{10,... | collective-permute-start | bytes 1179656 | tf_op jit(solution)/shard_map/ppermute | solution.py:666
  189.8 10.2 %collective-permute-start.17 = (bf16[256,768]{1,0:T(8,128)(2,1)}, bf16[256,768]{1,0:T(8,128)(2,1)S(1)}, u32[]{:S(2)}, u32[]{:S(2)}) collective-permute-start(bf16[256,768]{1,0:T(8,128)(2,1)} %get-tuple-element.218), channel_id=1, source_target_pairs={{0,3},{1,2},{2,1},{3,0},{4,7},{5,6},{6,5},{7,4},{8,11},{9,10},{10,... | collective-permute-start | bytes 1179656 | tf_op jit(solution)/shard_map/ppermute | solution.py:666
  207.2 40.5 %collective-permute-start.18 = (bf16[256,768]{1,0:T(8,128)(2,1)S(1)}, bf16[256,768]{1,0:T(8,128)(2,1)S(1)}, u32[]{:S(2)}, u32[]{:S(2)}) collective-permute-start(bf16[256,768]{1,0:T(8,128)(2,1)S(1)} %copy-done.48), channel_id=1, source_target_pairs={{0,1},{1,0},{2,3},{3,2},{4,5},{5,4},{6,7},{7,6},{8,9},{9,8},{10,11... | collective-permute-start | bytes 1179656 | tf_op jit(solution)/shard_map/ppermute | solution.py:666
  207.9 54.6 %collective-permute-start.19 = (bf16[256,768]{1,0:T(8,128)(2,1)S(1)}, bf16[256,768]{1,0:T(8,128)(2,1)S(1)}, u32[]{:S(2)}, u32[]{:S(2)}) collective-permute-start(bf16[256,768]{1,0:T(8,128)(2,1)S(1)} %copy-done.47), channel_id=1, source_target_pairs={{0,2},{1,3},{2,0},{3,1},{4,6},{5,7},{6,4},{7,5},{8,10},{9,11},{10,... | collective-permute-start | bytes 1179656 | tf_op jit(solution)/shard_map/ppermute | solution.py:666
  220.6 42.2 %collective-permute-start.21 = (bf16[384,768]{1,0:T(8,128)(2,1)}, bf16[384,768]{1,0:T(8,128)(2,1)S(1)}, u32[]{:S(2)}, u32[]{:S(2)}) collective-permute-start(bf16[384,768]{1,0:T(8,128)(2,1)} %get-tuple-element.240), channel_id=1, source_target_pairs={{0,4},{4,0},{8,12},{12,8},{16,20},{20,16},{24,28},{28,24},{1,5},{5... | collective-permute-start | bytes 1769480 | tf_op jit(solution)/shard_map/ppermute | solution.py:666
  233.8 29.0 %collective-permute-start.22 = (bf16[384,768]{1,0:T(8,128)(2,1)}, bf16[384,768]{1,0:T(8,128)(2,1)S(1)}, u32[]{:S(2)}, u32[]{:S(2)}) collective-permute-start(bf16[384,768]{1,0:T(8,128)(2,1)} %get-tuple-element.251), channel_id=1, source_target_pairs={{0,4},{4,0},{8,12},{12,8},{16,20},{20,16},{24,28},{28,24},{1,5},{5... | collective-permute-start | bytes 1769480 | tf_op jit(solution)/shard_map/ppermute | solution.py:666
  247.7 15.1 %collective-permute-start.23 = (bf16[384,768]{1,0:T(8,128)(2,1)}, bf16[384,768]{1,0:T(8,128)(2,1)S(1)}, u32[]{:S(2)}, u32[]{:S(2)}) collective-permute-start(bf16[384,768]{1,0:T(8,128)(2,1)} %get-tuple-element.257), channel_id=1, source_target_pairs={{0,4},{4,0},{8,12},{12,8},{16,20},{20,16},{24,28},{28,24},{1,5},{5... | collective-permute-start | bytes 1769480 | tf_op jit(solution)/shard_map/ppermute | solution.py:666
  247.7 14.7 %copy-start.18 = (bf16[256,768]{1,0:T(8,128)(2,1)}, bf16[256,768]{1,0:T(8,128)(2,1)S(1)}, u32[]{:S(2)}) copy-start(bf16[256,768]{1,0:T(8,128)(2,1)S(1)} %collective-permute-done.18.refs_1_) | copy-start | bytes 1179652
  247.7 15.1 %collective-permute-start.20 = (bf16[256,768]{1,0:T(8,128)(2,1)}, bf16[256,768]{1,0:T(8,128)(2,1)S(1)}, u32[]{:S(2)}, u32[]{:S(2)}) collective-permute-start(bf16[256,768]{1,0:T(8,128)(2,1)} %get-tuple-element.239), channel_id=1, source_target_pairs={{0,3},{1,2},{2,1},{3,0},{4,7},{5,6},{6,5},{7,4},{8,11},{9,10},{10,... | collective-permute-start | bytes 1179656 | tf_op jit(solution)/shard_map/ppermute | solution.py:666
  262.5 15.4 %copy-start.19 = (bf16[256,768]{1,0:T(8,128)(2,1)}, bf16[256,768]{1,0:T(8,128)(2,1)S(1)}, u32[]{:S(2)}) copy-start(bf16[256,768]{1,0:T(8,128)(2,1)S(1)} %collective-permute-done.19.refs_2_) | copy-start | bytes 1179652
  262.5 24.2 %collective-permute-start.28 = (bf16[384,768]{1,0:T(8,128)(2,1)}, bf16[384,768]{1,0:T(8,128)(2,1)S(1)}, u32[]{:S(2)}, u32[]{:S(2)}) collective-permute-start(bf16[384,768]{1,0:T(8,128)(2,1)} %get-tuple-element.263), channel_id=1, source_target_pairs={{0,4},{4,0},{8,12},{12,8},{16,20},{20,16},{24,28},{28,24},{1,5},{5... | collective-permute-start | bytes 1769480 | tf_op jit(solution)/shard_map/ppermute | solution.py:666
  262.8 15.1 %copy-start.20 = (bf16[256,768]{1,0:T(8,128)(2,1)}, bf16[256,768]{1,0:T(8,128)(2,1)S(1)}, u32[]{:S(2)}) copy-start(bf16[256,768]{1,0:T(8,128)(2,1)S(1)} %collective-permute-done.20.refs_3_) | copy-start | bytes 1179652
  267.7 12.8 %copy-start.46 = (bf16[288,768]{1,0:T(8,128)(2,1)S(1)}, bf16[288,768]{1,0:T(8,128)(2,1)}, u32[]{:S(2)}) copy-start(bf16[288,768]{1,0:T(8,128)(2,1)} %get-tuple-element.282) | copy-start | bytes 1327108
  277.9 8.8 %collective-permute-start.27 = (bf16[128,768]{1,0:T(8,128)(2,1)}, bf16[128,768]{1,0:T(8,128)(2,1)S(1)}, u32[]{:S(2)}, u32[]{:S(2)}) collective-permute-start(bf16[128,768]{1,0:T(8,128)(2,1)} %get-tuple-element.295), channel_id=1, source_target_pairs={{0,4},{4,0},{8,12},{12,8},{16,20},{20,16},{24,28},{28,24},{1,5},{5... | collective-permute-start | bytes 589832 | tf_op jit(solution)/shard_map/ppermute | solution.py:666
  278.3 37.4 %collective-permute-start.24 = (bf16[288,768]{1,0:T(8,128)(2,1)}, bf16[288,768]{1,0:T(8,128)(2,1)S(1)}, u32[]{:S(2)}, u32[]{:S(2)}) collective-permute-start(bf16[288,768]{1,0:T(8,128)(2,1)} %get-tuple-element.280), channel_id=1, source_target_pairs={{0,1},{1,0},{2,3},{3,2},{4,5},{5,4},{6,7},{7,6},{8,9},{9,8},{10,11... | collective-permute-start | bytes 1327112 | tf_op jit(solution)/shard_map/ppermute | solution.py:666
  279.2 36.5 %collective-permute-start.25 = (bf16[288,768]{1,0:T(8,128)(2,1)}, bf16[288,768]{1,0:T(8,128)(2,1)S(1)}, u32[]{:S(2)}, u32[]{:S(2)}) collective-permute-start(bf16[288,768]{1,0:T(8,128)(2,1)} %get-tuple-element.281), channel_id=1, source_target_pairs={{0,2},{1,3},{2,0},{3,1},{4,6},{5,7},{6,4},{7,5},{8,10},{9,11},{10,... | collective-permute-start | bytes 1327112 | tf_op jit(solution)/shard_map/ppermute | solution.py:666
  280.5 35.2 %collective-permute-start.26 = (bf16[288,768]{1,0:T(8,128)(2,1)S(1)}, bf16[288,768]{1,0:T(8,128)(2,1)S(1)}, u32[]{:S(2)}, u32[]{:S(2)}) collective-permute-start(bf16[288,768]{1,0:T(8,128)(2,1)S(1)} %copy-done.46), channel_id=1, source_target_pairs={{0,3},{1,2},{2,1},{3,0},{4,7},{5,6},{6,5},{7,4},{8,11},{9,10},{10,... | collective-permute-start | bytes 1327112 | tf_op jit(solution)/shard_map/ppermute | solution.py:666
  289.9 14.6 %collective-permute-start.29 = (bf16[128,768]{1,0:T(8,128)(2,1)}, bf16[128,768]{1,0:T(8,128)(2,1)S(1)}, u32[]{:S(2)}, u32[]{:S(2)}) collective-permute-start(bf16[128,768]{1,0:T(8,128)(2,1)} %get-tuple-element.302), channel_id=1, source_target_pairs={{0,1},{1,0},{2,3},{3,2},{4,5},{5,4},{6,7},{7,6},{8,9},{9,8},{10,11... | collective-permute-start | bytes 589832 | tf_op jit(solution)/shard_map/ppermute | solution.py:666
  290.7 25.0 %collective-permute-start.30 = (bf16[128,768]{1,0:T(8,128)(2,1)}, bf16[128,768]{1,0:T(8,128)(2,1)S(1)}, u32[]{:S(2)}, u32[]{:S(2)}) collective-permute-start(bf16[128,768]{1,0:T(8,128)(2,1)} %get-tuple-element.303), channel_id=1, source_target_pairs={{0,2},{1,3},{2,0},{3,1},{4,6},{5,7},{6,4},{7,5},{8,10},{9,11},{10,... | collective-permute-start | bytes 589832 | tf_op jit(solution)/shard_map/ppermute | solution.py:666
  304.5 11.1 %collective-permute-start.31 = (bf16[128,768]{1,0:T(8,128)(2,1)}, bf16[128,768]{1,0:T(8,128)(2,1)S(1)}, u32[]{:S(2)}, u32[]{:S(2)}) collective-permute-start(bf16[128,768]{1,0:T(8,128)(2,1)} %get-tuple-element.304), channel_id=1, source_target_pairs={{0,3},{1,2},{2,1},{3,0},{4,7},{5,6},{6,5},{7,4},{8,11},{9,10},{10,... | collective-permute-start | bytes 589832 | tf_op jit(solution)/shard_map/ppermute | solution.py:666
  319.6 15.1 %collective-permute-start.32 = (bf16[104,768]{1,0:T(8,128)(2,1)}, bf16[104,768]{1,0:T(8,128)(2,1)S(1)}, u32[]{:S(2)}, u32[]{:S(2)}) collective-permute-start(bf16[104,768]{1,0:T(8,128)(2,1)} %get-tuple-element.322), channel_id=1, source_target_pairs={{0,8},{4,12},{8,0},{12,4},{16,24},{20,28},{24,16},{28,20},{1,9},{5... | collective-permute-start | bytes 479240 | tf_op jit(solution)/shard_map/ppermute | solution.py:666
  321.3 15.0 %collective-permute-start.33 = (bf16[104,768]{1,0:T(8,128)(2,1)}, bf16[104,768]{1,0:T(8,128)(2,1)S(1)}, u32[]{:S(2)}, u32[]{:S(2)}) collective-permute-start(bf16[104,768]{1,0:T(8,128)(2,1)} %get-tuple-element.323), channel_id=1, source_target_pairs={{0,16},{4,20},{8,24},{12,28},{16,0},{20,4},{24,8},{28,12},{1,17},{... | collective-permute-start | bytes 479240 | tf_op jit(solution)/shard_map/ppermute | solution.py:666
  322.5 20.7 %collective-permute-start.34 = (bf16[104,768]{1,0:T(8,128)(2,1)}, bf16[104,768]{1,0:T(8,128)(2,1)S(1)}, u32[]{:S(2)}, u32[]{:S(2)}) collective-permute-start(bf16[104,768]{1,0:T(8,128)(2,1)} %get-tuple-element.324), channel_id=1, source_target_pairs={{0,24},{4,28},{8,16},{12,20},{16,8},{20,12},{24,0},{28,4},{1,25},{... | collective-permute-start | bytes 479240 | tf_op jit(solution)/shard_map/ppermute | solution.py:666
  334.7 8.5 %copy-start.34 = (bf16[104,768]{1,0:T(8,128)(2,1)}, bf16[104,768]{1,0:T(8,128)(2,1)S(1)}, u32[]{:S(2)}) copy-start(bf16[104,768]{1,0:T(8,128)(2,1)S(1)} %collective-permute-done.32.refs_1_) | copy-start | bytes 479236
  345.8 9.1 %collective-permute-start.37 = (bf16[104,768]{1,0:T(8,128)(2,1)}, bf16[104,768]{1,0:T(8,128)(2,1)S(1)}, u32[]{:S(2)}, u32[]{:S(2)}) collective-permute-start(bf16[104,768]{1,0:T(8,128)(2,1)} %add_parts.1.refs_0_), channel_id=1, source_target_pairs={{0,24},{4,28},{8,16},{12,20},{16,8},{20,12},{24,0},{28,4},{1,25},{... | collective-permute-start | bytes 479240 | tf_op jit(solution)/shard_map/ppermute | solution.py:666
  346.2 17.5 %collective-permute-start.36 = (bf16[104,768]{1,0:T(8,128)(2,1)}, bf16[104,768]{1,0:T(8,128)(2,1)S(1)}, u32[]{:S(2)}, u32[]{:S(2)}) collective-permute-start(bf16[104,768]{1,0:T(8,128)(2,1)} %add_parts.1.refs_0_), channel_id=1, source_target_pairs={{0,16},{4,20},{8,24},{12,28},{16,0},{20,4},{24,8},{28,12},{1,17},{... | collective-permute-start | bytes 479240 | tf_op jit(solution)/shard_map/ppermute | solution.py:666
  350.7 13.0 %collective-permute-start.35 = (bf16[104,768]{1,0:T(8,128)(2,1)}, bf16[104,768]{1,0:T(8,128)(2,1)S(1)}, u32[]{:S(2)}, u32[]{:S(2)}) collective-permute-start(bf16[104,768]{1,0:T(8,128)(2,1)} %add_parts.1.refs_0_), channel_id=1, source_target_pairs={{0,8},{4,12},{8,0},{12,4},{16,24},{20,28},{24,16},{28,20},{1,9},{5... | collective-permute-start | bytes 479240 | tf_op jit(solution)/shard_map/ppermute | solution.py:666
  354.8 8.8 %copy-start.36 = (bf16[104,768]{1,0:T(8,128)(2,1)}, bf16[104,768]{1,0:T(8,128)(2,1)S(1)}, u32[]{:S(2)}) copy-start(bf16[104,768]{1,0:T(8,128)(2,1)S(1)} %collective-permute-done.37.refs_3_) | copy-start | bytes 479236
  367.0 18.4 %collective-permute-start.40 = (bf16[416,768]{1,0:T(8,128)(2,1)}, bf16[416,768]{1,0:T(8,128)(2,1)S(1)}, u32[]{:S(2)}, u32[]{:S(2)}) collective-permute-start(bf16[416,768]{1,0:T(8,128)(2,1)} %line_up.1.refs_0_), channel_id=1, source_target_pairs={{0,3},{1,2},{2,1},{3,0},{4,7},{5,6},{6,5},{7,4},{8,11},{9,10},{10,... | collective-permute-start | bytes 1916936 | tf_op jit(solution)/shard_map/ppermute | solution.py:666
  369.0 29.1 %collective-permute-start.39 = (bf16[416,768]{1,0:T(8,128)(2,1)}, bf16[416,768]{1,0:T(8,128)(2,1)S(1)}, u32[]{:S(2)}, u32[]{:S(2)}) collective-permute-start(bf16[416,768]{1,0:T(8,128)(2,1)} %line_up.1.refs_0_), channel_id=1, source_target_pairs={{0,2},{1,3},{2,0},{3,1},{4,6},{5,7},{6,4},{7,5},{8,10},{9,11},{10,... | collective-permute-start | bytes 1916936 | tf_op jit(solution)/shard_map/ppermute | solution.py:666
  369.9 28.3 %collective-permute-start.38 = (bf16[416,768]{1,0:T(8,128)(2,1)}, bf16[416,768]{1,0:T(8,128)(2,1)S(1)}, u32[]{:S(2)}, u32[]{:S(2)}) collective-permute-start(bf16[416,768]{1,0:T(8,128)(2,1)} %line_up.1.refs_0_), channel_id=1, source_target_pairs={{0,1},{1,0},{2,3},{3,2},{4,5},{5,4},{6,7},{7,6},{8,9},{9,8},{10,11... | collective-permute-start | bytes 1916936 | tf_op jit(solution)/shard_map/ppermute | solution.py:666
  385.4 16.5 %copy-start.6 = (bf16[416,768]{1,0:T(8,128)(2,1)}, bf16[416,768]{1,0:T(8,128)(2,1)S(1)}, u32[]{:S(2)}) copy-start(bf16[416,768]{1,0:T(8,128)(2,1)S(1)} %collective-permute-done.40.refs_3_) | copy-start | bytes 1916932
  398.1 3.8 collective-permute-start.41
  398.2 3.8 collective-permute-start.42
  398.7 3.7 collective-permute-start.43
  398.8 4.6 %collective-permute-start.44 = (bf16[416,768]{1,0:T(8,128)(2,1)S(1)}, bf16[416,768]{1,0:T(8,128)(2,1)}, u32[]{:S(2)}, u32[]{:S(2)}) collective-permute-start(bf16[416,768]{1,0:T(8,128)(2,1)S(1)} %collective-permute-done.40.refs_3_), channel_id=1, source_target_pairs={{0,4},{4,0},{8,12},{12,8},{16,20},{20,16},{24,28},{28,24},{1,5},{5... | collective-permute-start | bytes 1916936 | tf_op jit(solution)/shard_map/ppermute | solution.py:666
  (32 other events, 51.3 us)
Sparse Core Ops, SparseCore 0:
  126.0 107.8 reduce-scatter.2
  236.2 105.8 reduce-scatter.4
